TPU v7x, 512 devices: a whole 4x8x8 slice. The times are simulated.
512 devices in a mesh: space: 64 (over y, x, core), chan: 8 (over z).
Axes of the slice: x: 4, y: 8, z: 8, core: 2. Of those that a mesh axis runs over, the one named last changes fastest.
Arguments:
- features: bfloat16 [65536, 256], P('space', 'chan'), may hold values from -6 to 6
- weights: bfloat16 [27, 256, 256], P(None, 'chan'), may hold values from -0.125 to 0.125
- send_rows: int32 [64, 8, 768], P('space'), may hold values from 0 to 1024, as said below
- gather_map: int32 [27, 65536], P(None, 'space'), may hold values from 0 to 7168, as said below
Outputs:
- output: bfloat16 [65536, 256], P('space', 'chan')
Inputs may be any that keep to these rules, and one draw needn't show every extreme that they name: `send_rows`: an entry of 1024 marks an empty slot; the others are local row numbers of the sending block. Every direction of every block has some empty slots. `gather_map`: an entry of 7168 names the zero row; offset 13 (the centre) maps each voxel to its own local row.
All inputs are finite; a program needn't handle non-finite values.
Results may differ from a plain program's by a relative error of at most 0.001.
Values may be sent and summed in bfloat16 or wider, within the bound.
No kernel may reach another device: no remote copies, remote signals or barrier semaphores. Data moves between devices by JAX's collectives and lax.ppermute only.
A program may use at most 64 MiB of HBM per device.

v0:
```python
import jax
import jax.numpy as jnp
from jax import lax
from jax.sharding import PartitionSpec as P

GRID_COLS = 8


directions = [(-1, -1), (-1, 0), (-1, 1), (0, -1), (0, 1), (1, -1), (1, 0), (1, 1)]


def shifted(value, axis, steps):
    count = lax.axis_size(axis)
    first, last = (max(0, -steps), min(count, count - steps))
    return lax.ppermute(value, axis, [(source, source + steps) for source in range(first, last)])


def inside_grid(grid_row, grid_col, grid_rows):
    return (grid_row >= 0) & (grid_row < grid_rows) & (grid_col >= 0) & (grid_col < GRID_COLS)


def local(features, weights, send_rows, gather_map):
    group_width = features.shape[1]
    spaces = lax.axis_size("space")
    grid_rows = spaces // GRID_COLS
    myself = lax.axis_index("space")
    my_row = myself // GRID_COLS
    my_col = myself % GRID_COLS
    padded = jnp.concatenate([features, jnp.zeros((1, group_width), jnp.bfloat16)], axis=0)
    outgoing = padded[send_rows[0]]
    slots = outgoing.shape[1]
    pieces = []
    for number, (step_x, step_y) in enumerate(directions):
        got = shifted(outgoing[number], "space", step_x * GRID_COLS + step_y)
        usable = inside_grid(my_row - step_x, my_col - step_y, grid_rows)
        pieces.append(jnp.where(usable, got, jnp.zeros_like(got)))
    received = jnp.stack(pieces, axis=0)
    table = jnp.concatenate(
        [
            features,
            received.reshape(8 * slots, group_width),
            jnp.zeros((1, group_width), jnp.bfloat16),
        ],
        axis=0,
    )
    picked = table[gather_map]
    partial_value = jnp.einsum("kvc,kco->vo", picked, weights, preferred_element_type=jnp.float32)
    summed = lax.psum_scatter(partial_value, "chan", scatter_dimension=1, tiled=True)
    return summed.astype(jnp.bfloat16)


def solution(mesh):
    in_specs = (P("space", "chan"), P(None, "chan", None), P("space", None, None), P(None, "space"))
    out_specs = P("space", "chan")
    return jax.shard_map(local, mesh=mesh, in_specs=in_specs, out_specs=out_specs, check_vma=False)
```

profile of v0, /device:TPU:2, one launch (start us, length us, event | category | flops | bytes accessed | tf_op | source)
XLA Modules:
  0.0 242.3 jit_solution(18241414781143499284)
XLA Ops:
  6.5 0.8 compare_select_fusion.1
  7.3 1.0 copy.31
  8.4 18.1 %gather_fusion = bf16[6144,32]{1,0:T(8,128)(2,1)S(1)} fusion(bf16[1025,32]{1,0:T(8,128)(2,1)S(1)} %concatenate.6, s32[6144]{0:T(1024)S(1)} %broadcast_clamp_fusion.1), kind=kCustom, calls=%fused_computation | custom fusion | bytes 811008 | tf_op jit(solution)/shard_map/gather | solution.py:30
  26.5 0.8 fusion
  27.3 3.6 %collective-permute-start.7 = (bf16[768,32]{1,0:T(8,128)(2,1)S(1)}, bf16[768,32]{1,0:T(8,128)(2,1)}, u32[]{:S(2)}, u32[]{:S(2)}) collective-permute-start(bf16[768,32]{1,0:T(8,128)(2,1)S(1)} %get-tuple-element.5), channel_id=1, source_target_pairs={{0,72},{8,80},{16,88},{24,96},{32,104},{40,112},{48,120},{56,128},... | collective-permute-start | bytes 147464 | tf_op jit(solution)/shard_map/ppermute | solution.py:15
  30.9 3.5 %collective-permute-start.6 = (bf16[768,32]{1,0:T(8,128)(2,1)S(1)}, bf16[768,32]{1,0:T(8,128)(2,1)}, u32[]{:S(2)}, u32[]{:S(2)}) collective-permute-start(bf16[768,32]{1,0:T(8,128)(2,1)S(1)} %get-tuple-element.6), channel_id=1, source_target_pairs={{0,64},{8,72},{16,80},{24,88},{32,96},{40,104},{48,112},{56,120},{... | collective-permute-start | bytes 147464 | tf_op jit(solution)/shard_map/ppermute | solution.py:15
  34.4 4.4 %collective-permute-start.5 = (bf16[768,32]{1,0:T(8,128)(2,1)S(1)}, bf16[768,32]{1,0:T(8,128)(2,1)}, u32[]{:S(2)}, u32[]{:S(2)}) collective-permute-start(bf16[768,32]{1,0:T(8,128)(2,1)S(1)} %get-tuple-element.7), channel_id=1, source_target_pairs={{0,56},{8,64},{16,72},{24,80},{32,88},{40,96},{48,104},{56,112},{6... | collective-permute-start | bytes 147464 | tf_op jit(solution)/shard_map/ppermute | solution.py:15
  38.8 1.9 collective-permute-start.4
  40.7 1.3 collective-permute-start
  42.2 9.4 %collective-permute-done = bf16[768,32]{1,0:T(8,128)(2,1)} collective-permute-done((bf16[768,32]{1,0:T(8,128)(2,1)}, bf16[768,32]{1,0:T(8,128)(2,1)}, u32[]{:S(2)}, u32[]{:S(2)}) %collective-permute-start) | collective-permute-done | bytes 49184 | tf_op jit(solution)/shard_map/ppermute | solution.py:15
  51.6 1.3 collective-permute-start.1
  52.9 1.0 bitcast_dynamic-update-slice_fusion.7
  53.8 7.0 %collective-permute-done.1 = bf16[768,32]{1,0:T(8,128)(2,1)S(1)} collective-permute-done((bf16[768,32]{1,0:T(8,128)(2,1)S(1)}, bf16[768,32]{1,0:T(8,128)(2,1)S(1)}, u32[]{:S(2)}, u32[]{:S(2)}) %collective-permute-start.1) | collective-permute-done | bytes 49184 | tf_op jit(solution)/shard_map/ppermute | solution.py:15
  60.9 1.3 collective-permute-start.2
  62.2 7.2 %collective-permute-done.2 = bf16[768,32]{1,0:T(8,128)(2,1)S(1)} collective-permute-done((bf16[768,32]{1,0:T(8,128)(2,1)S(1)}, bf16[768,32]{1,0:T(8,128)(2,1)S(1)}, u32[]{:S(2)}, u32[]{:S(2)}) %collective-permute-start.2) | collective-permute-done | bytes 49184 | tf_op jit(solution)/shard_map/ppermute | solution.py:15
  69.5 1.9 collective-permute-start.3
  71.4 3.1 %collective-permute-done.3 = bf16[768,32]{1,0:T(8,128)(2,1)S(1)} collective-permute-done((bf16[768,32]{1,0:T(8,128)(2,1)S(1)}, bf16[768,32]{1,0:T(8,128)(2,1)S(1)}, u32[]{:S(2)}, u32[]{:S(2)}) %collective-permute-start.3) | collective-permute-done | bytes 49184 | tf_op jit(solution)/shard_map/ppermute | solution.py:15
  74.6 1.0 bitcast_dynamic-update-slice_fusion.3
  75.9 0.6 copy.36
  76.6 1.6 copy.33
  78.3 97.3 %gather_fusion.1 = bf16[27648,32]{1,0:T(8,128)(2,1)} fusion(bf16[7169,32]{1,0:T(8,128)(2,1)S(1)} %copy.33, s32[27648]{0:T(1024)S(1)} %broadcast_clamp_fusion), kind=kCustom, calls=%fused_computation.1 | custom fusion | bytes 3649536 | tf_op jit(solution)/shard_map/gather | solution.py:46
  175.5 6.1 %convolution_bitcast_fusion = f32[1024,256]{0,1:T(8,128)} fusion(bf16[27,1024,32]{2,1,0:T(8,128)(2,1)} %bitcast.27, bf16[27,32,256]{2,1,0:T(8,128)(2,1)S(1)} %copy-done), kind=kOutput, calls=%fused_computation.2 | convolution fusion | flops 452984832 | bytes 3260416 | tf_op jit(solution)/shard_map/kvc,kco->vo/dot_general | solution.py:47
  181.7 52.3 %reduce-scatter.2.cloned.1.call-done = f32[1024,32]{0,1:T(8,128)} async-done(((f32[1024,256]{0,1:T(8,128)}), f32[1024,32]{0,1:T(8,128)}) %reduce-scatter.2.cloned.1.call-update) | async-done | bytes 131088 | tf_op jit(solution)/shard_map/reduce_scatter | solution.py:48
  233.9 1.5 convert_element_type.3
  (26 shorter events, 0.7 us)
Async XLA Ops:
  6.5 169.0 %copy-start = (bf16[27,32,256]{2,1,0:T(8,128)(2,1)S(1)}, bf16[27,32,256]{2,1,0:T(8,128)(2,1)}, u32[]{:S(2)}) copy-start(bf16[27,32,256]{2,1,0:T(8,128)(2,1)} %param.5) | copy-start | bytes 1327108
  6.5 227.4 %reduce-scatter.2.cloned.1.call-start = ((), (), s32[]{:S(2)}) async-start(), calls=%async_computation.1 | async-start | bytes 1179648 | tf_op jit(solution)/shard_map/reduce_scatter | solution.py:48
  26.5 15.5 %copy-start.2 = (s32[27,1024]{1,0:T(8,128)S(1)}, s32[27,1024]{1,0:T(8,128)}, u32[]{:S(2)}) copy-start(s32[27,1024]{1,0:T(8,128)} %param.7) | copy-start | bytes 331780
  27.3 48.5 %collective-permute-start.7 = (bf16[768,32]{1,0:T(8,128)(2,1)S(1)}, bf16[768,32]{1,0:T(8,128)(2,1)}, u32[]{:S(2)}, u32[]{:S(2)}) collective-permute-start(bf16[768,32]{1,0:T(8,128)(2,1)S(1)} %get-tuple-element.5), channel_id=1, source_target_pairs={{0,72},{8,80},{16,88},{24,96},{32,104},{40,112},{48,120},{56,128},... | collective-permute-start | bytes 147464 | tf_op jit(solution)/shard_map/ppermute | solution.py:15
  30.9 44.8 %collective-permute-start.6 = (bf16[768,32]{1,0:T(8,128)(2,1)S(1)}, bf16[768,32]{1,0:T(8,128)(2,1)}, u32[]{:S(2)}, u32[]{:S(2)}) collective-permute-start(bf16[768,32]{1,0:T(8,128)(2,1)S(1)} %get-tuple-element.6), channel_id=1, source_target_pairs={{0,64},{8,72},{16,80},{24,88},{32,96},{40,104},{48,112},{56,120},{... | collective-permute-start | bytes 147464 | tf_op jit(solution)/shard_map/ppermute | solution.py:15
  34.4 41.2 %collective-permute-start.5 = (bf16[768,32]{1,0:T(8,128)(2,1)S(1)}, bf16[768,32]{1,0:T(8,128)(2,1)}, u32[]{:S(2)}, u32[]{:S(2)}) collective-permute-start(bf16[768,32]{1,0:T(8,128)(2,1)S(1)} %get-tuple-element.7), channel_id=1, source_target_pairs={{0,56},{8,64},{16,72},{24,80},{32,88},{40,96},{48,104},{56,112},{6... | collective-permute-start | bytes 147464 | tf_op jit(solution)/shard_map/ppermute | solution.py:15
  38.8 35.8 %collective-permute-start.4 = (bf16[768,32]{1,0:T(8,128)(2,1)S(1)}, bf16[768,32]{1,0:T(8,128)(2,1)}, u32[]{:S(2)}, u32[]{:S(2)}) collective-permute-start(bf16[768,32]{1,0:T(8,128)(2,1)S(1)} %get-tuple-element.8), channel_id=1, source_target_pairs={{0,8},{8,16},{16,24},{24,32},{32,40},{40,48},{48,56},{56,64},{64,7... | collective-permute-start | bytes 147464 | tf_op jit(solution)/shard_map/ppermute | solution.py:15
  40.7 10.9 %collective-permute-start = (bf16[768,32]{1,0:T(8,128)(2,1)}, bf16[768,32]{1,0:T(8,128)(2,1)}, u32[]{:S(2)}, u32[]{:S(2)}) collective-permute-start(bf16[768,32]{1,0:T(8,128)(2,1)} %get-tuple-element.12), channel_id=1, source_target_pairs={{72,0},{80,8},{88,16},{96,24},{104,32},{112,40},{120,48},{128,56},... | collective-permute-start | bytes 147464 | tf_op jit(solution)/shard_map/ppermute | solution.py:15
  51.6 9.3 %collective-permute-start.1 = (bf16[768,32]{1,0:T(8,128)(2,1)S(1)}, bf16[768,32]{1,0:T(8,128)(2,1)S(1)}, u32[]{:S(2)}, u32[]{:S(2)}) collective-permute-start(bf16[768,32]{1,0:T(8,128)(2,1)S(1)} %get-tuple-element.11), channel_id=1, source_target_pairs={{64,0},{72,8},{80,16},{88,24},{96,32},{104,40},{112,48},{120,56},{... | collective-permute-start | bytes 147464 | tf_op jit(solution)/shard_map/ppermute | solution.py:15
  60.9 8.6 %collective-permute-start.2 = (bf16[768,32]{1,0:T(8,128)(2,1)S(1)}, bf16[768,32]{1,0:T(8,128)(2,1)S(1)}, u32[]{:S(2)}, u32[]{:S(2)}) collective-permute-start(bf16[768,32]{1,0:T(8,128)(2,1)S(1)} %get-tuple-element.10), channel_id=1, source_target_pairs={{56,0},{64,8},{72,16},{80,24},{88,32},{96,40},{104,48},{112,56},{1... | collective-permute-start | bytes 147464 | tf_op jit(solution)/shard_map/ppermute | solution.py:15
  69.5 5.1 %collective-permute-start.3 = (bf16[768,32]{1,0:T(8,128)(2,1)S(1)}, bf16[768,32]{1,0:T(8,128)(2,1)S(1)}, u32[]{:S(2)}, u32[]{:S(2)}) collective-permute-start(bf16[768,32]{1,0:T(8,128)(2,1)S(1)} %get-tuple-element.9), channel_id=1, source_target_pairs={{8,0},{16,8},{24,16},{32,24},{40,32},{48,40},{56,48},{64,56},{72,6... | collective-permute-start | bytes 147464 | tf_op jit(solution)/shard_map/ppermute | solution.py:15
  75.6 0.9 copy-start.1
Sparse Core Ops, SparseCore 0:
  181.8 52.0 reduce-scatter.1
where the time goes:
time: 243 us; the launch traced here: 242 us
  local copies, waits for them, and re-layouts  120 us (49%)
  waiting for transfers between devices  79 us (33%)
  starting transfers between devices  19.1 us (8%)
  between operations  13.6 us (6%)
  matrix products  6.09 us (3%)
  other arithmetic  4.86 us (2%)
    gather x1, local copies, waits for them, and re-layouts, local(): picked = table[gather_map]  97.3 us
    reduce_scatter x1, waiting for transfers between devices, local(): lax.psum_scatter(partial_value, 'chan', scatter_dimension=1, tiled=True)  52.3 us
    ppermute x8, waiting for transfers between devices, shifted(): lax.ppermute(value, axis, [(source, source + steps) for source in range(f...  26.8 us
    ppermute x8, starting transfers between devices, shifted(): lax.ppermute(value, axis, [(source, source + steps) for source in range(f...  19.1 us
    gather x1, local copies, waits for them, and re-layouts, local(): outgoing = padded[send_rows[0]]  18.1 us
    dot_general x1, matrix products, local(): jnp.einsum('kvc,kco->vo', picked, weights, preferred_element_type=jnp.flo...  6.09 us
  transfers between devices with their start and end apart: 9, of which 5 were waited for; matrix products, arithmetic and copies ran while one was open for 1% of the time, Pallas kernels for 0%

commit v1 on v0

v1 whole, which is shorter than its diff:
```python
import jax
import jax.numpy as jnp
from jax import lax
from jax.experimental import pallas as pl
from jax.experimental.pallas import tpu as pltpu
from jax.sharding import PartitionSpec as P

GRID = 8
V = 1024
HALF = V // 2
HALO = 768
OFFS = 27
PAIRS = 14
ZERO = 9 * V
ROWS = ZERO + 8
BLOCK_OF = (8, 2, 5, 6, 3, 7, 1, 4)


def shift(value, step_row, step_col):
    pairs = [
        (row * GRID + col, (row + step_row) * GRID + col + step_col)
        for row in range(GRID)
        for col in range(GRID)
        if 0 <= row + step_row < GRID and 0 <= col + step_col < GRID
    ]
    return lax.ppermute(value, "space", pairs)


def digits(rows):
    parts = []
    for row in rows:
        parts += [row >> 5, row & 31]
    table = jnp.stack(parts, axis=0).astype(jnp.bfloat16)
    return jnp.pad(table, ((0, 8 - len(parts)), (0, V - HALO)))


def conv_kernel(par_ref, gm_ref, own_ref, up_ref, dn_ref, xp_ref, xm_ref, w0_ref, w1_ref,
                out_ref, table, lut, comp, index, lhs, wall, sem):
    par = par_ref[0]
    sources = [own_ref.at[pl.ds(0, 72)], up_ref.at[pl.ds(0, 72)], dn_ref.at[pl.ds(0, 72)]]
    for ref in (xp_ref, xm_ref):
        sources += [ref.at[pl.ds(72 * i, 72)] for i in range(3)]

    for number, block in enumerate(BLOCK_OF):
        step_col = (-1, 0, 1, -1, 1, -1, 0, 1)[number]
        at = 2 * (step_col + 1)
        pieces = sources[block][64:72, :HALO].astype(jnp.float32)
        slot = (pieces[at:at + 1] * 32.0 + pieces[at + 1:at + 2]).astype(jnp.int32)
        slot = jnp.where(slot >= V, ZERO, slot + block * V)
        for j in range(HALO // 128):
            lut[6 * number + j:6 * number + j + 1, :] = slot[:, 128 * j:128 * (j + 1)]

    for k0 in range(0, 32, 8):
        rows = min(8, OFFS - k0)
        for c in range(HALF // 128):
            here = gm_ref[k0:k0 + rows, pl.ds(pl.multiple_of(par * HALF + 128 * c, 128), 128)]
            if rows < 8:
                here = jnp.concatenate([here, jnp.full((8 - rows, 128), 8 * HALO + V, jnp.int32)], axis=0)
            slot = here - V
            hi = lax.shift_right_arithmetic(slot, 7)
            lo = slot & 127
            got = jnp.where(slot < 0, here, ZERO)
            for t in range(8 * HALO // 128):
                line = jnp.broadcast_to(lut[t:t + 1, :], (8, 128))
                value = jnp.take_along_axis(line, lo, axis=1)
                got = jnp.where(hi == t, value, got)
            comp[k0:k0 + 8, 128 * c:128 * (c + 1)] = got
    copy = pltpu.make_async_copy(comp, index, sem)
    copy.start()

    for block, source in enumerate(sources):
        for c in range(V // 128):
            x = source[0:64, 128 * c:128 * (c + 1)].astype(jnp.float32)
            x = jnp.concatenate([x, x], axis=0)
            table[block * V + 128 * c:block * V + 128 * (c + 1), :] = x.T
    table[ZERO:ROWS, :] = jnp.zeros((8, 128), jnp.float32)

    for k in range(OFFS):
        for side, w_ref in ((par, w0_ref), (1 - par, w1_ref)):
            wall[pl.ds(pl.multiple_of(64 * k + 32 * side, 32), 32), :] = w_ref[32 * k:32 * k + 32, :]
    wall[64 * OFFS:, :] = jnp.zeros((64, 256), jnp.bfloat16)
    copy.wait()

    sub = lax.broadcasted_iota(jnp.int32, (8, 128), 0)
    lane = lax.broadcasted_iota(jnp.int32, (8, 128), 1)
    masks = [sub == j for j in range(8)]
    left = lane < 64

    for pair in range(PAIRS):
        @pl.loop(0, HALF // 32)
        def _(step):
            base = pl.multiple_of(step * 32, 32)
            tiles = []
            for g in range(4):
                sides = []
                for k in (2 * pair, 2 * pair + 1):
                    acc = None
                    for j in range(8):
                        if k >= OFFS:
                            acc = jnp.zeros((8, 128), jnp.float32)
                            continue
                        row = table[pl.ds(index[k, base + 8 * g + j], 8, stride=0), :]
                        acc = row if acc is None else jnp.where(masks[j], row, acc)
                    sides.append(acc)
                tiles.append(jnp.where(left, sides[0], sides[1]))
            lhs[pl.ds(base, 32), 128 * pair:128 * (pair + 1)] = jnp.concatenate(tiles, axis=0).astype(jnp.bfloat16)

    total = jnp.dot(lhs[...], wall[...], preferred_element_type=jnp.float32)
    out_ref[...] = total.T


def add_kernel(got_ref, out_ref):
    for half in range(2):
        total = got_ref[half]
        for p in range(1, 4):
            total = total + got_ref[2 * p + half]
        out_ref[HALF * half:HALF * (half + 1), :] = total.T.astype(jnp.bfloat16)


def local(features, weights, send_rows, gather_map):
    width = features.shape[1]
    par = lax.axis_index("chan") % 2
    flip = [(i, i ^ 1) for i in range(8)]
    duo = [[2 * i, 2 * i + 1] for i in range(4)]
    w0 = weights.reshape(OFFS * width, 256)
    both = lax.all_gather(features.T, "chan", axis=0, tiled=True, axis_index_groups=duo)
    rows = send_rows[0]
    own = jnp.concatenate([both, digits([rows[3], rows[3], rows[4]])], axis=0)
    to_up = jnp.concatenate([both, digits([rows[5], rows[6], rows[7]])], axis=0)
    to_dn = jnp.concatenate([both, digits([rows[0], rows[1], rows[2]])], axis=0)
    up = shift(to_up, 1, 0)
    dn = shift(to_dn, -1, 0)
    w1 = lax.ppermute(w0, "chan", flip)
    strip = jnp.concatenate([own, up, dn], axis=0)
    xp = shift(strip, 0, 1)
    xm = shift(strip, 0, -1)
    vmem = pl.BlockSpec(memory_space=pltpu.VMEM)
    part = pl.pallas_call(
        conv_kernel,
        out_shape=jax.ShapeDtypeStruct((256, HALF), jnp.float32),
        in_specs=[pl.BlockSpec(memory_space=pltpu.SMEM)] + [vmem] * 8,
        out_specs=vmem,
        scratch_shapes=[
            pltpu.VMEM((ROWS, 128), jnp.float32),
            pltpu.VMEM((48, 128), jnp.int32),
            pltpu.VMEM((32, HALF), jnp.int32),
            pltpu.SMEM((32, HALF), jnp.int32),
            pltpu.VMEM((HALF, 128 * PAIRS), jnp.bfloat16),
            pltpu.VMEM((128 * PAIRS, 256), jnp.bfloat16),
            pltpu.SemaphoreType.DMA,
        ],
        compiler_params=pltpu.CompilerParams(vmem_limit_bytes=40 * 2**20),
        name="conv",
    )(par.reshape(1).astype(jnp.int32), gather_map, own, up, dn, xp, xm, w0, w1)
    got = lax.all_to_all(part, "chan", 0, 0, tiled=True).reshape(8, 32, HALF)
    return pl.pallas_call(
        add_kernel,
        out_shape=jax.ShapeDtypeStruct((V, 32), jnp.bfloat16),
        in_specs=[vmem],
        out_specs=vmem,
        name="add",
    )(got)


def solution(mesh):
    in_specs = (P("space", "chan"), P(None, "chan", None), P("space", None, None), P(None, "space"))
    out_specs = P("space", "chan")
    return jax.shard_map(local, mesh=mesh, in_specs=in_specs, out_specs=out_specs, check_vma=False)
```

time: 243 us -> 90.8 us (0.37)
  the two profiles are of different devices: /device:TPU:2 before, /device:TPU:26 now
where the time goes in v1:
time: 90.8 us; the launch traced here: 90.4 us
  Pallas kernels  33.1 us (36%)
  blocking collectives  31.5 us (35%)
  starting transfers between devices  15.5 us (17%)
  waiting for transfers between devices  7.2 us (8%)
  local copies, waits for them, and re-layouts  1.85 us (2%)
  other arithmetic  1.15 us (1%)
    pallas_call x1, Pallas kernels, local(): pl.pallas_call(conv_kernel, out_shape=jax.ShapeDtypeStruct((256, HALF), j...  31.2 us
    all_to_all x1, blocking collectives, local(): got = lax.all_to_all(part, 'chan', 0, 0, tiled=True).reshape(8, 32, HALF)  26.1 us
    ppermute x4, starting transfers between devices, shift(): return lax.ppermute(value, 'space', pairs)  11.4 us
    all_gather x1, blocking collectives, local(): lax.all_gather(features.T, 'chan', axis=0, tiled=True, axis_index_groups=...  5.4 us
    ppermute x1, starting transfers between devices, local(): w1 = lax.ppermute(w0, 'chan', flip)  4.09 us
    ppermute x1, waiting for transfers between devices, local(): w1 = lax.ppermute(w0, 'chan', flip)  4.03 us
    ppermute x4, waiting for transfers between devices, shift(): return lax.ppermute(value, 'space', pairs)  3.17 us
    pallas_call x1, Pallas kernels, local(): pl.pallas_call(add_kernel, out_shape=jax.ShapeDtypeStruct((V, 32), jnp.bf...  1.89 us
  transfers between devices with their start and end apart: 5, of which 2 were waited for; matrix products, arithmetic and copies ran while one was open for 0% of the time, Pallas kernels for 0%

profile of v1, /device:TPU:26, one launch (start us, length us, event | category | flops | bytes accessed | tf_op | source)
XLA Modules:
  0.0 90.4 jit_solution(2092653461572310627)
XLA Ops:
  0.0 0.0 copy-start.2
  0.0 1.1 %convert_bitcast_fusion.2 = (bf16[1,768]{1,0:T(2,128)(2,1)S(1)}, bf16[1,768]{1,0:T(2,128)(2,1)S(1)}, bf16[1,768]{1,0:T(2,128)(2,1)S(1)}, bf16[1,768]{1,0:T(2,128...) fusion(s32[1,8,768]{2,1,0:T(8,128)} %param.6), kind=kLoop, calls=%fused_computation.9 | loop fusion | flops 24576 | bytes 49152 | tf_op jit(solution)/shard_map/and | solution.py:32
  1.1 0.0 copy-done.2
  1.1 0.0 copy-start
  1.1 5.4 %all_gather.3 = bf16[64,1024]{1,0:T(8,128)(2,1)S(1)} all-gather(bf16[32,1024]{1,0:T(8,128)(2,1)S(1)} %bitcast.39), channel_id=1, replica_groups={{0,1},{2,3},{4,5},{6,7},{8,9},{10,11},{12,13},{14,15},{16,17},{18,19},{..., dimensions={0}, use_global_device_ids=true | all-gather | bytes 196608 | tf_op jit(solution)/shard_map/all_gather | solution.py:126
  6.7 2.4 %collective-permute-start.1 = (bf16[72,1024]{1,0:T(8,128)(2,1)S(1)}, bf16[72,1024]{1,0:T(8,128)(2,1)S(1)}, u32[]{:S(2)}, u32[]{:S(2)}) collective-permute-start(bf16[72,1024]{1,0:T(8,128)(2,1)S(1)} %get-tuple-element.5), channel_id=1, source_target_pairs={{64,0},{72,8},{80,16},{88,24},{96,32},{104,40},{112,48},{120,56},{... | collective-permute-start | bytes 442376 | tf_op jit(solution)/shard_map/ppermute | solution.py:26
  9.1 4.7 %collective-permute-start = (bf16[72,1024]{1,0:T(8,128)(2,1)S(1)}, bf16[72,1024]{1,0:T(8,128)(2,1)S(1)}, u32[]{:S(2)}, u32[]{:S(2)}) collective-permute-start(bf16[72,1024]{1,0:T(8,128)(2,1)S(1)} %get-tuple-element.6), channel_id=1, source_target_pairs={{0,64},{8,72},{16,80},{24,88},{32,96},{40,104},{48,112},{56,120},{... | collective-permute-start | bytes 442376 | tf_op jit(solution)/shard_map/ppermute | solution.py:26
  13.8 0.0 copy-done
  13.8 0.0 copy-start.1
  13.8 4.1 %collective-permute-start.4 = (bf16[864,256]{1,0:T(8,128)(2,1)S(1)}, bf16[864,256]{1,0:T(8,128)(2,1)S(1)}, u32[]{:S(2)}, u32[]{:S(2)}) collective-permute-start(bf16[864,256]{1,0:T(8,128)(2,1)S(1)} %bitcast.37), channel_id=1, source_target_pairs={{0,1},{1,0},{2,3},{3,2},{4,5},{5,4},{6,7},{7,6},{8,9},{9,8},{10,11... | collective-permute-start | bytes 1327112 | tf_op jit(solution)/shard_map/ppermute | solution.py:133
  17.9 0.0 collective-permute-done.1.dn_ref
  17.9 0.0 collective-permute-done.up_ref
  17.9 1.9 %collective-permute-start.3 = (bf16[216,1024]{1,0:T(8,128)(2,1)S(1)}, bf16[216,1024]{1,0:T(8,128)(2,1)S(1)}, u32[]{:S(2)}, u32[]{:S(2)}) collective-permute-start(bf16[216,1024]{1,0:T(8,128)(2,1)S(1)} %pad_maximum_fusion), channel_id=1, source_target_pairs={{8,0},{16,8},{24,16},{32,24},{40,32},{48,40},{56,48},{72,64},{80,7... | collective-permute-start | bytes 1327112 | tf_op jit(solution)/shard_map/ppermute | solution.py:26
  19.9 2.4 %collective-permute-start.2 = (bf16[216,1024]{1,0:T(8,128)(2,1)S(1)}, bf16[216,1024]{1,0:T(8,128)(2,1)S(1)}, u32[]{:S(2)}, u32[]{:S(2)}) collective-permute-start(bf16[216,1024]{1,0:T(8,128)(2,1)S(1)} %pad_maximum_fusion), channel_id=1, source_target_pairs={{0,8},{8,16},{16,24},{24,32},{32,40},{40,48},{48,56},{64,72},{72,8... | collective-permute-start | bytes 1327112 | tf_op jit(solution)/shard_map/ppermute | solution.py:26
  22.3 4.0 %collective-permute-done.4.w1_ref = bf16[864,256]{1,0:T(8,128)(2,1)S(1)} collective-permute-done((bf16[864,256]{1,0:T(8,128)(2,1)S(1)}, bf16[864,256]{1,0:T(8,128)(2,1)S(1)}, u32[]{:S(2)}, u32[]{:S(2)}) %collective-permute-start.4) | collective-permute-done | bytes 442400 | tf_op jit(solution)/shard_map/ppermute | solution.py:133
  26.3 0.0 collective-permute-done.3.xm_ref
  26.3 3.2 %collective-permute-done.2.xp_ref = bf16[216,1024]{1,0:T(8,128)(2,1)S(1)} collective-permute-done((bf16[216,1024]{1,0:T(8,128)(2,1)S(1)}, bf16[216,1024]{1,0:T(8,128)(2,1)S(1)}, u32[]{:S(2)}, u32[]{:S(2)}) %collective-permute-start.2) | collective-permute-done | bytes 442400 | tf_op jit(solution)/shard_map/ppermute | solution.py:26
  29.5 0.0 copy-done.1
  29.5 31.2 %conv.1 = f32[256,512]{1,0:T(8,128)S(1)} custom-call(s32[1]{0:T(128)} %bitcast.par_ref, s32[27,1024]{1,0:T(8,128)S(1)} %copy-done.1, bf16[72,1024]{1,0:T(8,128)(2,1)S(1)} %get-tuple-element.7.own_ref, bf16[72,1024]{1,0:T(8,128)(2,1)S(1)} %collective-permute-done.up_ref, bf16[72,1024]{1,0:T(8,128)(2,1)S(1)} %collective-permute-done.1.dn_ref, ...), custom_call_target="tpu_custom_call" | custom-call | tf_op jit(solution)/shard_map/conv/pallas_call | solution.py:138
  60.7 26.1 %all_to_all.9.got_ref = f32[8,32,512]{2,1,0:T(8,128)} all-to-all(f32[8,32,512]{2,1,0:T(8,128)S(1)} %bitcast.36), channel_id=1, replica_groups=mesh['space'=64,'chan'=8] {'chan'}, dimensions={0} | all-to-all | bytes 1048576 | tf_op jit(solution)/shard_map/all_to_all | solution.py:155
  86.8 1.9 %add.12 = bf16[1024,32]{1,0:T(8,128)(2,1)} custom-call(f32[8,32,512]{2,1,0:T(8,128)} %all_to_all.9.got_ref), custom_call_target="tpu_custom_call" | custom-call | tf_op jit(solution)/shard_map/add/pallas_call | solution.py:156
  88.7 1.7 %copy.5 = bf16[1024,32]{0,1:T(8,128)(2,1)} copy(bf16[1024,32]{1,0:T(8,128)(2,1)} %add.12) | data formatting | bytes 131072 | tf_op jit(solution)/shard_map/add/pallas_call | solution.py:156
  (6 shorter events, 0.2 us)
Async XLA Ops:
  0.0 1.1 %copy-start.2 = (bf16[1024,32]{0,1:T(8,128)(2,1)S(1)}, bf16[1024,32]{0,1:T(8,128)(2,1)}, u32[]{:S(2)}) copy-start(bf16[1024,32]{0,1:T(8,128)(2,1)} %param.4) | copy-start | bytes 196612
  1.1 12.7 %copy-start = (bf16[27,32,256]{2,1,0:T(8,128)(2,1)S(1)}, bf16[27,32,256]{2,1,0:T(8,128)(2,1)}, u32[]{:S(2)}) copy-start(bf16[27,32,256]{2,1,0:T(8,128)(2,1)} %param.5) | copy-start | bytes 1327108
  6.7 11.2 %collective-permute-start.1 = (bf16[72,1024]{1,0:T(8,128)(2,1)S(1)}, bf16[72,1024]{1,0:T(8,128)(2,1)S(1)}, u32[]{:S(2)}, u32[]{:S(2)}) collective-permute-start(bf16[72,1024]{1,0:T(8,128)(2,1)S(1)} %get-tuple-element.5), channel_id=1, source_target_pairs={{64,0},{72,8},{80,16},{88,24},{96,32},{104,40},{112,48},{120,56},{... | collective-permute-start | bytes 442376 | tf_op jit(solution)/shard_map/ppermute | solution.py:26
  9.1 8.8 %collective-permute-start = (bf16[72,1024]{1,0:T(8,128)(2,1)S(1)}, bf16[72,1024]{1,0:T(8,128)(2,1)S(1)}, u32[]{:S(2)}, u32[]{:S(2)}) collective-permute-start(bf16[72,1024]{1,0:T(8,128)(2,1)S(1)} %get-tuple-element.6), channel_id=1, source_target_pairs={{0,64},{8,72},{16,80},{24,88},{32,96},{40,104},{48,112},{56,120},{... | collective-permute-start | bytes 442376 | tf_op jit(solution)/shard_map/ppermute | solution.py:26
  13.8 15.7 %copy-start.1 = (s32[27,1024]{1,0:T(8,128)S(1)}, s32[27,1024]{1,0:T(8,128)}, u32[]{:S(2)}) copy-start(s32[27,1024]{1,0:T(8,128)} %gm_ref.1) | copy-start | bytes 331780
  13.8 12.5 %collective-permute-start.4 = (bf16[864,256]{1,0:T(8,128)(2,1)S(1)}, bf16[864,256]{1,0:T(8,128)(2,1)S(1)}, u32[]{:S(2)}, u32[]{:S(2)}) collective-permute-start(bf16[864,256]{1,0:T(8,128)(2,1)S(1)} %bitcast.37), channel_id=1, source_target_pairs={{0,1},{1,0},{2,3},{3,2},{4,5},{5,4},{6,7},{7,6},{8,9},{9,8},{10,11... | collective-permute-start | bytes 1327112 | tf_op jit(solution)/shard_map/ppermute | solution.py:133
  17.9 8.4 %collective-permute-start.3 = (bf16[216,1024]{1,0:T(8,128)(2,1)S(1)}, bf16[216,1024]{1,0:T(8,128)(2,1)S(1)}, u32[]{:S(2)}, u32[]{:S(2)}) collective-permute-start(bf16[216,1024]{1,0:T(8,128)(2,1)S(1)} %pad_maximum_fusion), channel_id=1, source_target_pairs={{8,0},{16,8},{24,16},{32,24},{40,32},{48,40},{56,48},{72,64},{80,7... | collective-permute-start | bytes 1327112 | tf_op jit(solution)/shard_map/ppermute | solution.py:26
  19.9 9.6 %collective-permute-start.2 = (bf16[216,1024]{1,0:T(8,128)(2,1)S(1)}, bf16[216,1024]{1,0:T(8,128)(2,1)S(1)}, u32[]{:S(2)}, u32[]{:S(2)}) collective-permute-start(bf16[216,1024]{1,0:T(8,128)(2,1)S(1)} %pad_maximum_fusion), channel_id=1, source_target_pairs={{0,8},{8,16},{16,24},{24,32},{32,40},{40,48},{48,56},{64,72},{72,8... | collective-permute-start | bytes 1327112 | tf_op jit(solution)/shard_map/ppermute | solution.py:26

commit v2 on v1

--- a/solution.py
+++ b/solution.py
@@ -64,7 +64,7 @@
                 line = jnp.broadcast_to(lut[t:t + 1, :], (8, 128))
                 value = jnp.take_along_axis(line, lo, axis=1)
                 got = jnp.where(hi == t, value, got)
-            comp[k0:k0 + 8, 128 * c:128 * (c + 1)] = got
+            comp[32 * c + k0:32 * c + k0 + 8, :] = got
     copy = pltpu.make_async_copy(comp, index, sem)
     copy.start()
 
@@ -86,24 +86,33 @@
     masks = [sub == j for j in range(8)]
     left = lane < 64
 
-    for pair in range(PAIRS):
-        @pl.loop(0, HALF // 32)
-        def _(step):
-            base = pl.multiple_of(step * 32, 32)
+    def pick(step, last):
+        pair = PAIRS - 1 if last else step >> 2
+        quarter = step & 3
+        line = quarter * 32 + 2 * pair
+        for h in range(0, 128, 16):
             tiles = []
-            for g in range(4):
+            for g in range(h, h + 16, 8):
                 sides = []
-                for k in (2 * pair, 2 * pair + 1):
+                for side in range(1 if last else 2):
                     acc = None
                     for j in range(8):
-                        if k >= OFFS:
-                            acc = jnp.zeros((8, 128), jnp.float32)
-                            continue
-                        row = table[pl.ds(index[k, base + 8 * g + j], 8, stride=0), :]
+                        at = index.at[pl.ds(side, 127), pl.ds(g + j, 1)][line, 0]
+                        row = table[pl.ds(at, 8, stride=0), :]
                         acc = row if acc is None else jnp.where(masks[j], row, acc)
                     sides.append(acc)
-                tiles.append(jnp.where(left, sides[0], sides[1]))
-            lhs[pl.ds(base, 32), 128 * pair:128 * (pair + 1)] = jnp.concatenate(tiles, axis=0).astype(jnp.bfloat16)
+                tiles.append(jnp.where(left, sides[0], 0.0 if last else sides[1]))
+            rows = pl.ds(pl.multiple_of(quarter * 128 + h, 16), 16)
+            lanes = pl.ds(pl.multiple_of(128 * pair, 128), 128)
+            lhs[rows, lanes] = jnp.concatenate(tiles, axis=0).astype(jnp.bfloat16)
+
+    @pl.loop(0, 4 * (PAIRS - 1))
+    def _(step):
+        pick(step, False)
+
+    @pl.loop(0, 4)
+    def _(step):
+        pick(step, True)
 
     total = jnp.dot(lhs[...], wall[...], preferred_element_type=jnp.float32)
     out_ref[...] = total.T
@@ -114,7 +123,7 @@
         total = got_ref[half]
         for p in range(1, 4):
             total = total + got_ref[2 * p + half]
-        out_ref[HALF * half:HALF * (half + 1), :] = total.T.astype(jnp.bfloat16)
+        out_ref[:, HALF * half:HALF * (half + 1)] = total.astype(jnp.bfloat16)
 
 
 def local(features, weights, send_rows, gather_map):
@@ -143,8 +152,8 @@
         scratch_shapes=[
             pltpu.VMEM((ROWS, 128), jnp.float32),
             pltpu.VMEM((48, 128), jnp.int32),
-            pltpu.VMEM((32, HALF), jnp.int32),
-            pltpu.SMEM((32, HALF), jnp.int32),
+            pltpu.VMEM((128, 128), jnp.int32),
+            pltpu.SMEM((128, 128), jnp.int32),
             pltpu.VMEM((HALF, 128 * PAIRS), jnp.bfloat16),
             pltpu.VMEM((128 * PAIRS, 256), jnp.bfloat16),
             pltpu.SemaphoreType.DMA,
@@ -155,11 +164,11 @@
     got = lax.all_to_all(part, "chan", 0, 0, tiled=True).reshape(8, 32, HALF)
     return pl.pallas_call(
         add_kernel,
-        out_shape=jax.ShapeDtypeStruct((V, 32), jnp.bfloat16),
+        out_shape=jax.ShapeDtypeStruct((32, V), jnp.bfloat16),
         in_specs=[vmem],
         out_specs=vmem,
         name="add",
-    )(got)
+    )(got).T
 
 
 def solution(mesh):

time: 90.8 us -> 70.3 us (0.77)
  Pallas kernels: 33.1 us -> 14.3 us
  local copies, waits for them, and re-layouts: 1.85 us -> 0.15 us
    pallas_call x1, Pallas kernels: 31.2 us -> 12.6 us  [local(): pl.pallas_call(conv_kernel, out_shape=jax.ShapeDtypeStruct((256, HALF), j...]
    pallas_call x1 -> x0, local copies, waits for them, and re-layouts: 1.69 us -> none  [local(): pl.pallas_call(add_kernel, out_shape=jax.ShapeDtypeStruct((V, 32), jnp.bf...]
where the time goes in v2:
time: 70.3 us; the launch traced here: 69.9 us
  blocking collectives  31.5 us (45%)
  starting transfers between devices  15.5 us (22%)
  Pallas kernels  14.3 us (20%)
  waiting for transfers between devices  7.2 us (10%)
  other arithmetic  1.16 us (2%)
    all_to_all x1, blocking collectives, local(): got = lax.all_to_all(part, 'chan', 0, 0, tiled=True).reshape(8, 32, HALF)  26.1 us
    pallas_call x1, Pallas kernels, local(): pl.pallas_call(conv_kernel, out_shape=jax.ShapeDtypeStruct((256, HALF), j...  12.6 us
    ppermute x4, starting transfers between devices, shift(): return lax.ppermute(value, 'space', pairs)  11.4 us
    all_gather x1, blocking collectives, local(): lax.all_gather(features.T, 'chan', axis=0, tiled=True, axis_index_groups=...  5.4 us
    ppermute x1, starting transfers between devices, local(): w1 = lax.ppermute(w0, 'chan', flip)  4.09 us
    ppermute x1, waiting for transfers between devices, local(): w1 = lax.ppermute(w0, 'chan', flip)  4.03 us
    ppermute x4, waiting for transfers between devices, shift(): return lax.ppermute(value, 'space', pairs)  3.17 us
    pallas_call x1, Pallas kernels, local(): pl.pallas_call(add_kernel, out_shape=jax.ShapeDtypeStruct((32, V), jnp.bf...  1.7 us
  transfers between devices with their start and end apart: 5, of which 2 were waited for; matrix products, arithmetic and copies ran while one was open for 0% of the time, Pallas kernels for 0%

profile of v2, /device:TPU:26, one launch (start us, length us, event | category | flops | bytes accessed | tf_op | source)
XLA Modules:
  0.0 69.9 jit_solution(13109319460043461971)
XLA Ops:
  0.0 0.0 copy-start.2
  0.0 1.1 %convert_bitcast_fusion.2 = (bf16[1,768]{1,0:T(2,128)(2,1)S(1)}, bf16[1,768]{1,0:T(2,128)(2,1)S(1)}, bf16[1,768]{1,0:T(2,128)(2,1)S(1)}, bf16[1,768]{1,0:T(2,128...) fusion(s32[1,8,768]{2,1,0:T(8,128)} %param.6), kind=kLoop, calls=%fused_computation.9 | loop fusion | flops 24576 | bytes 49152 | tf_op jit(solution)/shard_map/and | solution.py:32
  1.1 0.0 copy-done.2
  1.1 0.0 copy-start
  1.1 5.4 %all_gather.3 = bf16[64,1024]{1,0:T(8,128)(2,1)S(1)} all-gather(bf16[32,1024]{1,0:T(8,128)(2,1)S(1)} %bitcast.40), channel_id=1, replica_groups={{0,1},{2,3},{4,5},{6,7},{8,9},{10,11},{12,13},{14,15},{16,17},{18,19},{..., dimensions={0}, use_global_device_ids=true | all-gather | bytes 196608 | tf_op jit(solution)/shard_map/all_gather | solution.py:135
  6.7 2.4 %collective-permute-start.1 = (bf16[72,1024]{1,0:T(8,128)(2,1)S(1)}, bf16[72,1024]{1,0:T(8,128)(2,1)S(1)}, u32[]{:S(2)}, u32[]{:S(2)}) collective-permute-start(bf16[72,1024]{1,0:T(8,128)(2,1)S(1)} %get-tuple-element.5), channel_id=1, source_target_pairs={{64,0},{72,8},{80,16},{88,24},{96,32},{104,40},{112,48},{120,56},{... | collective-permute-start | bytes 442376 | tf_op jit(solution)/shard_map/ppermute | solution.py:26
  9.1 4.7 %collective-permute-start = (bf16[72,1024]{1,0:T(8,128)(2,1)S(1)}, bf16[72,1024]{1,0:T(8,128)(2,1)S(1)}, u32[]{:S(2)}, u32[]{:S(2)}) collective-permute-start(bf16[72,1024]{1,0:T(8,128)(2,1)S(1)} %get-tuple-element.6), channel_id=1, source_target_pairs={{0,64},{8,72},{16,80},{24,88},{32,96},{40,104},{48,112},{56,120},{... | collective-permute-start | bytes 442376 | tf_op jit(solution)/shard_map/ppermute | solution.py:26
  13.8 0.0 copy-done
  13.8 0.0 copy-start.1
  13.8 4.1 %collective-permute-start.4 = (bf16[864,256]{1,0:T(8,128)(2,1)S(1)}, bf16[864,256]{1,0:T(8,128)(2,1)S(1)}, u32[]{:S(2)}, u32[]{:S(2)}) collective-permute-start(bf16[864,256]{1,0:T(8,128)(2,1)S(1)} %bitcast.38), channel_id=1, source_target_pairs={{0,1},{1,0},{2,3},{3,2},{4,5},{5,4},{6,7},{7,6},{8,9},{9,8},{10,11... | collective-permute-start | bytes 1327112 | tf_op jit(solution)/shard_map/ppermute | solution.py:142
  17.9 0.0 collective-permute-done.1.dn_ref
  17.9 0.0 collective-permute-done.up_ref
  18.0 1.9 %collective-permute-start.3 = (bf16[216,1024]{1,0:T(8,128)(2,1)S(1)}, bf16[216,1024]{1,0:T(8,128)(2,1)S(1)}, u32[]{:S(2)}, u32[]{:S(2)}) collective-permute-start(bf16[216,1024]{1,0:T(8,128)(2,1)S(1)} %pad_maximum_fusion), channel_id=1, source_target_pairs={{8,0},{16,8},{24,16},{32,24},{40,32},{48,40},{56,48},{72,64},{80,7... | collective-permute-start | bytes 1327112 | tf_op jit(solution)/shard_map/ppermute | solution.py:26
  19.9 2.4 %collective-permute-start.2 = (bf16[216,1024]{1,0:T(8,128)(2,1)S(1)}, bf16[216,1024]{1,0:T(8,128)(2,1)S(1)}, u32[]{:S(2)}, u32[]{:S(2)}) collective-permute-start(bf16[216,1024]{1,0:T(8,128)(2,1)S(1)} %pad_maximum_fusion), channel_id=1, source_target_pairs={{0,8},{8,16},{16,24},{24,32},{32,40},{40,48},{48,56},{64,72},{72,8... | collective-permute-start | bytes 1327112 | tf_op jit(solution)/shard_map/ppermute | solution.py:26
  22.3 4.0 %collective-permute-done.4.w1_ref = bf16[864,256]{1,0:T(8,128)(2,1)S(1)} collective-permute-done((bf16[864,256]{1,0:T(8,128)(2,1)S(1)}, bf16[864,256]{1,0:T(8,128)(2,1)S(1)}, u32[]{:S(2)}, u32[]{:S(2)}) %collective-permute-start.4) | collective-permute-done | bytes 442400 | tf_op jit(solution)/shard_map/ppermute | solution.py:142
  26.3 0.0 collective-permute-done.3.xm_ref
  26.3 3.2 %collective-permute-done.2.xp_ref = bf16[216,1024]{1,0:T(8,128)(2,1)S(1)} collective-permute-done((bf16[216,1024]{1,0:T(8,128)(2,1)S(1)}, bf16[216,1024]{1,0:T(8,128)(2,1)S(1)}, u32[]{:S(2)}, u32[]{:S(2)}) %collective-permute-start.2) | collective-permute-done | bytes 442400 | tf_op jit(solution)/shard_map/ppermute | solution.py:26
  29.5 0.0 copy-done.1
  29.5 12.6 %conv.1 = f32[256,512]{1,0:T(8,128)S(1)} custom-call(s32[1]{0:T(128)} %bitcast.par_ref, s32[27,1024]{1,0:T(8,128)S(1)} %copy-done.1, bf16[72,1024]{1,0:T(8,128)(2,1)S(1)} %get-tuple-element.7.own_ref, bf16[72,1024]{1,0:T(8,128)(2,1)S(1)} %collective-permute-done.up_ref, bf16[72,1024]{1,0:T(8,128)(2,1)S(1)} %collective-permute-done.1.dn_ref, ...), custom_call_target="tpu_custom_call" | custom-call | tf_op jit(solution)/shard_map/conv/pallas_call | solution.py:147
  42.1 26.1 %all_to_all.9.got_ref = f32[8,32,512]{2,1,0:T(8,128)} all-to-all(f32[8,32,512]{2,1,0:T(8,128)S(1)} %bitcast.37), channel_id=1, replica_groups=mesh['space'=64,'chan'=8] {'chan'}, dimensions={0} | all-to-all | bytes 1048576 | tf_op jit(solution)/shard_map/all_to_all | solution.py:164
  68.2 1.7 %add.12 = bf16[32,1024]{1,0:T(8,128)(2,1)} custom-call(f32[8,32,512]{2,1,0:T(8,128)} %all_to_all.9.got_ref), custom_call_target="tpu_custom_call" | custom-call | tf_op jit(solution)/shard_map/add/pallas_call | solution.py:165
  (6 shorter events, 0.2 us)
Async XLA Ops:
  0.0 1.1 %copy-start.2 = (bf16[1024,32]{0,1:T(8,128)(2,1)S(1)}, bf16[1024,32]{0,1:T(8,128)(2,1)}, u32[]{:S(2)}) copy-start(bf16[1024,32]{0,1:T(8,128)(2,1)} %param.4) | copy-start | bytes 196612
  1.1 12.7 %copy-start = (bf16[27,32,256]{2,1,0:T(8,128)(2,1)S(1)}, bf16[27,32,256]{2,1,0:T(8,128)(2,1)}, u32[]{:S(2)}) copy-start(bf16[27,32,256]{2,1,0:T(8,128)(2,1)} %param.5) | copy-start | bytes 1327108
  6.7 11.2 %collective-permute-start.1 = (bf16[72,1024]{1,0:T(8,128)(2,1)S(1)}, bf16[72,1024]{1,0:T(8,128)(2,1)S(1)}, u32[]{:S(2)}, u32[]{:S(2)}) collective-permute-start(bf16[72,1024]{1,0:T(8,128)(2,1)S(1)} %get-tuple-element.5), channel_id=1, source_target_pairs={{64,0},{72,8},{80,16},{88,24},{96,32},{104,40},{112,48},{120,56},{... | collective-permute-start | bytes 442376 | tf_op jit(solution)/shard_map/ppermute | solution.py:26
  9.1 8.8 %collective-permute-start = (bf16[72,1024]{1,0:T(8,128)(2,1)S(1)}, bf16[72,1024]{1,0:T(8,128)(2,1)S(1)}, u32[]{:S(2)}, u32[]{:S(2)}) collective-permute-start(bf16[72,1024]{1,0:T(8,128)(2,1)S(1)} %get-tuple-element.6), channel_id=1, source_target_pairs={{0,64},{8,72},{16,80},{24,88},{32,96},{40,104},{48,112},{56,120},{... | collective-permute-start | bytes 442376 | tf_op jit(solution)/shard_map/ppermute | solution.py:26
  13.8 15.7 %copy-start.1 = (s32[27,1024]{1,0:T(8,128)S(1)}, s32[27,1024]{1,0:T(8,128)}, u32[]{:S(2)}) copy-start(s32[27,1024]{1,0:T(8,128)} %gm_ref.1) | copy-start | bytes 331780
  13.8 12.5 %collective-permute-start.4 = (bf16[864,256]{1,0:T(8,128)(2,1)S(1)}, bf16[864,256]{1,0:T(8,128)(2,1)S(1)}, u32[]{:S(2)}, u32[]{:S(2)}) collective-permute-start(bf16[864,256]{1,0:T(8,128)(2,1)S(1)} %bitcast.38), channel_id=1, source_target_pairs={{0,1},{1,0},{2,3},{3,2},{4,5},{5,4},{6,7},{7,6},{8,9},{9,8},{10,11... | collective-permute-start | bytes 1327112 | tf_op jit(solution)/shard_map/ppermute | solution.py:142
  18.0 8.4 %collective-permute-start.3 = (bf16[216,1024]{1,0:T(8,128)(2,1)S(1)}, bf16[216,1024]{1,0:T(8,128)(2,1)S(1)}, u32[]{:S(2)}, u32[]{:S(2)}) collective-permute-start(bf16[216,1024]{1,0:T(8,128)(2,1)S(1)} %pad_maximum_fusion), channel_id=1, source_target_pairs={{8,0},{16,8},{24,16},{32,24},{40,32},{48,40},{56,48},{72,64},{80,7... | collective-permute-start | bytes 1327112 | tf_op jit(solution)/shard_map/ppermute | solution.py:26
  19.9 9.6 %collective-permute-start.2 = (bf16[216,1024]{1,0:T(8,128)(2,1)S(1)}, bf16[216,1024]{1,0:T(8,128)(2,1)S(1)}, u32[]{:S(2)}, u32[]{:S(2)}) collective-permute-start(bf16[216,1024]{1,0:T(8,128)(2,1)S(1)} %pad_maximum_fusion), channel_id=1, source_target_pairs={{0,8},{8,16},{16,24},{24,32},{32,40},{40,48},{48,56},{64,72},{72,8... | collective-permute-start | bytes 1327112 | tf_op jit(solution)/shard_map/ppermute | solution.py:26

commit v3 on v2

v3 whole, which is shorter than its diff:
```python
import jax
import jax.numpy as jnp
from jax import lax
from jax.experimental import pallas as pl
from jax.experimental.pallas import tpu as pltpu
from jax.sharding import PartitionSpec as P

GRID = 8
V = 1024
HALF = V // 2
HALO = 768
OFFS = 27
CENTRE = 13
PAIRS = 14
MSG = 80
ZERO = 9 * V
ROWS = ZERO + 8
STEPS = ((-1, -1), (-1, 0), (-1, 1), (0, -1), (0, 1), (1, -1), (1, 0), (1, 1))


def shift(value, step_row):
    pairs = [
        (row * GRID + col, (row + step_row) * GRID + col)
        for row in range(GRID)
        for col in range(GRID)
        if 0 <= row + step_row < GRID
    ]
    return lax.ppermute(value, "space", pairs)


def conv_kernel(where_ref, gm_ref, both_ref, outer_ref, w0_ref, w1_ref,
                out_ref, table, digit, lut, comp, index, lhs, wall, sem):
    par = where_ref[0]
    core = where_ref[1]
    sources = [both_ref.at[pl.ds(MSG * i, MSG)] for i in range(6)]
    sources += [outer_ref.at[pl.ds(MSG * i, MSG)] for i in range(3)]
    own_base = 3 * core

    for block, source in enumerate(sources):
        digit[16 * block:16 * block + 16, :] = source[64:80, :HALO].astype(jnp.float32)
    base_of = {
        0: own_base,
        1: jnp.where(core == 0, 6, 0),
        -1: jnp.where(core == 0, 3, 6),
    }
    for number, (step_row, step_col) in enumerate(STEPS):
        block = base_of[step_col] + (0, 1, 2)[step_row]
        high = digit[pl.ds(16 * block + number, 1), :]
        low = digit[pl.ds(16 * block + 8 + number, 1), :]
        slot = (high * 32.0 + low).astype(jnp.int32)
        slot = jnp.where(slot >= V, ZERO, slot + block * V)
        for j in range(HALO // 128):
            lut[6 * number + j:6 * number + j + 1, :] = slot[:, 128 * j:128 * (j + 1)]

    def compose(c):
        for k0 in range(0, 32, 8):
            rows = min(8, OFFS - k0)
            here = gm_ref[k0:k0 + rows, pl.ds(pl.multiple_of(par * HALF + 128 * c, 128), 128)]
            if rows < 8:
                here = jnp.concatenate([here, jnp.full((8 - rows, 128), 8 * HALO + V, jnp.int32)], axis=0)
            slot = here - V
            hi = lax.shift_right_arithmetic(slot, 7)
            lo = slot & 127
            got = jnp.where(slot < 0, here + own_base * V, ZERO)
            for t in range(8 * HALO // 128):
                line = jnp.broadcast_to(lut[t:t + 1, :], (8, 128))
                value = jnp.take_along_axis(line, lo, axis=1)
                got = jnp.where(hi == t, value, got)
            comp[32 * c + k0:32 * c + k0 + 8, :] = got
            if rows < 8:
                comp[32 * c + CENTRE:32 * c + CENTRE + 1, :] = got[rows - 1:rows, :]
        rows = pl.ds(32 * c, 32)
        copy = pltpu.make_async_copy(comp.at[rows], index.at[rows], sem.at[c])
        copy.start()
        return copy

    copies = [compose(c) for c in range(HALF // 128)]

    for block, source in enumerate(sources):
        for c in range(V // 128):
            x = source[0:64, 128 * c:128 * (c + 1)].astype(jnp.float32)
            x = jnp.concatenate([x, x], axis=0)
            table[block * V + 128 * c:block * V + 128 * (c + 1), :] = x.T
    table[ZERO:ROWS, :] = jnp.zeros((8, 128), jnp.float32)

    for place in range(OFFS):
        k = {CENTRE: OFFS - 1, OFFS - 1: CENTRE}.get(place, place)
        for side, w_ref in ((par, w0_ref), (1 - par, w1_ref)):
            wall[pl.ds(pl.multiple_of(64 * place + 32 * side, 32), 32), :] = w_ref[32 * k:32 * k + 32, :]
    wall[64 * OFFS:, :] = jnp.zeros((64, 256), jnp.bfloat16)

    own = pl.multiple_of(own_base * V + par * HALF, 128)
    lhs[:, 128 * (PAIRS - 1):] = table[pl.ds(own, HALF), :].astype(jnp.bfloat16)

    sub = lax.broadcasted_iota(jnp.int32, (8, 128), 0)
    lane = lax.broadcasted_iota(jnp.int32, (8, 128), 1)
    masks = [sub == j for j in range(8)]
    left = lane < 64
    for copy in copies:
        copy.wait()

    @pl.loop(0, 4 * (PAIRS - 1))
    def _(step):
        pair = step >> 2
        quarter = step & 3
        line = quarter * 32 + 2 * pair
        for h in range(0, 128, 16):
            tiles = []
            for g in range(h, h + 16, 8):
                sides = []
                for side in range(2):
                    acc = None
                    for j in range(8):
                        at = index.at[pl.ds(side, 127), pl.ds(g + j, 1)][line, 0]
                        row = table[pl.ds(at, 8, stride=0), :]
                        acc = row if acc is None else jnp.where(masks[j], row, acc)
                    sides.append(acc)
                tiles.append(jnp.where(left, sides[0], sides[1]))
            rows = pl.ds(pl.multiple_of(quarter * 128 + h, 16), 16)
            lanes = pl.ds(pl.multiple_of(128 * pair, 128), 128)
            lhs[rows, lanes] = jnp.concatenate(tiles, axis=0).astype(jnp.bfloat16)

    total = jnp.dot(lhs[...], wall[...], preferred_element_type=jnp.float32)
    out_ref[...] = total.T


def add_kernel(got_ref, out_ref):
    for half in range(2):
        total = got_ref[half]
        for p in range(1, 4):
            total = total + got_ref[2 * p + half]
        out_ref[:, HALF * half:HALF * (half + 1)] = total.astype(jnp.bfloat16)


def local(features, weights, send_rows, gather_map):
    width = features.shape[1]
    par = lax.axis_index("chan") % 2
    core = lax.axis_index("space") % 2
    flip = [(i, i ^ 1) for i in range(8)]
    duo = [[2 * i, 2 * i + 1] for i in range(4)]
    chips = [[2 * i, 2 * i + 1] for i in range(GRID * GRID // 2)]
    facing = [
        (row * GRID + a, row * GRID + b)
        for row in range(GRID)
        for col in range(1, GRID - 1, 2)
        for a, b in ((col, col + 1), (col + 1, col))
    ]
    w0 = weights.reshape(OFFS * width, 256)
    mine = lax.all_gather(features.T, "chan", axis=0, tiled=True, axis_index_groups=duo)
    rows = jnp.pad(send_rows[0], ((0, 0), (0, V - HALO)))
    message = jnp.concatenate([mine, (rows >> 5).astype(jnp.bfloat16), (rows & 31).astype(jnp.bfloat16)], axis=0)
    up = shift(message, 1)
    dn = shift(message, -1)
    w1 = lax.ppermute(w0, "chan", flip)
    strip = jnp.concatenate([message, up, dn], axis=0)
    outer = lax.ppermute(strip, "space", facing)
    both = lax.all_gather(strip, "space", axis=0, tiled=True, axis_index_groups=chips)
    vmem = pl.BlockSpec(memory_space=pltpu.VMEM)
    part = pl.pallas_call(
        conv_kernel,
        out_shape=jax.ShapeDtypeStruct((256, HALF), jnp.float32),
        in_specs=[pl.BlockSpec(memory_space=pltpu.SMEM)] + [vmem] * 5,
        out_specs=vmem,
        scratch_shapes=[
            pltpu.VMEM((ROWS, 128), jnp.float32),
            pltpu.VMEM((144, HALO), jnp.float32),
            pltpu.VMEM((48, 128), jnp.int32),
            pltpu.VMEM((128, 128), jnp.int32),
            pltpu.SMEM((128, 128), jnp.int32),
            pltpu.VMEM((HALF, 128 * PAIRS), jnp.bfloat16),
            pltpu.VMEM((128 * PAIRS, 256), jnp.bfloat16),
            pltpu.SemaphoreType.DMA((4,)),
        ],
        compiler_params=pltpu.CompilerParams(vmem_limit_bytes=40 * 2**20),
        name="conv",
    )(jnp.stack([par, core]).astype(jnp.int32), gather_map, both, outer, w0, w1)
    got = lax.all_to_all(part, "chan", 0, 0, tiled=True).reshape(8, 32, HALF)
    return pl.pallas_call(
        add_kernel,
        out_shape=jax.ShapeDtypeStruct((32, V), jnp.bfloat16),
        in_specs=[vmem],
        out_specs=vmem,
        compiler_params=pltpu.CompilerParams(vmem_limit_bytes=4 * 2**20),
        name="add",
    )(got).T


def solution(mesh):
    in_specs = (P("space", "chan"), P(None, "chan", None), P("space", None, None), P(None, "space"))
    out_specs = P("space", "chan")
    return jax.shard_map(local, mesh=mesh, in_specs=in_specs, out_specs=out_specs, check_vma=False)
```

time: 70.3 us -> 76.7 us (1.091)
  waiting for transfers between devices: 7.2 us -> 13 us
  blocking collectives: 31.5 us -> 37.2 us
  starting transfers between devices: 15.5 us -> 12.6 us
  Pallas kernels: 14.3 us -> 12.6 us
  other arithmetic: 1.16 us -> 0.1 us
    ppermute x4 -> x2, starting transfers between devices: 11.4 us -> 6.75 us  [shift(): return lax.ppermute(value, 'space', pairs)]
    all_gather x0 -> x1, blocking collectives: none -> 3.57 us  [local(): lax.all_gather(strip, 'space', axis=0, tiled=True, axis_index_groups=chips)]
    ppermute x4 -> x2, waiting for transfers between devices: 3.17 us -> 6.48 us  [shift(): return lax.ppermute(value, 'space', pairs)]
    ppermute x1, waiting for transfers between devices: 4.03 us -> 6.53 us  [local(): w1 = lax.ppermute(w0, 'chan', flip)]
    all_to_all x1, blocking collectives: 26.1 us -> 28.1 us  [local(): got = lax.all_to_all(part, 'chan', 0, 0, tiled=True).reshape(8, 32, HALF)]
    ppermute x0 -> x1, starting transfers between devices: none -> 1.92 us  [local(): outer = lax.ppermute(strip, 'space', facing)]
    and x1 -> x0, other arithmetic: 1.09 us -> none  [digits(): parts += [row >> 5, row & 31]]
    pallas_call x1, Pallas kernels: 1.7 us -> 0.66 us  [local(): pl.pallas_call(add_kernel, out_shape=jax.ShapeDtypeStruct((32, V), jnp.bf...]
  transfers between devices with their start and end apart: 5 -> 4, of which waited for: 2 -> 3; matrix products, arithmetic and copies ran while one was open for 0% -> 0% of each run, Pallas kernels for 0% -> 0%
where the time goes in v3:
time: 76.7 us; the launch traced here: 76.3 us
  blocking collectives  37.2 us (49%)
  waiting for transfers between devices  13 us (17%)
  starting transfers between devices  12.6 us (16%)
  Pallas kernels  12.6 us (16%)
  local copies, waits for them, and re-layouts  0.77 us (1%)
    all_to_all x1, blocking collectives, local(): got = lax.all_to_all(part, 'chan', 0, 0, tiled=True).reshape(8, 32, HALF)  28.1 us
    pallas_call x1, Pallas kernels, local(): pl.pallas_call(conv_kernel, out_shape=jax.ShapeDtypeStruct((256, HALF), j...  12 us
    ppermute x2, starting transfers between devices, shift(): return lax.ppermute(value, 'space', pairs)  6.75 us
    ppermute x1, waiting for transfers between devices, local(): w1 = lax.ppermute(w0, 'chan', flip)  6.53 us
    ppermute x2, waiting for transfers between devices, shift(): return lax.ppermute(value, 'space', pairs)  6.48 us
    all_gather x1, blocking collectives, local(): lax.all_gather(features.T, 'chan', axis=0, tiled=True, axis_index_groups=...  5.53 us
    ppermute x1, starting transfers between devices, local(): w1 = lax.ppermute(w0, 'chan', flip)  3.89 us
    all_gather x1, blocking collectives, local(): lax.all_gather(strip, 'space', axis=0, tiled=True, axis_index_groups=chips)  3.57 us
  transfers between devices with their start and end apart: 4, of which 3 were waited for; matrix products, arithmetic and copies ran while one was open for 0% of the time, Pallas kernels for 0%

profile of v3, /device:TPU:26, one launch (start us, length us, event | category | flops | bytes accessed | tf_op | source)
XLA Modules:
  0.0 76.3 jit_solution(2068057512272529326)
XLA Ops:
  0.0 5.5 %all_gather.6 = bf16[64,1024]{1,0:T(8,128)(2,1)S(1)} all-gather(bf16[32,1024]{1,0:T(8,128)(2,1)} %bitcast.12), channel_id=1, replica_groups={{0,1},{2,3},{4,5},{6,7},{8,9},{10,11},{12,13},{14,15},{16,17},{18,19},{..., dimensions={0}, use_global_device_ids=true | all-gather | bytes 196608 | tf_op jit(solution)/shard_map/all_gather | solution.py:149
  5.5 0.0 copy-start.2
  5.6 0.7 copy-done.2
  6.3 0.0 copy-start
  6.3 4.8 %collective-permute-start = (bf16[80,1024]{1,0:T(8,128)(2,1)S(1)}, bf16[80,1024]{1,0:T(8,128)(2,1)S(1)}, u32[]{:S(2)}, u32[]{:S(2)}) collective-permute-start(bf16[80,1024]{1,0:T(8,128)(2,1)S(1)} %pad_maximum_fusion), channel_id=1, source_target_pairs={{0,64},{8,72},{16,80},{24,88},{32,96},{40,104},{48,112},{56,120},{... | collective-permute-start | bytes 491528 | tf_op jit(solution)/shard_map/ppermute | solution.py:28
  11.2 1.9 %collective-permute-start.1 = (bf16[80,1024]{1,0:T(8,128)(2,1)S(1)}, bf16[80,1024]{1,0:T(8,128)(2,1)S(1)}, u32[]{:S(2)}, u32[]{:S(2)}) collective-permute-start(bf16[80,1024]{1,0:T(8,128)(2,1)S(1)} %pad_maximum_fusion), channel_id=1, source_target_pairs={{64,0},{72,8},{80,16},{88,24},{96,32},{104,40},{112,48},{120,56},{... | collective-permute-start | bytes 491528 | tf_op jit(solution)/shard_map/ppermute | solution.py:28
  13.1 0.9 %collective-permute-done = bf16[80,1024]{1,0:T(8,128)(2,1)S(1)} collective-permute-done((bf16[80,1024]{1,0:T(8,128)(2,1)S(1)}, bf16[80,1024]{1,0:T(8,128)(2,1)S(1)}, u32[]{:S(2)}, u32[]{:S(2)}) %collective-permute-start) | collective-permute-done | bytes 163872 | tf_op jit(solution)/shard_map/ppermute | solution.py:28
  14.0 5.6 %collective-permute-done.1 = bf16[80,1024]{1,0:T(8,128)(2,1)S(1)} collective-permute-done((bf16[80,1024]{1,0:T(8,128)(2,1)S(1)}, bf16[80,1024]{1,0:T(8,128)(2,1)S(1)}, u32[]{:S(2)}, u32[]{:S(2)}) %collective-permute-start.1) | collective-permute-done | bytes 163872 | tf_op jit(solution)/shard_map/ppermute | solution.py:28
  19.6 1.9 %collective-permute-start.2 = (bf16[240,1024]{1,0:T(8,128)(2,1)S(1)}, bf16[240,1024]{1,0:T(8,128)(2,1)S(1)}, u32[]{:S(2)}, u32[]{:S(2)}) collective-permute-start(bf16[240,1024]{1,0:T(8,128)(2,1)S(1)} %constant_dynamic-update-slice_fusion), channel_id=1, source_target_pairs={{8,16},{16,8},{24,32},{32,24},{40,48},{48,40},{72,80},{80,72},{88,... | collective-permute-start | bytes 1474568 | tf_op jit(solution)/shard_map/ppermute | solution.py:156
  21.5 0.0 copy-done
  21.5 3.9 %collective-permute-start.3 = (bf16[864,256]{1,0:T(8,128)(2,1)S(1)}, bf16[864,256]{1,0:T(8,128)(2,1)S(1)}, u32[]{:S(2)}, u32[]{:S(2)}) collective-permute-start(bf16[864,256]{1,0:T(8,128)(2,1)S(1)} %bitcast.8), channel_id=1, source_target_pairs={{0,1},{1,0},{2,3},{3,2},{4,5},{5,4},{6,7},{7,6},{8,9},{9,8},{10,11... | collective-permute-start | bytes 1327112 | tf_op jit(solution)/shard_map/ppermute | solution.py:154
  25.4 0.1 pad_add_fusion.where_ref
  25.5 0.0 copy-start.1
  25.5 3.6 %all_gather.7.both_ref = bf16[480,1024]{1,0:T(8,128)(2,1)S(1)} all-gather(bf16[240,1024]{1,0:T(8,128)(2,1)S(1)} %constant_dynamic-update-slice_fusion), channel_id=1, replica_groups={{0,8},{16,24},{32,40},{48,56},{64,72},{80,88},{96,104},{112,120},{128,1..., dimensions={0}, use_global_device_ids=true | all-gather | bytes 1474560 | tf_op jit(solution)/shard_map/all_gather | solution.py:157
  29.1 6.5 %collective-permute-done.3.w1_ref = bf16[864,256]{1,0:T(8,128)(2,1)S(1)} collective-permute-done((bf16[864,256]{1,0:T(8,128)(2,1)S(1)}, bf16[864,256]{1,0:T(8,128)(2,1)S(1)}, u32[]{:S(2)}, u32[]{:S(2)}) %collective-permute-start.3) | collective-permute-done | bytes 442400 | tf_op jit(solution)/shard_map/ppermute | solution.py:154
  35.6 0.0 collective-permute-done.2.outer_ref
  35.6 0.0 copy-done.1
  35.6 12.0 %conv.1 = f32[256,512]{1,0:T(8,128)S(1)} custom-call(s32[2]{0:T(128)S(1)} %pad_add_fusion.where_ref, s32[27,1024]{1,0:T(8,128)S(1)} %copy-done.1, bf16[480,1024]{1,0:T(8,128)(2,1)S(1)} %all_gather.7.both_ref, bf16[240,1024]{1,0:T(8,128)(2,1)S(1)} %collective-permute-done.2.outer_ref, bf16[864,256]{1,0:T(8,128)(2,1)S(1)} %bitcast.9, ...), custom_call_target="tpu_custom_call" | custom-call | tf_op jit(solution)/shard_map/conv/pallas_call | solution.py:159
  47.6 28.1 %all_to_all.9.got_ref = f32[8,32,512]{2,1,0:T(8,128)S(1)} all-to-all(f32[8,32,512]{2,1,0:T(8,128)S(1)} %bitcast.7), channel_id=1, replica_groups=mesh['space'=64,'chan'=8] {'chan'}, dimensions={0} | all-to-all | bytes 1048576 | tf_op jit(solution)/shard_map/all_to_all | solution.py:177
  75.7 0.7 add.14
  (6 shorter events, 0.1 us)
Async XLA Ops:
  5.5 0.7 copy-start.2
  6.3 15.2 %copy-start = (bf16[27,32,256]{2,1,0:T(8,128)(2,1)S(1)}, bf16[27,32,256]{2,1,0:T(8,128)(2,1)}, u32[]{:S(2)}) copy-start(bf16[27,32,256]{2,1,0:T(8,128)(2,1)} %param.5) | copy-start | bytes 1327108
  6.3 7.7 %collective-permute-start = (bf16[80,1024]{1,0:T(8,128)(2,1)S(1)}, bf16[80,1024]{1,0:T(8,128)(2,1)S(1)}, u32[]{:S(2)}, u32[]{:S(2)}) collective-permute-start(bf16[80,1024]{1,0:T(8,128)(2,1)S(1)} %pad_maximum_fusion), channel_id=1, source_target_pairs={{0,64},{8,72},{16,80},{24,88},{32,96},{40,104},{48,112},{56,120},{... | collective-permute-start | bytes 491528 | tf_op jit(solution)/shard_map/ppermute | solution.py:28
  11.2 8.4 %collective-permute-start.1 = (bf16[80,1024]{1,0:T(8,128)(2,1)S(1)}, bf16[80,1024]{1,0:T(8,128)(2,1)S(1)}, u32[]{:S(2)}, u32[]{:S(2)}) collective-permute-start(bf16[80,1024]{1,0:T(8,128)(2,1)S(1)} %pad_maximum_fusion), channel_id=1, source_target_pairs={{64,0},{72,8},{80,16},{88,24},{96,32},{104,40},{112,48},{120,56},{... | collective-permute-start | bytes 491528 | tf_op jit(solution)/shard_map/ppermute | solution.py:28
  19.6 16.0 %collective-permute-start.2 = (bf16[240,1024]{1,0:T(8,128)(2,1)S(1)}, bf16[240,1024]{1,0:T(8,128)(2,1)S(1)}, u32[]{:S(2)}, u32[]{:S(2)}) collective-permute-start(bf16[240,1024]{1,0:T(8,128)(2,1)S(1)} %constant_dynamic-update-slice_fusion), channel_id=1, source_target_pairs={{8,16},{16,8},{24,32},{32,24},{40,48},{48,40},{72,80},{80,72},{88,... | collective-permute-start | bytes 1474568 | tf_op jit(solution)/shard_map/ppermute | solution.py:156
  21.5 14.1 %collective-permute-start.3 = (bf16[864,256]{1,0:T(8,128)(2,1)S(1)}, bf16[864,256]{1,0:T(8,128)(2,1)S(1)}, u32[]{:S(2)}, u32[]{:S(2)}) collective-permute-start(bf16[864,256]{1,0:T(8,128)(2,1)S(1)} %bitcast.8), channel_id=1, source_target_pairs={{0,1},{1,0},{2,3},{3,2},{4,5},{5,4},{6,7},{7,6},{8,9},{9,8},{10,11... | collective-permute-start | bytes 1327112 | tf_op jit(solution)/shard_map/ppermute | solution.py:154
  25.5 10.1 %copy-start.1 = (s32[27,1024]{1,0:T(8,128)S(1)}, s32[27,1024]{1,0:T(8,128)}, u32[]{:S(2)}) copy-start(s32[27,1024]{1,0:T(8,128)} %gm_ref.1) | copy-start | bytes 331780

commit v4 on v3

--- a/solution.py
+++ b/solution.py
@@ -85,8 +85,9 @@
 
     for place in range(OFFS):
         k = {CENTRE: OFFS - 1, OFFS - 1: CENTRE}.get(place, place)
-        for side, w_ref in ((par, w0_ref), (1 - par, w1_ref)):
-            wall[pl.ds(pl.multiple_of(64 * place + 32 * side, 32), 32), :] = w_ref[32 * k:32 * k + 32, :]
+        k1 = k if k <= CENTRE else k + 1
+        for side, w_ref, at in ((par, w0_ref, 32 * k), (1 - par, w1_ref, 32 * k1)):
+            wall[pl.ds(pl.multiple_of(64 * place + 32 * side, 32), 32), :] = w_ref[at:at + 32, :]
     wall[64 * OFFS:, :] = jnp.zeros((64, 256), jnp.bfloat16)
 
     own = pl.multiple_of(own_base * V + par * HALF, 128)
@@ -151,10 +152,13 @@
     message = jnp.concatenate([mine, (rows >> 5).astype(jnp.bfloat16), (rows & 31).astype(jnp.bfloat16)], axis=0)
     up = shift(message, 1)
     dn = shift(message, -1)
-    w1 = lax.ppermute(w0, "chan", flip)
+    part = lax.dynamic_slice_in_dim(w0, core * (CENTRE * width), (CENTRE + 1) * width, 0)
+    part = lax.ppermute(part, "chan", flip)
     strip = jnp.concatenate([message, up, dn], axis=0)
+    strip, part = lax.optimization_barrier((strip, part))
     outer = lax.ppermute(strip, "space", facing)
     both = lax.all_gather(strip, "space", axis=0, tiled=True, axis_index_groups=chips)
+    w1 = lax.all_gather(part, "space", axis=0, tiled=True, axis_index_groups=chips)
     vmem = pl.BlockSpec(memory_space=pltpu.VMEM)
     part = pl.pallas_call(
         conv_kernel,

time: 76.7 us -> 72.2 us (0.941)
  the two profiles are of different devices: /device:TPU:26 before, /device:TPU:34 now
where the time goes in v4:
time: 72.2 us; the launch traced here: 71.8 us
  blocking collectives  39.1 us (54%)
  starting transfers between devices  12.8 us (18%)
  Pallas kernels  12.6 us (17%)
  waiting for transfers between devices  6.12 us (8%)
  other arithmetic  0.9 us (1%)
    all_to_all x1, blocking collectives, local(): got = lax.all_to_all(part, 'chan', 0, 0, tiled=True).reshape(8, 32, HALF)  27.5 us
    pallas_call x1, Pallas kernels, local(): pl.pallas_call(conv_kernel, out_shape=jax.ShapeDtypeStruct((256, HALF), j...  12 us
    ppermute x2, starting transfers between devices, shift(): return lax.ppermute(value, 'space', pairs)  7.05 us
    all_gather x1, blocking collectives, local(): lax.all_gather(features.T, 'chan', axis=0, tiled=True, axis_index_groups=...  5.67 us
    ppermute x1, waiting for transfers between devices, local(): part = lax.ppermute(part, 'chan', flip)  3.96 us
    ppermute x1, starting transfers between devices, local(): part = lax.ppermute(part, 'chan', flip)  3.89 us
    all_gather x1, blocking collectives, local(): lax.all_gather(part, 'space', axis=0, tiled=True, axis_index_groups=chips)  3.34 us
    all_gather x1, blocking collectives, local(): lax.all_gather(strip, 'space', axis=0, tiled=True, axis_index_groups=chips)  2.63 us
  transfers between devices with their start and end apart: 4, of which 2 were waited for; matrix products, arithmetic and copies ran while one was open for 0% of the time, Pallas kernels for 0%

profile of v4, /device:TPU:34, one launch (start us, length us, event | category | flops | bytes accessed | tf_op | source)
XLA Modules:
  0.0 71.8 jit_solution(3539366879033644414)
XLA Ops:
  0.0 0.0 copy-start
  0.0 5.7 %all_gather.9 = bf16[64,1024]{1,0:T(8,128)(2,1)S(1)} all-gather(bf16[32,1024]{1,0:T(8,128)(2,1)} %bitcast.12), channel_id=1, replica_groups={{0,1},{2,3},{4,5},{6,7},{8,9},{10,11},{12,13},{14,15},{16,17},{18,19},{..., dimensions={0}, use_global_device_ids=true | all-gather | bytes 196608 | tf_op jit(solution)/shard_map/all_gather | solution.py:150
  5.7 0.0 copy-start.2
  5.7 0.8 %constant_dynamic-update-slice_fusion.3 = (bf16[240,1024]{1,0:T(8,128)(2,1)S(1)}, bf16[8,1024]{1,0:T(8,128)(2,1)S(1)}) fusion(bf16[240,1024]{1,0:T(8,128)(2,1)S(1)} %constant_dynamic-update-slice_fusion.4, s32[8,768]{1,0:T(8,128)} %bitcast.10), kind=kLoop, calls=%fused_computation.8 | loop fusion | flops 16384 | bytes 57344
  6.5 0.0 copy-done.2
  6.5 2.6 %collective-permute-start = (bf16[80,1024]{1,0:T(8,128)(2,1)S(1)}, bf16[80,1024]{1,0:T(8,128)(2,1)S(1)}, u32[]{:S(2)}, u32[]{:S(2)}) collective-permute-start(bf16[80,1024]{1,0:T(8,128)(2,1)S(1)} %pad_maximum_fusion), channel_id=1, source_target_pairs={{0,64},{8,72},{16,80},{24,88},{32,96},{40,104},{48,112},{56,120},{... | collective-permute-start | bytes 491528 | tf_op jit(solution)/shard_map/ppermute | solution.py:28
  9.1 4.5 %collective-permute-start.1 = (bf16[80,1024]{1,0:T(8,128)(2,1)S(1)}, bf16[80,1024]{1,0:T(8,128)(2,1)S(1)}, u32[]{:S(2)}, u32[]{:S(2)}) collective-permute-start(bf16[80,1024]{1,0:T(8,128)(2,1)S(1)} %pad_maximum_fusion), channel_id=1, source_target_pairs={{64,0},{72,8},{80,16},{88,24},{96,32},{104,40},{112,48},{120,56},{... | collective-permute-start | bytes 491528 | tf_op jit(solution)/shard_map/ppermute | solution.py:28
  13.6 0.0 copy-done
  13.7 3.9 %collective-permute-start.2 = (bf16[448,256]{1,0:T(8,128)(2,1)S(1)}, bf16[448,256]{1,0:T(8,128)(2,1)S(1)}, u32[]{:S(2)}, u32[]{:S(2)}) collective-permute-start(bf16[448,256]{1,0:T(8,128)(2,1)S(1)} %constant_dynamic-slice_fusion), channel_id=1, source_target_pairs={{0,1},{1,0},{2,3},{3,2},{4,5},{5,4},{6,7},{7,6},{8,9},{9,8},{10,11... | collective-permute-start | bytes 688136 | tf_op jit(solution)/shard_map/ppermute | solution.py:156
  17.6 0.0 collective-permute-done
  17.6 0.0 collective-permute-done.1
  17.6 4.0 %collective-permute-done.2 = bf16[448,256]{1,0:T(8,128)(2,1)S(1)} collective-permute-done((bf16[448,256]{1,0:T(8,128)(2,1)S(1)}, bf16[448,256]{1,0:T(8,128)(2,1)S(1)}, u32[]{:S(2)}, u32[]{:S(2)}) %collective-permute-start.2) | collective-permute-done | bytes 229408 | tf_op jit(solution)/shard_map/ppermute | solution.py:156
  21.6 1.9 %collective-permute-start.3 = (bf16[240,1024]{1,0:T(8,128)(2,1)S(1)}, bf16[240,1024]{1,0:T(8,128)(2,1)S(1)}, u32[]{:S(2)}, u32[]{:S(2)}) collective-permute-start(bf16[240,1024]{1,0:T(8,128)(2,1)S(1)} %constant_dynamic-update-slice_fusion), channel_id=1, source_target_pairs={{8,16},{16,8},{24,32},{32,24},{40,48},{48,40},{72,80},{80,72},{88,... | collective-permute-start | bytes 1474568 | tf_op jit(solution)/shard_map/ppermute | solution.py:159
  23.5 0.1 pad_add_fusion.where_ref
  23.6 3.3 %all_gather.11.w1_ref = bf16[896,256]{1,0:T(8,128)(2,1)S(1)} all-gather(bf16[448,256]{1,0:T(8,128)(2,1)S(1)} %collective-permute-done.2), channel_id=1, replica_groups={{0,8},{16,24},{32,40},{48,56},{64,72},{80,88},{96,104},{112,120},{128,1..., dimensions={0}, use_global_device_ids=true | all-gather | bytes 688128 | tf_op jit(solution)/shard_map/all_gather | solution.py:161
  26.9 0.0 copy-start.1
  26.9 2.6 %all_gather.10.both_ref = bf16[480,1024]{1,0:T(8,128)(2,1)S(1)} all-gather(bf16[240,1024]{1,0:T(8,128)(2,1)S(1)} %constant_dynamic-update-slice_fusion), channel_id=1, replica_groups={{0,8},{16,24},{32,40},{48,56},{64,72},{80,88},{96,104},{112,120},{128,1..., dimensions={0}, use_global_device_ids=true | all-gather | bytes 1474560 | tf_op jit(solution)/shard_map/all_gather | solution.py:160
  29.6 2.2 %collective-permute-done.3.outer_ref = bf16[240,1024]{1,0:T(8,128)(2,1)S(1)} collective-permute-done((bf16[240,1024]{1,0:T(8,128)(2,1)S(1)}, bf16[240,1024]{1,0:T(8,128)(2,1)S(1)}, u32[]{:S(2)}, u32[]{:S(2)}) %collective-permute-start.3) | collective-permute-done | bytes 491552 | tf_op jit(solution)/shard_map/ppermute | solution.py:159
  31.7 0.0 copy-done.1
  31.7 12.0 %conv.1 = f32[256,512]{1,0:T(8,128)S(1)} custom-call(s32[2]{0:T(128)S(1)} %pad_add_fusion.where_ref, s32[27,1024]{1,0:T(8,128)S(1)} %copy-done.1, bf16[480,1024]{1,0:T(8,128)(2,1)S(1)} %all_gather.10.both_ref, bf16[240,1024]{1,0:T(8,128)(2,1)S(1)} %collective-permute-done.3.outer_ref, bf16[864,256]{1,0:T(8,128)(2,1)S(1)} %bitcast.9, ...), custom_call_target="tpu_custom_call" | custom-call | tf_op jit(solution)/shard_map/conv/pallas_call | solution.py:163
  43.7 27.5 %all_to_all.9.got_ref = f32[8,32,512]{2,1,0:T(8,128)S(1)} all-to-all(f32[8,32,512]{2,1,0:T(8,128)S(1)} %bitcast.7), channel_id=1, replica_groups=mesh['space'=64,'chan'=8] {'chan'}, dimensions={0} | all-to-all | bytes 1048576 | tf_op jit(solution)/shard_map/all_to_all | solution.py:181
  71.2 0.7 add.18
  (6 shorter events, 0.1 us)
Async XLA Ops:
  0.0 13.6 %copy-start = (bf16[27,32,256]{2,1,0:T(8,128)(2,1)S(1)}, bf16[27,32,256]{2,1,0:T(8,128)(2,1)}, u32[]{:S(2)}) copy-start(bf16[27,32,256]{2,1,0:T(8,128)(2,1)} %param.5) | copy-start | bytes 1327108
  5.7 0.8 %copy-start.2 = (s32[1,8,768]{2,1,0:T(8,128)S(1)}, s32[1,8,768]{2,1,0:T(8,128)}, u32[]{:S(2)}) copy-start(s32[1,8,768]{2,1,0:T(8,128)} %param.6) | copy-start | bytes 73732
  6.5 11.0 %collective-permute-start = (bf16[80,1024]{1,0:T(8,128)(2,1)S(1)}, bf16[80,1024]{1,0:T(8,128)(2,1)S(1)}, u32[]{:S(2)}, u32[]{:S(2)}) collective-permute-start(bf16[80,1024]{1,0:T(8,128)(2,1)S(1)} %pad_maximum_fusion), channel_id=1, source_target_pairs={{0,64},{8,72},{16,80},{24,88},{32,96},{40,104},{48,112},{56,120},{... | collective-permute-start | bytes 491528 | tf_op jit(solution)/shard_map/ppermute | solution.py:28
  9.1 8.5 %collective-permute-start.1 = (bf16[80,1024]{1,0:T(8,128)(2,1)S(1)}, bf16[80,1024]{1,0:T(8,128)(2,1)S(1)}, u32[]{:S(2)}, u32[]{:S(2)}) collective-permute-start(bf16[80,1024]{1,0:T(8,128)(2,1)S(1)} %pad_maximum_fusion), channel_id=1, source_target_pairs={{64,0},{72,8},{80,16},{88,24},{96,32},{104,40},{112,48},{120,56},{... | collective-permute-start | bytes 491528 | tf_op jit(solution)/shard_map/ppermute | solution.py:28
  13.7 7.9 %collective-permute-start.2 = (bf16[448,256]{1,0:T(8,128)(2,1)S(1)}, bf16[448,256]{1,0:T(8,128)(2,1)S(1)}, u32[]{:S(2)}, u32[]{:S(2)}) collective-permute-start(bf16[448,256]{1,0:T(8,128)(2,1)S(1)} %constant_dynamic-slice_fusion), channel_id=1, source_target_pairs={{0,1},{1,0},{2,3},{3,2},{4,5},{5,4},{6,7},{7,6},{8,9},{9,8},{10,11... | collective-permute-start | bytes 688136 | tf_op jit(solution)/shard_map/ppermute | solution.py:156
  21.6 10.1 %collective-permute-start.3 = (bf16[240,1024]{1,0:T(8,128)(2,1)S(1)}, bf16[240,1024]{1,0:T(8,128)(2,1)S(1)}, u32[]{:S(2)}, u32[]{:S(2)}) collective-permute-start(bf16[240,1024]{1,0:T(8,128)(2,1)S(1)} %constant_dynamic-update-slice_fusion), channel_id=1, source_target_pairs={{8,16},{16,8},{24,32},{32,24},{40,48},{48,40},{72,80},{80,72},{88,... | collective-permute-start | bytes 1474568 | tf_op jit(solution)/shard_map/ppermute | solution.py:159
  26.9 4.8 %copy-start.1 = (s32[27,1024]{1,0:T(8,128)S(1)}, s32[27,1024]{1,0:T(8,128)}, u32[]{:S(2)}) copy-start(s32[27,1024]{1,0:T(8,128)} %gm_ref.1) | copy-start | bytes 331780

commit v5 on v4

--- a/solution.py
+++ b/solution.py
@@ -147,18 +147,19 @@
         for a, b in ((col, col + 1), (col + 1, col))
     ]
     w0 = weights.reshape(OFFS * width, 256)
+    part = lax.dynamic_slice_in_dim(w0, core * (CENTRE * width), (CENTRE + 1) * width, 0)
+    part = lax.ppermute(part, "chan", flip)
     mine = lax.all_gather(features.T, "chan", axis=0, tiled=True, axis_index_groups=duo)
     rows = jnp.pad(send_rows[0], ((0, 0), (0, V - HALO)))
     message = jnp.concatenate([mine, (rows >> 5).astype(jnp.bfloat16), (rows & 31).astype(jnp.bfloat16)], axis=0)
+    message, part = lax.optimization_barrier((message, part))
     up = shift(message, 1)
     dn = shift(message, -1)
-    part = lax.dynamic_slice_in_dim(w0, core * (CENTRE * width), (CENTRE + 1) * width, 0)
-    part = lax.ppermute(part, "chan", flip)
     strip = jnp.concatenate([message, up, dn], axis=0)
-    strip, part = lax.optimization_barrier((strip, part))
+    w1 = lax.all_gather(part, "space", axis=0, tiled=True, axis_index_groups=chips)
+    strip, w1 = lax.optimization_barrier((strip, w1))
     outer = lax.ppermute(strip, "space", facing)
     both = lax.all_gather(strip, "space", axis=0, tiled=True, axis_index_groups=chips)
-    w1 = lax.all_gather(part, "space", axis=0, tiled=True, axis_index_groups=chips)
     vmem = pl.BlockSpec(memory_space=pltpu.VMEM)
     part = pl.pallas_call(
         conv_kernel,

time: 72.2 us -> 73.5 us (1.018)
  blocking collectives: 39.1 us -> 40.2 us
  waiting for transfers between devices: 6.12 us -> 7.08 us
  local copies, waits for them, and re-layouts: 0.07 us -> 1 us
  starting transfers between devices: 12.8 us -> 12 us
  other arithmetic: 0.9 us -> 0.13 us
    ppermute x1, waiting for transfers between devices: 3.96 us -> 0.01 us  [local(): part = lax.ppermute(part, 'chan', flip)]
    ppermute x2, waiting for transfers between devices: 0.01 us -> 2.79 us  [shift(): return lax.ppermute(value, 'space', pairs)]
    ppermute x1, waiting for transfers between devices: 2.16 us -> 4.28 us  [local(): outer = lax.ppermute(strip, 'space', facing)]
    all_gather x1, blocking collectives: 5.67 us -> 6.97 us  [local(): lax.all_gather(features.T, 'chan', axis=0, tiled=True, axis_index_groups=...]
    all_gather x1, blocking collectives: 2.63 us -> 3.85 us  [local(): lax.all_gather(strip, 'space', axis=0, tiled=True, axis_index_groups=chips)]
    ppermute x2, starting transfers between devices: 7.05 us -> 5.84 us  [shift(): return lax.ppermute(value, 'space', pairs)]
    all_gather x1, blocking collectives: 3.34 us -> 2.13 us  [local(): lax.all_gather(part, 'space', axis=0, tiled=True, axis_index_groups=chips)]
    dynamic_slice x1, local copies, waits for them, and re-layouts: 0.02 us -> 0.99 us  [local(): lax.dynamic_slice_in_dim(w0, core * (CENTRE * width), (CENTRE + 1) * widt...]
where the time goes in v5:
time: 73.5 us; the launch traced here: 73.2 us
  blocking collectives  40.2 us (55%)
  Pallas kernels  12.6 us (17%)
  starting transfers between devices  12 us (16%)
  waiting for transfers between devices  7.08 us (10%)
  local copies, waits for them, and re-layouts  1 us (1%)
    all_to_all x1, blocking collectives, local(): got = lax.all_to_all(part, 'chan', 0, 0, tiled=True).reshape(8, 32, HALF)  27.2 us
    pallas_call x1, Pallas kernels, local(): pl.pallas_call(conv_kernel, out_shape=jax.ShapeDtypeStruct((256, HALF), j...  12 us
    all_gather x1, blocking collectives, local(): lax.all_gather(features.T, 'chan', axis=0, tiled=True, axis_index_groups=...  6.97 us
    ppermute x2, starting transfers between devices, shift(): return lax.ppermute(value, 'space', pairs)  5.84 us
    ppermute x1, starting transfers between devices, local(): part = lax.ppermute(part, 'chan', flip)  4.28 us
    ppermute x1, waiting for transfers between devices, local(): outer = lax.ppermute(strip, 'space', facing)  4.28 us
    all_gather x1, blocking collectives, local(): lax.all_gather(strip, 'space', axis=0, tiled=True, axis_index_groups=chips)  3.85 us
    ppermute x2, waiting for transfers between devices, shift(): return lax.ppermute(value, 'space', pairs)  2.79 us
  transfers between devices with their start and end apart: 4, of which 2 were waited for; matrix products, arithmetic and copies ran while one was open for 0% of the time, Pallas kernels for 0%

profile of v5, /device:TPU:34, one launch (start us, length us, event | category | flops | bytes accessed | tf_op | source)
XLA Modules:
  0.0 73.2 jit_solution(7618450735340061131)
XLA Ops:
  0.0 0.0 copy-start.2
  0.0 1.0 %constant_dynamic-slice_fusion = bf16[448,256]{1,0:T(8,128)(2,1)S(1)} fusion(bf16[864,256]{1,0:T(8,128)(2,1)} %bitcast.8, s32[]{:T(128)S(6)} %select_n.16), kind=kLoop, calls=%fused_computation.7 | loop fusion | bytes 458756 | tf_op jit(solution)/shard_map/dynamic_slice | solution.py:150
  1.0 4.3 %collective-permute-start = (bf16[448,256]{1,0:T(8,128)(2,1)S(1)}, bf16[448,256]{1,0:T(8,128)(2,1)S(1)}, u32[]{:S(2)}, u32[]{:S(2)}) collective-permute-start(bf16[448,256]{1,0:T(8,128)(2,1)S(1)} %constant_dynamic-slice_fusion), channel_id=1, source_target_pairs={{0,1},{1,0},{2,3},{3,2},{4,5},{5,4},{6,7},{7,6},{8,9},{9,8},{10,11... | collective-permute-start | bytes 688136 | tf_op jit(solution)/shard_map/ppermute | solution.py:151
  5.3 0.0 copy-done.2
  5.3 0.0 copy-start.3
  5.3 7.0 %all_gather.9 = bf16[64,1024]{1,0:T(8,128)(2,1)S(1)} all-gather(bf16[32,1024]{1,0:T(8,128)(2,1)S(1)} %bitcast.10), channel_id=1, replica_groups={{0,1},{2,3},{4,5},{6,7},{8,9},{10,11},{12,13},{14,15},{16,17},{18,19},{..., dimensions={0}, use_global_device_ids=true | all-gather | bytes 196608 | tf_op jit(solution)/shard_map/all_gather | solution.py:152
  12.3 0.0 copy-done.3
  12.3 0.0 collective-permute-done
  12.3 2.4 %collective-permute-start.2 = (bf16[80,1024]{1,0:T(8,128)(2,1)S(1)}, bf16[80,1024]{1,0:T(8,128)(2,1)S(1)}, u32[]{:S(2)}, u32[]{:S(2)}) collective-permute-start(bf16[80,1024]{1,0:T(8,128)(2,1)S(1)} %pad_maximum_fusion.1), channel_id=1, source_target_pairs={{64,0},{72,8},{80,16},{88,24},{96,32},{104,40},{112,48},{120,56},{... | collective-permute-start | bytes 491528 | tf_op jit(solution)/shard_map/ppermute | solution.py:28
  14.7 3.5 %collective-permute-start.1 = (bf16[80,1024]{1,0:T(8,128)(2,1)S(1)}, bf16[80,1024]{1,0:T(8,128)(2,1)S(1)}, u32[]{:S(2)}, u32[]{:S(2)}) collective-permute-start(bf16[80,1024]{1,0:T(8,128)(2,1)S(1)} %pad_maximum_fusion.1), channel_id=1, source_target_pairs={{0,64},{8,72},{16,80},{24,88},{32,96},{40,104},{48,112},{56,120},{... | collective-permute-start | bytes 491528 | tf_op jit(solution)/shard_map/ppermute | solution.py:28
  18.2 2.1 %all_gather.10.w1_ref = bf16[896,256]{1,0:T(8,128)(2,1)S(1)} all-gather(bf16[448,256]{1,0:T(8,128)(2,1)S(1)} %collective-permute-done), channel_id=1, replica_groups={{0,8},{16,24},{32,40},{48,56},{64,72},{80,88},{96,104},{112,120},{128,1..., dimensions={0}, use_global_device_ids=true | all-gather | bytes 688128 | tf_op jit(solution)/shard_map/all_gather | solution.py:159
  20.3 0.0 collective-permute-done.2
  20.3 2.8 %collective-permute-done.1 = bf16[80,1024]{1,0:T(8,128)(2,1)S(1)} collective-permute-done((bf16[80,1024]{1,0:T(8,128)(2,1)S(1)}, bf16[80,1024]{1,0:T(8,128)(2,1)S(1)}, u32[]{:S(2)}, u32[]{:S(2)}) %collective-permute-start.1) | collective-permute-done | bytes 163872 | tf_op jit(solution)/shard_map/ppermute | solution.py:28
  23.1 1.9 %collective-permute-start.3 = (bf16[240,1024]{1,0:T(8,128)(2,1)S(1)}, bf16[240,1024]{1,0:T(8,128)(2,1)S(1)}, u32[]{:S(2)}, u32[]{:S(2)}) collective-permute-start(bf16[240,1024]{1,0:T(8,128)(2,1)S(1)} %pad_maximum_fusion), channel_id=1, source_target_pairs={{8,16},{16,8},{24,32},{32,24},{40,48},{48,40},{72,80},{80,72},{88,... | collective-permute-start | bytes 1474568 | tf_op jit(solution)/shard_map/ppermute | solution.py:161
  25.1 0.1 pad_add_fusion.where_ref
  25.2 0.0 copy-start
  25.2 0.0 copy-start.1
  25.2 3.8 %all_gather.11.both_ref = bf16[480,1024]{1,0:T(8,128)(2,1)S(1)} all-gather(bf16[240,1024]{1,0:T(8,128)(2,1)S(1)} %pad_maximum_fusion), channel_id=1, replica_groups={{0,8},{16,24},{32,40},{48,56},{64,72},{80,88},{96,104},{112,120},{128,1..., dimensions={0}, use_global_device_ids=true | all-gather | bytes 1474560 | tf_op jit(solution)/shard_map/all_gather | solution.py:162
  29.0 4.3 %collective-permute-done.3.outer_ref = bf16[240,1024]{1,0:T(8,128)(2,1)S(1)} collective-permute-done((bf16[240,1024]{1,0:T(8,128)(2,1)S(1)}, bf16[240,1024]{1,0:T(8,128)(2,1)S(1)}, u32[]{:S(2)}, u32[]{:S(2)}) %collective-permute-start.3) | collective-permute-done | bytes 491552 | tf_op jit(solution)/shard_map/ppermute | solution.py:161
  33.3 0.0 copy-done
  33.3 0.0 copy-done.1
  33.3 12.0 %conv.1 = f32[256,512]{1,0:T(8,128)S(1)} custom-call(s32[2]{0:T(128)S(1)} %pad_add_fusion.where_ref, s32[27,1024]{1,0:T(8,128)S(1)} %copy-done.1, bf16[480,1024]{1,0:T(8,128)(2,1)S(1)} %all_gather.11.both_ref, bf16[240,1024]{1,0:T(8,128)(2,1)S(1)} %collective-permute-done.3.outer_ref, bf16[864,256]{1,0:T(8,128)(2,1)S(1)} %bitcast.9, ...), custom_call_target="tpu_custom_call" | custom-call | tf_op jit(solution)/shard_map/conv/pallas_call | solution.py:164
  45.3 27.2 %all_to_all.9.got_ref = f32[8,32,512]{2,1,0:T(8,128)S(1)} all-to-all(f32[8,32,512]{2,1,0:T(8,128)S(1)} %bitcast.7), channel_id=1, replica_groups=mesh['space'=64,'chan'=8] {'chan'}, dimensions={0} | all-to-all | bytes 1048576 | tf_op jit(solution)/shard_map/all_to_all | solution.py:182
  72.5 0.7 add.18
  (3 shorter events, 0.1 us)
Async XLA Ops:
  0.0 5.3 %copy-start.2 = (bf16[1024,32]{0,1:T(8,128)(2,1)S(1)}, bf16[1024,32]{0,1:T(8,128)(2,1)}, u32[]{:S(2)}) copy-start(bf16[1024,32]{0,1:T(8,128)(2,1)} %param.4) | copy-start | bytes 196612
  1.0 11.3 %collective-permute-start = (bf16[448,256]{1,0:T(8,128)(2,1)S(1)}, bf16[448,256]{1,0:T(8,128)(2,1)S(1)}, u32[]{:S(2)}, u32[]{:S(2)}) collective-permute-start(bf16[448,256]{1,0:T(8,128)(2,1)S(1)} %constant_dynamic-slice_fusion), channel_id=1, source_target_pairs={{0,1},{1,0},{2,3},{3,2},{4,5},{5,4},{6,7},{7,6},{8,9},{9,8},{10,11... | collective-permute-start | bytes 688136 | tf_op jit(solution)/shard_map/ppermute | solution.py:151
  5.3 7.0 %copy-start.3 = (s32[1,8,768]{2,1,0:T(8,128)S(1)}, s32[1,8,768]{2,1,0:T(8,128)}, u32[]{:S(2)}) copy-start(s32[1,8,768]{2,1,0:T(8,128)} %param.6) | copy-start | bytes 73732
  12.3 8.0 %collective-permute-start.2 = (bf16[80,1024]{1,0:T(8,128)(2,1)S(1)}, bf16[80,1024]{1,0:T(8,128)(2,1)S(1)}, u32[]{:S(2)}, u32[]{:S(2)}) collective-permute-start(bf16[80,1024]{1,0:T(8,128)(2,1)S(1)} %pad_maximum_fusion.1), channel_id=1, source_target_pairs={{64,0},{72,8},{80,16},{88,24},{96,32},{104,40},{112,48},{120,56},{... | collective-permute-start | bytes 491528 | tf_op jit(solution)/shard_map/ppermute | solution.py:28
  14.7 8.4 %collective-permute-start.1 = (bf16[80,1024]{1,0:T(8,128)(2,1)S(1)}, bf16[80,1024]{1,0:T(8,128)(2,1)S(1)}, u32[]{:S(2)}, u32[]{:S(2)}) collective-permute-start(bf16[80,1024]{1,0:T(8,128)(2,1)S(1)} %pad_maximum_fusion.1), channel_id=1, source_target_pairs={{0,64},{8,72},{16,80},{24,88},{32,96},{40,104},{48,112},{56,120},{... | collective-permute-start | bytes 491528 | tf_op jit(solution)/shard_map/ppermute | solution.py:28
  23.1 10.1 %collective-permute-start.3 = (bf16[240,1024]{1,0:T(8,128)(2,1)S(1)}, bf16[240,1024]{1,0:T(8,128)(2,1)S(1)}, u32[]{:S(2)}, u32[]{:S(2)}) collective-permute-start(bf16[240,1024]{1,0:T(8,128)(2,1)S(1)} %pad_maximum_fusion), channel_id=1, source_target_pairs={{8,16},{16,8},{24,32},{32,24},{40,48},{48,40},{72,80},{80,72},{88,... | collective-permute-start | bytes 1474568 | tf_op jit(solution)/shard_map/ppermute | solution.py:161
  25.2 8.1 %copy-start = (bf16[27,32,256]{2,1,0:T(8,128)(2,1)S(1)}, bf16[27,32,256]{2,1,0:T(8,128)(2,1)}, u32[]{:S(2)}) copy-start(bf16[27,32,256]{2,1,0:T(8,128)(2,1)} %param.5) | copy-start | bytes 1327108
  25.2 8.1 %copy-start.1 = (s32[27,1024]{1,0:T(8,128)S(1)}, s32[27,1024]{1,0:T(8,128)}, u32[]{:S(2)}) copy-start(s32[27,1024]{1,0:T(8,128)} %gm_ref.1) | copy-start | bytes 331780

commit v6 on v3

--- a/solution.py
+++ b/solution.py
@@ -12,41 +12,37 @@
 OFFS = 27
 CENTRE = 13
 PAIRS = 14
-MSG = 80
+MSG = 72
 ZERO = 9 * V
 ROWS = ZERO + 8
+FIRST = (3, 5, 0)
 STEPS = ((-1, -1), (-1, 0), (-1, 1), (0, -1), (0, 1), (1, -1), (1, 0), (1, 1))
 
 
-def shift(value, step_row):
+def shift(value, step_row, step_col):
     pairs = [
-        (row * GRID + col, (row + step_row) * GRID + col)
+        (row * GRID + col, (row + step_row) * GRID + col + step_col)
         for row in range(GRID)
         for col in range(GRID)
-        if 0 <= row + step_row < GRID
+        if 0 <= row + step_row < GRID and 0 <= col + step_col < GRID
     ]
     return lax.ppermute(value, "space", pairs)
 
 
-def conv_kernel(where_ref, gm_ref, both_ref, outer_ref, w0_ref, w1_ref,
+def conv_kernel(par_ref, gm_ref, own_ref, up_ref, dn_ref, left_ref, right_ref, w0_ref, w1_ref,
                 out_ref, table, digit, lut, comp, index, lhs, wall, sem):
-    par = where_ref[0]
-    core = where_ref[1]
-    sources = [both_ref.at[pl.ds(MSG * i, MSG)] for i in range(6)]
-    sources += [outer_ref.at[pl.ds(MSG * i, MSG)] for i in range(3)]
-    own_base = 3 * core
+    par = par_ref[0]
+    sources = [own_ref, up_ref, dn_ref]
+    sources += [ref.at[pl.ds(MSG * i, MSG)] for ref in (left_ref, right_ref) for i in range(3)]
 
     for block, source in enumerate(sources):
-        digit[16 * block:16 * block + 16, :] = source[64:80, :HALO].astype(jnp.float32)
-    base_of = {
-        0: own_base,
-        1: jnp.where(core == 0, 6, 0),
-        -1: jnp.where(core == 0, 3, 6),
-    }
+        digit[8 * block:8 * block + 8, :] = source[64:72, :HALO].astype(jnp.float32)
     for number, (step_row, step_col) in enumerate(STEPS):
-        block = base_of[step_col] + (0, 1, 2)[step_row]
-        high = digit[pl.ds(16 * block + number, 1), :]
-        low = digit[pl.ds(16 * block + 8 + number, 1), :]
+        sent = (0, 1, 2)[step_row]
+        block = 3 * (0, 1, 2)[step_col] + sent
+        at = 8 * block + number - FIRST[sent]
+        high = digit[at:at + 1, :]
+        low = digit[at + 3:at + 4, :]
         slot = (high * 32.0 + low).astype(jnp.int32)
         slot = jnp.where(slot >= V, ZERO, slot + block * V)
         for j in range(HALO // 128):
@@ -61,7 +57,7 @@
             slot = here - V
             hi = lax.shift_right_arithmetic(slot, 7)
             lo = slot & 127
-            got = jnp.where(slot < 0, here + own_base * V, ZERO)
+            got = jnp.where(slot < 0, here, ZERO)
             for t in range(8 * HALO // 128):
                 line = jnp.broadcast_to(lut[t:t + 1, :], (8, 128))
                 value = jnp.take_along_axis(line, lo, axis=1)
@@ -89,7 +85,7 @@
             wall[pl.ds(pl.multiple_of(64 * place + 32 * side, 32), 32), :] = w_ref[32 * k:32 * k + 32, :]
     wall[64 * OFFS:, :] = jnp.zeros((64, 256), jnp.bfloat16)
 
-    own = pl.multiple_of(own_base * V + par * HALF, 128)
+    own = pl.multiple_of(par * HALF, 128)
     lhs[:, 128 * (PAIRS - 1):] = table[pl.ds(own, HALF), :].astype(jnp.bfloat16)
 
     sub = lax.broadcasted_iota(jnp.int32, (8, 128), 0)
@@ -135,35 +131,33 @@
 def local(features, weights, send_rows, gather_map):
     width = features.shape[1]
     par = lax.axis_index("chan") % 2
-    core = lax.axis_index("space") % 2
     flip = [(i, i ^ 1) for i in range(8)]
     duo = [[2 * i, 2 * i + 1] for i in range(4)]
-    chips = [[2 * i, 2 * i + 1] for i in range(GRID * GRID // 2)]
-    facing = [
-        (row * GRID + a, row * GRID + b)
-        for row in range(GRID)
-        for col in range(1, GRID - 1, 2)
-        for a, b in ((col, col + 1), (col + 1, col))
-    ]
     w0 = weights.reshape(OFFS * width, 256)
     mine = lax.all_gather(features.T, "chan", axis=0, tiled=True, axis_index_groups=duo)
     rows = jnp.pad(send_rows[0], ((0, 0), (0, V - HALO)))
-    message = jnp.concatenate([mine, (rows >> 5).astype(jnp.bfloat16), (rows & 31).astype(jnp.bfloat16)], axis=0)
-    up = shift(message, 1)
-    dn = shift(message, -1)
+    high, low = (rows >> 5).astype(jnp.bfloat16), (rows & 31).astype(jnp.bfloat16)
+    blank = jnp.zeros((2, V), jnp.bfloat16)
+
+    def message(first):
+        return jnp.concatenate([mine, high[first:first + 3], low[first:first + 3], blank], axis=0)
+
+    own = message(FIRST[0])
+    up = shift(message(FIRST[1]), 1, 0)
+    dn = shift(message(FIRST[2]), -1, 0)
     w1 = lax.ppermute(w0, "chan", flip)
-    strip = jnp.concatenate([message, up, dn], axis=0)
-    outer = lax.ppermute(strip, "space", facing)
-    both = lax.all_gather(strip, "space", axis=0, tiled=True, axis_index_groups=chips)
+    strip = jnp.concatenate([own, up, dn], axis=0)
+    left = shift(strip, 0, 1)
+    right = shift(strip, 0, -1)
     vmem = pl.BlockSpec(memory_space=pltpu.VMEM)
     part = pl.pallas_call(
         conv_kernel,
         out_shape=jax.ShapeDtypeStruct((256, HALF), jnp.float32),
-        in_specs=[pl.BlockSpec(memory_space=pltpu.SMEM)] + [vmem] * 5,
+        in_specs=[pl.BlockSpec(memory_space=pltpu.SMEM)] + [vmem] * 8,
         out_specs=vmem,
         scratch_shapes=[
             pltpu.VMEM((ROWS, 128), jnp.float32),
-            pltpu.VMEM((144, HALO), jnp.float32),
+            pltpu.VMEM((72, HALO), jnp.float32),
             pltpu.VMEM((48, 128), jnp.int32),
             pltpu.VMEM((128, 128), jnp.int32),
             pltpu.SMEM((128, 128), jnp.int32),
@@ -173,7 +167,7 @@
         ],
         compiler_params=pltpu.CompilerParams(vmem_limit_bytes=40 * 2**20),
         name="conv",
-    )(jnp.stack([par, core]).astype(jnp.int32), gather_map, both, outer, w0, w1)
+    )(par.reshape(1).astype(jnp.int32), gather_map, own, up, dn, left, right, w0, w1)
     got = lax.all_to_all(part, "chan", 0, 0, tiled=True).reshape(8, 32, HALF)
     return pl.pallas_call(
         add_kernel,

time: 76.7 us -> 67.9 us (0.89)
  waiting for transfers between devices: 13 us -> 7.2 us
  blocking collectives: 37.2 us -> 31.7 us
  starting transfers between devices: 12.6 us -> 15.4 us
    ppermute x2 -> x4, starting transfers between devices: 6.75 us -> 11.4 us  [shift(): return lax.ppermute(value, 'space', pairs)]
    all_gather x1 -> x0, blocking collectives: 3.57 us -> none  [local(): lax.all_gather(strip, 'space', axis=0, tiled=True, axis_index_groups=chips)]
    ppermute x2 -> x4, waiting for transfers between devices: 6.48 us -> 3.31 us  [shift(): return lax.ppermute(value, 'space', pairs)]
    ppermute x1, waiting for transfers between devices: 6.53 us -> 3.89 us  [local(): w1 = lax.ppermute(w0, 'chan', flip)]
    all_to_all x1, blocking collectives: 28.1 us -> 26 us  [local(): got = lax.all_to_all(part, 'chan', 0, 0, tiled=True).reshape(8, 32, HALF)]
    ppermute x1 -> x0, starting transfers between devices: 1.92 us -> none  [local(): outer = lax.ppermute(strip, 'space', facing)]
  transfers between devices with their start and end apart: 4 -> 5, of which waited for: 3 -> 2; matrix products, arithmetic and copies ran while one was open for 0% -> 0% of each run, Pallas kernels for 0% -> 0%
where the time goes in v6:
time: 67.9 us; the launch traced here: 67.6 us
  blocking collectives  31.7 us (47%)
  starting transfers between devices  15.4 us (23%)
  Pallas kernels  12.2 us (18%)
  waiting for transfers between devices  7.2 us (11%)
  other arithmetic  0.8 us (1%)
    all_to_all x1, blocking collectives, local(): got = lax.all_to_all(part, 'chan', 0, 0, tiled=True).reshape(8, 32, HALF)  26 us
    pallas_call x1, Pallas kernels, local(): pl.pallas_call(conv_kernel, out_shape=jax.ShapeDtypeStruct((256, HALF), j...  11.5 us
    ppermute x4, starting transfers between devices, shift(): return lax.ppermute(value, 'space', pairs)  11.4 us
    all_gather x1, blocking collectives, local(): lax.all_gather(features.T, 'chan', axis=0, tiled=True, axis_index_groups=...  5.67 us
    ppermute x1, starting transfers between devices, local(): w1 = lax.ppermute(w0, 'chan', flip)  4.02 us
    ppermute x1, waiting for transfers between devices, local(): w1 = lax.ppermute(w0, 'chan', flip)  3.89 us
    ppermute x4, waiting for transfers between devices, shift(): return lax.ppermute(value, 'space', pairs)  3.31 us
  transfers between devices with their start and end apart: 5, of which 2 were waited for; matrix products, arithmetic and copies ran while one was open for 0% of the time, Pallas kernels for 0%

profile of v6, /device:TPU:26, one launch (start us, length us, event | category | flops | bytes accessed | tf_op | source)
XLA Modules:
  0.0 67.6 jit_solution(7988032674499252221)
XLA Ops:
  0.0 0.7 %fusion = (bf16[8,1024]{1,0:T(8,128)(2,1)S(1)}, bf16[8,1024]{1,0:T(8,128)(2,1)S(1)}) fusion(s32[8,768]{1,0:T(8,128)} %bitcast.10), kind=kLoop, calls=%fused_computation.5 | loop fusion | flops 32768 | bytes 57344 | tf_op jit(solution)/shard_map/convert_element_type | solution.py:139
  0.7 0.0 copy-start
  0.7 5.7 %all_gather.3 = bf16[64,1024]{1,0:T(8,128)(2,1)S(1)} all-gather(bf16[32,1024]{1,0:T(8,128)(2,1)} %bitcast.9), channel_id=1, replica_groups={{0,1},{2,3},{4,5},{6,7},{8,9},{10,11},{12,13},{14,15},{16,17},{18,19},{..., dimensions={0}, use_global_device_ids=true | all-gather | bytes 196608 | tf_op jit(solution)/shard_map/all_gather | solution.py:137
  6.5 0.1 pad_maximum_fusion
  6.5 2.4 %collective-permute-start.1 = (bf16[72,1024]{1,0:T(8,128)(2,1)S(1)}, bf16[72,1024]{1,0:T(8,128)(2,1)S(1)}, u32[]{:S(2)}, u32[]{:S(2)}) collective-permute-start(bf16[72,1024]{1,0:T(8,128)(2,1)S(1)} %get-tuple-element.5), channel_id=1, source_target_pairs={{64,0},{72,8},{80,16},{88,24},{96,32},{104,40},{112,48},{120,56},{... | collective-permute-start | bytes 442376 | tf_op jit(solution)/shard_map/ppermute | solution.py:29
  8.9 4.7 %collective-permute-start = (bf16[72,1024]{1,0:T(8,128)(2,1)S(1)}, bf16[72,1024]{1,0:T(8,128)(2,1)S(1)}, u32[]{:S(2)}, u32[]{:S(2)}) collective-permute-start(bf16[72,1024]{1,0:T(8,128)(2,1)S(1)} %get-tuple-element.6), channel_id=1, source_target_pairs={{0,64},{8,72},{16,80},{24,88},{32,96},{40,104},{48,112},{56,120},{... | collective-permute-start | bytes 442376 | tf_op jit(solution)/shard_map/ppermute | solution.py:29
  13.6 0.0 copy-done
  13.6 0.0 copy-start.1
  13.6 4.0 %collective-permute-start.4 = (bf16[864,256]{1,0:T(8,128)(2,1)S(1)}, bf16[864,256]{1,0:T(8,128)(2,1)S(1)}, u32[]{:S(2)}, u32[]{:S(2)}) collective-permute-start(bf16[864,256]{1,0:T(8,128)(2,1)S(1)} %bitcast.7), channel_id=1, source_target_pairs={{0,1},{1,0},{2,3},{3,2},{4,5},{5,4},{6,7},{7,6},{8,9},{9,8},{10,11... | collective-permute-start | bytes 1327112 | tf_op jit(solution)/shard_map/ppermute | solution.py:148
  17.6 0.0 collective-permute-done.1.dn_ref
  17.6 0.0 collective-permute-done.up_ref
  17.7 0.2 concatenate.16
  17.9 1.9 %collective-permute-start.3 = (bf16[216,1024]{1,0:T(8,128)(2,1)S(1)}, bf16[216,1024]{1,0:T(8,128)(2,1)S(1)}, u32[]{:S(2)}, u32[]{:S(2)}) collective-permute-start(bf16[216,1024]{1,0:T(8,128)(2,1)S(1)} %concatenate.16), channel_id=1, source_target_pairs={{8,0},{16,8},{24,16},{32,24},{40,32},{48,40},{56,48},{72,64},{80,7... | collective-permute-start | bytes 1327112 | tf_op jit(solution)/shard_map/ppermute | solution.py:29
  19.8 2.4 %collective-permute-start.2 = (bf16[216,1024]{1,0:T(8,128)(2,1)S(1)}, bf16[216,1024]{1,0:T(8,128)(2,1)S(1)}, u32[]{:S(2)}, u32[]{:S(2)}) collective-permute-start(bf16[216,1024]{1,0:T(8,128)(2,1)S(1)} %concatenate.16), channel_id=1, source_target_pairs={{0,8},{8,16},{16,24},{24,32},{32,40},{40,48},{48,56},{64,72},{72,8... | collective-permute-start | bytes 1327112 | tf_op jit(solution)/shard_map/ppermute | solution.py:29
  22.2 3.9 %collective-permute-done.4.w1_ref = bf16[864,256]{1,0:T(8,128)(2,1)S(1)} collective-permute-done((bf16[864,256]{1,0:T(8,128)(2,1)S(1)}, bf16[864,256]{1,0:T(8,128)(2,1)S(1)}, u32[]{:S(2)}, u32[]{:S(2)}) %collective-permute-start.4) | collective-permute-done | bytes 442400 | tf_op jit(solution)/shard_map/ppermute | solution.py:148
  26.1 0.0 collective-permute-done.3.right_ref
  26.1 3.3 %collective-permute-done.2.left_ref = bf16[216,1024]{1,0:T(8,128)(2,1)S(1)} collective-permute-done((bf16[216,1024]{1,0:T(8,128)(2,1)S(1)}, bf16[216,1024]{1,0:T(8,128)(2,1)S(1)}, u32[]{:S(2)}, u32[]{:S(2)}) %collective-permute-start.2) | collective-permute-done | bytes 442400 | tf_op jit(solution)/shard_map/ppermute | solution.py:29
  29.4 0.0 copy-done.1
  29.4 11.5 %conv.1 = f32[256,512]{1,0:T(8,128)S(1)} custom-call(s32[1]{0:T(128)} %bitcast.par_ref, s32[27,1024]{1,0:T(8,128)S(1)} %copy-done.1, bf16[72,1024]{1,0:T(8,128)(2,1)S(1)} %get-tuple-element.7.own_ref, bf16[72,1024]{1,0:T(8,128)(2,1)S(1)} %collective-permute-done.up_ref, bf16[72,1024]{1,0:T(8,128)(2,1)S(1)} %collective-permute-done.1.dn_ref, ...), custom_call_target="tpu_custom_call" | custom-call | tf_op jit(solution)/shard_map/conv/pallas_call | solution.py:153
  40.9 26.0 %all_to_all.9.got_ref = f32[8,32,512]{2,1,0:T(8,128)S(1)} all-to-all(f32[8,32,512]{2,1,0:T(8,128)S(1)} %bitcast.6), channel_id=1, replica_groups=mesh['space'=64,'chan'=8] {'chan'}, dimensions={0} | all-to-all | bytes 1048576 | tf_op jit(solution)/shard_map/all_to_all | solution.py:171
  66.9 0.7 add.8
  (2 shorter events, 0.0 us)
Async XLA Ops:
  0.7 12.8 %copy-start = (bf16[27,32,256]{2,1,0:T(8,128)(2,1)S(1)}, bf16[27,32,256]{2,1,0:T(8,128)(2,1)}, u32[]{:S(2)}) copy-start(bf16[27,32,256]{2,1,0:T(8,128)(2,1)} %param.5) | copy-start | bytes 1327108
  6.5 11.1 %collective-permute-start.1 = (bf16[72,1024]{1,0:T(8,128)(2,1)S(1)}, bf16[72,1024]{1,0:T(8,128)(2,1)S(1)}, u32[]{:S(2)}, u32[]{:S(2)}) collective-permute-start(bf16[72,1024]{1,0:T(8,128)(2,1)S(1)} %get-tuple-element.5), channel_id=1, source_target_pairs={{64,0},{72,8},{80,16},{88,24},{96,32},{104,40},{112,48},{120,56},{... | collective-permute-start | bytes 442376 | tf_op jit(solution)/shard_map/ppermute | solution.py:29
  8.9 8.8 %collective-permute-start = (bf16[72,1024]{1,0:T(8,128)(2,1)S(1)}, bf16[72,1024]{1,0:T(8,128)(2,1)S(1)}, u32[]{:S(2)}, u32[]{:S(2)}) collective-permute-start(bf16[72,1024]{1,0:T(8,128)(2,1)S(1)} %get-tuple-element.6), channel_id=1, source_target_pairs={{0,64},{8,72},{16,80},{24,88},{32,96},{40,104},{48,112},{56,120},{... | collective-permute-start | bytes 442376 | tf_op jit(solution)/shard_map/ppermute | solution.py:29
  13.6 15.8 %copy-start.1 = (s32[27,1024]{1,0:T(8,128)S(1)}, s32[27,1024]{1,0:T(8,128)}, u32[]{:S(2)}) copy-start(s32[27,1024]{1,0:T(8,128)} %gm_ref.1) | copy-start | bytes 331780
  13.6 12.5 %collective-permute-start.4 = (bf16[864,256]{1,0:T(8,128)(2,1)S(1)}, bf16[864,256]{1,0:T(8,128)(2,1)S(1)}, u32[]{:S(2)}, u32[]{:S(2)}) collective-permute-start(bf16[864,256]{1,0:T(8,128)(2,1)S(1)} %bitcast.7), channel_id=1, source_target_pairs={{0,1},{1,0},{2,3},{3,2},{4,5},{5,4},{6,7},{7,6},{8,9},{9,8},{10,11... | collective-permute-start | bytes 1327112 | tf_op jit(solution)/shard_map/ppermute | solution.py:148
  17.9 8.2 %collective-permute-start.3 = (bf16[216,1024]{1,0:T(8,128)(2,1)S(1)}, bf16[216,1024]{1,0:T(8,128)(2,1)S(1)}, u32[]{:S(2)}, u32[]{:S(2)}) collective-permute-start(bf16[216,1024]{1,0:T(8,128)(2,1)S(1)} %concatenate.16), channel_id=1, source_target_pairs={{8,0},{16,8},{24,16},{32,24},{40,32},{48,40},{56,48},{72,64},{80,7... | collective-permute-start | bytes 1327112 | tf_op jit(solution)/shard_map/ppermute | solution.py:29
  19.8 9.6 %collective-permute-start.2 = (bf16[216,1024]{1,0:T(8,128)(2,1)S(1)}, bf16[216,1024]{1,0:T(8,128)(2,1)S(1)}, u32[]{:S(2)}, u32[]{:S(2)}) collective-permute-start(bf16[216,1024]{1,0:T(8,128)(2,1)S(1)} %concatenate.16), channel_id=1, source_target_pairs={{0,8},{8,16},{16,24},{24,32},{32,40},{40,48},{48,56},{64,72},{72,8... | collective-permute-start | bytes 1327112 | tf_op jit(solution)/shard_map/ppermute | solution.py:29

commit v7 on v6

--- a/solution.py
+++ b/solution.py
@@ -29,20 +29,23 @@
     return lax.ppermute(value, "space", pairs)
 
 
-def conv_kernel(par_ref, gm_ref, own_ref, up_ref, dn_ref, left_ref, right_ref, w0_ref, w1_ref,
+def conv_kernel(where_ref, gm_ref, both_ref, outer_ref, w0_ref, w1_ref,
                 out_ref, table, digit, lut, comp, index, lhs, wall, sem):
-    par = par_ref[0]
-    sources = [own_ref, up_ref, dn_ref]
-    sources += [ref.at[pl.ds(MSG * i, MSG)] for ref in (left_ref, right_ref) for i in range(3)]
+    par = where_ref[0]
+    core = where_ref[1]
+    sources = [both_ref.at[pl.ds(MSG * i, MSG)] for i in range(6)]
+    sources += [outer_ref.at[pl.ds(MSG * i, MSG)] for i in range(3)]
+    own_base = 3 * core
+    base_of = (own_base, jnp.where(core == 0, 6, 0), jnp.where(core == 0, 3, 6))
 
     for block, source in enumerate(sources):
         digit[8 * block:8 * block + 8, :] = source[64:72, :HALO].astype(jnp.float32)
     for number, (step_row, step_col) in enumerate(STEPS):
         sent = (0, 1, 2)[step_row]
-        block = 3 * (0, 1, 2)[step_col] + sent
+        block = base_of[step_col] + sent
         at = 8 * block + number - FIRST[sent]
-        high = digit[at:at + 1, :]
-        low = digit[at + 3:at + 4, :]
+        high = digit[pl.ds(at, 1), :]
+        low = digit[pl.ds(at + 3, 1), :]
         slot = (high * 32.0 + low).astype(jnp.int32)
         slot = jnp.where(slot >= V, ZERO, slot + block * V)
         for j in range(HALO // 128):
@@ -57,7 +60,7 @@
             slot = here - V
             hi = lax.shift_right_arithmetic(slot, 7)
             lo = slot & 127
-            got = jnp.where(slot < 0, here, ZERO)
+            got = jnp.where(slot < 0, here + own_base * V, ZERO)
             for t in range(8 * HALO // 128):
                 line = jnp.broadcast_to(lut[t:t + 1, :], (8, 128))
                 value = jnp.take_along_axis(line, lo, axis=1)
@@ -85,7 +88,7 @@
             wall[pl.ds(pl.multiple_of(64 * place + 32 * side, 32), 32), :] = w_ref[32 * k:32 * k + 32, :]
     wall[64 * OFFS:, :] = jnp.zeros((64, 256), jnp.bfloat16)
 
-    own = pl.multiple_of(par * HALF, 128)
+    own = pl.multiple_of(own_base * V + par * HALF, 128)
     lhs[:, 128 * (PAIRS - 1):] = table[pl.ds(own, HALF), :].astype(jnp.bfloat16)
 
     sub = lax.broadcasted_iota(jnp.int32, (8, 128), 0)
@@ -131,8 +134,16 @@
 def local(features, weights, send_rows, gather_map):
     width = features.shape[1]
     par = lax.axis_index("chan") % 2
+    core = lax.axis_index("space") % 2
     flip = [(i, i ^ 1) for i in range(8)]
     duo = [[2 * i, 2 * i + 1] for i in range(4)]
+    chips = [[2 * i, 2 * i + 1] for i in range(GRID * GRID // 2)]
+    facing = [
+        (row * GRID + a, row * GRID + b)
+        for row in range(GRID)
+        for col in range(1, GRID - 1, 2)
+        for a, b in ((col, col + 1), (col + 1, col))
+    ]
     w0 = weights.reshape(OFFS * width, 256)
     mine = lax.all_gather(features.T, "chan", axis=0, tiled=True, axis_index_groups=duo)
     rows = jnp.pad(send_rows[0], ((0, 0), (0, V - HALO)))
@@ -147,13 +158,13 @@
     dn = shift(message(FIRST[2]), -1, 0)
     w1 = lax.ppermute(w0, "chan", flip)
     strip = jnp.concatenate([own, up, dn], axis=0)
-    left = shift(strip, 0, 1)
-    right = shift(strip, 0, -1)
+    outer = lax.ppermute(strip, "space", facing)
+    both = lax.all_gather(strip, "space", axis=0, tiled=True, axis_index_groups=chips)
     vmem = pl.BlockSpec(memory_space=pltpu.VMEM)
     part = pl.pallas_call(
         conv_kernel,
         out_shape=jax.ShapeDtypeStruct((256, HALF), jnp.float32),
-        in_specs=[pl.BlockSpec(memory_space=pltpu.SMEM)] + [vmem] * 8,
+        in_specs=[pl.BlockSpec(memory_space=pltpu.SMEM)] + [vmem] * 5,
         out_specs=vmem,
         scratch_shapes=[
             pltpu.VMEM((ROWS, 128), jnp.float32),
@@ -167,7 +178,7 @@
         ],
         compiler_params=pltpu.CompilerParams(vmem_limit_bytes=40 * 2**20),
         name="conv",
-    )(par.reshape(1).astype(jnp.int32), gather_map, own, up, dn, left, right, w0, w1)
+    )(jnp.stack([par, core]).astype(jnp.int32), gather_map, both, outer, w0, w1)
     got = lax.all_to_all(part, "chan", 0, 0, tiled=True).reshape(8, 32, HALF)
     return pl.pallas_call(
         add_kernel,

time: 67.9 us -> 67.2 us (0.990)
  the two profiles are of different devices: /device:TPU:26 before, /device:TPU:34 now
where the time goes in v7:
time: 67.2 us; the launch traced here: 67 us
  blocking collectives  36.8 us (55%)
  Pallas kernels  12.6 us (19%)
  starting transfers between devices  11.7 us (17%)
  waiting for transfers between devices  4.66 us (7%)
  other arithmetic  0.91 us (1%)
    all_to_all x1, blocking collectives, local(): got = lax.all_to_all(part, 'chan', 0, 0, tiled=True).reshape(8, 32, HALF)  27.5 us
    pallas_call x1, Pallas kernels, local(): pl.pallas_call(conv_kernel, out_shape=jax.ShapeDtypeStruct((256, HALF), j...  11.9 us
    ppermute x2, starting transfers between devices, shift(): return lax.ppermute(value, 'space', pairs)  5.84 us
    all_gather x1, blocking collectives, local(): lax.all_gather(features.T, 'chan', axis=0, tiled=True, axis_index_groups=...  5.53 us
    ppermute x1, starting transfers between devices, local(): w1 = lax.ppermute(w0, 'chan', flip)  3.89 us
    all_gather x1, blocking collectives, local(): lax.all_gather(strip, 'space', axis=0, tiled=True, axis_index_groups=chips)  3.78 us
    ppermute x1, waiting for transfers between devices, local(): outer = lax.ppermute(strip, 'space', facing)  2.2 us
    ppermute x1, starting transfers between devices, local(): outer = lax.ppermute(strip, 'space', facing)  1.92 us
  transfers between devices with their start and end apart: 4, of which 3 were waited for; matrix products, arithmetic and copies ran while one was open for 0% of the time, Pallas kernels for 0%

profile of v7, /device:TPU:34, one launch (start us, length us, event | category | flops | bytes accessed | tf_op | source)
XLA Modules:
  0.0 67.0 jit_solution(3665305739113507310)
XLA Ops:
  0.0 0.0 copy-start
  0.0 0.8 %fusion.1 = (bf16[8,1024]{1,0:T(8,128)(2,1)S(1)}, bf16[8,1024]{1,0:T(8,128)(2,1)S(1)}) fusion(s32[8,768]{1,0:T(8,128)} %bitcast.11), kind=kLoop, calls=%fused_computation.5 | loop fusion | flops 32768 | bytes 57344 | tf_op jit(solution)/shard_map/convert_element_type | solution.py:150
  0.8 5.5 %all_gather.6 = bf16[64,1024]{1,0:T(8,128)(2,1)S(1)} all-gather(bf16[32,1024]{1,0:T(8,128)(2,1)} %bitcast.10), channel_id=1, replica_groups={{0,1},{2,3},{4,5},{6,7},{8,9},{10,11},{12,13},{14,15},{16,17},{18,19},{..., dimensions={0}, use_global_device_ids=true | all-gather | bytes 196608 | tf_op jit(solution)/shard_map/all_gather | solution.py:148
  6.4 2.4 %collective-permute-start.1 = (bf16[72,1024]{1,0:T(8,128)(2,1)S(1)}, bf16[72,1024]{1,0:T(8,128)(2,1)S(1)}, u32[]{:S(2)}, u32[]{:S(2)}) collective-permute-start(bf16[72,1024]{1,0:T(8,128)(2,1)S(1)} %get-tuple-element.5), channel_id=1, source_target_pairs={{64,0},{72,8},{80,16},{88,24},{96,32},{104,40},{112,48},{120,56},{... | collective-permute-start | bytes 442376 | tf_op jit(solution)/shard_map/ppermute | solution.py:29
  8.8 3.5 %collective-permute-start = (bf16[72,1024]{1,0:T(8,128)(2,1)S(1)}, bf16[72,1024]{1,0:T(8,128)(2,1)S(1)}, u32[]{:S(2)}, u32[]{:S(2)}) collective-permute-start(bf16[72,1024]{1,0:T(8,128)(2,1)S(1)} %get-tuple-element.6), channel_id=1, source_target_pairs={{0,64},{8,72},{16,80},{24,88},{32,96},{40,104},{48,112},{56,120},{... | collective-permute-start | bytes 442376 | tf_op jit(solution)/shard_map/ppermute | solution.py:29
  12.3 0.0 copy-done
  12.3 3.9 %collective-permute-start.3 = (bf16[864,256]{1,0:T(8,128)(2,1)S(1)}, bf16[864,256]{1,0:T(8,128)(2,1)S(1)}, u32[]{:S(2)}, u32[]{:S(2)}) collective-permute-start(bf16[864,256]{1,0:T(8,128)(2,1)S(1)} %bitcast.8), channel_id=1, source_target_pairs={{0,1},{1,0},{2,3},{3,2},{4,5},{5,4},{6,7},{7,6},{8,9},{9,8},{10,11... | collective-permute-start | bytes 1327112 | tf_op jit(solution)/shard_map/ppermute | solution.py:159
  16.2 0.0 collective-permute-done.1
  16.2 0.8 %collective-permute-done = bf16[72,1024]{1,0:T(8,128)(2,1)S(1)} collective-permute-done((bf16[72,1024]{1,0:T(8,128)(2,1)S(1)}, bf16[72,1024]{1,0:T(8,128)(2,1)S(1)}, u32[]{:S(2)}, u32[]{:S(2)}) %collective-permute-start) | collective-permute-done | bytes 147488 | tf_op jit(solution)/shard_map/ppermute | solution.py:29
  17.0 0.2 concatenate.11
  17.2 1.9 %collective-permute-start.2 = (bf16[216,1024]{1,0:T(8,128)(2,1)S(1)}, bf16[216,1024]{1,0:T(8,128)(2,1)S(1)}, u32[]{:S(2)}, u32[]{:S(2)}) collective-permute-start(bf16[216,1024]{1,0:T(8,128)(2,1)S(1)} %concatenate.11), channel_id=1, source_target_pairs={{8,16},{16,8},{24,32},{32,24},{40,48},{48,40},{72,80},{80,72},{88,... | collective-permute-start | bytes 1327112 | tf_op jit(solution)/shard_map/ppermute | solution.py:161
  19.2 0.1 pad_add_fusion.where_ref
  19.3 0.0 copy-start.1
  19.3 3.8 %all_gather.7.both_ref = bf16[432,1024]{1,0:T(8,128)(2,1)S(1)} all-gather(bf16[216,1024]{1,0:T(8,128)(2,1)S(1)} %concatenate.11), channel_id=1, replica_groups={{0,8},{16,24},{32,40},{48,56},{64,72},{80,88},{96,104},{112,120},{128,1..., dimensions={0}, use_global_device_ids=true | all-gather | bytes 1327104 | tf_op jit(solution)/shard_map/all_gather | solution.py:162
  23.0 1.6 %collective-permute-done.3.w1_ref = bf16[864,256]{1,0:T(8,128)(2,1)S(1)} collective-permute-done((bf16[864,256]{1,0:T(8,128)(2,1)S(1)}, bf16[864,256]{1,0:T(8,128)(2,1)S(1)}, u32[]{:S(2)}, u32[]{:S(2)}) %collective-permute-start.3) | collective-permute-done | bytes 442400 | tf_op jit(solution)/shard_map/ppermute | solution.py:159
  24.7 2.2 %collective-permute-done.2.outer_ref = bf16[216,1024]{1,0:T(8,128)(2,1)S(1)} collective-permute-done((bf16[216,1024]{1,0:T(8,128)(2,1)S(1)}, bf16[216,1024]{1,0:T(8,128)(2,1)S(1)}, u32[]{:S(2)}, u32[]{:S(2)}) %collective-permute-start.2) | collective-permute-done | bytes 442400 | tf_op jit(solution)/shard_map/ppermute | solution.py:161
  26.9 0.0 copy-done.1
  26.9 11.9 %conv.1 = f32[256,512]{1,0:T(8,128)S(1)} custom-call(s32[2]{0:T(128)S(1)} %pad_add_fusion.where_ref, s32[27,1024]{1,0:T(8,128)S(1)} %copy-done.1, bf16[432,1024]{1,0:T(8,128)(2,1)S(1)} %all_gather.7.both_ref, bf16[216,1024]{1,0:T(8,128)(2,1)S(1)} %collective-permute-done.2.outer_ref, bf16[864,256]{1,0:T(8,128)(2,1)S(1)} %bitcast.9, ...), custom_call_target="tpu_custom_call" | custom-call | tf_op jit(solution)/shard_map/conv/pallas_call | solution.py:164
  38.8 27.5 %all_to_all.9.got_ref = f32[8,32,512]{2,1,0:T(8,128)S(1)} all-to-all(f32[8,32,512]{2,1,0:T(8,128)S(1)} %bitcast.7), channel_id=1, replica_groups=mesh['space'=64,'chan'=8] {'chan'}, dimensions={0} | all-to-all | bytes 1048576 | tf_op jit(solution)/shard_map/all_to_all | solution.py:182
  66.3 0.7 add.14
  (3 shorter events, 0.1 us)
Async XLA Ops:
  0.0 12.3 %copy-start = (bf16[27,32,256]{2,1,0:T(8,128)(2,1)S(1)}, bf16[27,32,256]{2,1,0:T(8,128)(2,1)}, u32[]{:S(2)}) copy-start(bf16[27,32,256]{2,1,0:T(8,128)(2,1)} %param.5) | copy-start | bytes 1327108
  6.4 9.8 %collective-permute-start.1 = (bf16[72,1024]{1,0:T(8,128)(2,1)S(1)}, bf16[72,1024]{1,0:T(8,128)(2,1)S(1)}, u32[]{:S(2)}, u32[]{:S(2)}) collective-permute-start(bf16[72,1024]{1,0:T(8,128)(2,1)S(1)} %get-tuple-element.5), channel_id=1, source_target_pairs={{64,0},{72,8},{80,16},{88,24},{96,32},{104,40},{112,48},{120,56},{... | collective-permute-start | bytes 442376 | tf_op jit(solution)/shard_map/ppermute | solution.py:29
  8.8 8.2 %collective-permute-start = (bf16[72,1024]{1,0:T(8,128)(2,1)S(1)}, bf16[72,1024]{1,0:T(8,128)(2,1)S(1)}, u32[]{:S(2)}, u32[]{:S(2)}) collective-permute-start(bf16[72,1024]{1,0:T(8,128)(2,1)S(1)} %get-tuple-element.6), channel_id=1, source_target_pairs={{0,64},{8,72},{16,80},{24,88},{32,96},{40,104},{48,112},{56,120},{... | collective-permute-start | bytes 442376 | tf_op jit(solution)/shard_map/ppermute | solution.py:29
  12.3 12.4 %collective-permute-start.3 = (bf16[864,256]{1,0:T(8,128)(2,1)S(1)}, bf16[864,256]{1,0:T(8,128)(2,1)S(1)}, u32[]{:S(2)}, u32[]{:S(2)}) collective-permute-start(bf16[864,256]{1,0:T(8,128)(2,1)S(1)} %bitcast.8), channel_id=1, source_target_pairs={{0,1},{1,0},{2,3},{3,2},{4,5},{5,4},{6,7},{7,6},{8,9},{9,8},{10,11... | collective-permute-start | bytes 1327112 | tf_op jit(solution)/shard_map/ppermute | solution.py:159
  17.2 9.6 %collective-permute-start.2 = (bf16[216,1024]{1,0:T(8,128)(2,1)S(1)}, bf16[216,1024]{1,0:T(8,128)(2,1)S(1)}, u32[]{:S(2)}, u32[]{:S(2)}) collective-permute-start(bf16[216,1024]{1,0:T(8,128)(2,1)S(1)} %concatenate.11), channel_id=1, source_target_pairs={{8,16},{16,8},{24,32},{32,24},{40,48},{48,40},{72,80},{80,72},{88,... | collective-permute-start | bytes 1327112 | tf_op jit(solution)/shard_map/ppermute | solution.py:161
  19.3 7.6 %copy-start.1 = (s32[27,1024]{1,0:T(8,128)S(1)}, s32[27,1024]{1,0:T(8,128)}, u32[]{:S(2)}) copy-start(s32[27,1024]{1,0:T(8,128)} %gm_ref.1) | copy-start | bytes 331780

commit v8 on v7

--- a/solution.py
+++ b/solution.py
@@ -29,8 +29,8 @@
     return lax.ppermute(value, "space", pairs)
 
 
-def conv_kernel(where_ref, gm_ref, both_ref, outer_ref, w0_ref, w1_ref,
-                out_ref, table, digit, lut, comp, index, lhs, wall, sem):
+def pick_kernel(where_ref, gm_ref, both_ref, outer_ref,
+                lhs, table, digit, lut, comp, index, sem):
     par = where_ref[0]
     core = where_ref[1]
     sources = [both_ref.at[pl.ds(MSG * i, MSG)] for i in range(6)]
@@ -82,12 +82,6 @@
             table[block * V + 128 * c:block * V + 128 * (c + 1), :] = x.T
     table[ZERO:ROWS, :] = jnp.zeros((8, 128), jnp.float32)
 
-    for place in range(OFFS):
-        k = {CENTRE: OFFS - 1, OFFS - 1: CENTRE}.get(place, place)
-        for side, w_ref in ((par, w0_ref), (1 - par, w1_ref)):
-            wall[pl.ds(pl.multiple_of(64 * place + 32 * side, 32), 32), :] = w_ref[32 * k:32 * k + 32, :]
-    wall[64 * OFFS:, :] = jnp.zeros((64, 256), jnp.bfloat16)
-
     own = pl.multiple_of(own_base * V + par * HALF, 128)
     lhs[:, 128 * (PAIRS - 1):] = table[pl.ds(own, HALF), :].astype(jnp.bfloat16)
 
@@ -119,6 +113,14 @@
             lanes = pl.ds(pl.multiple_of(128 * pair, 128), 128)
             lhs[rows, lanes] = jnp.concatenate(tiles, axis=0).astype(jnp.bfloat16)
 
+
+def multiply_kernel(where_ref, lhs, w0_ref, w1_ref, out_ref, wall):
+    par = where_ref[0]
+    for place in range(OFFS):
+        k = {CENTRE: OFFS - 1, OFFS - 1: CENTRE}.get(place, place)
+        for side, w_ref in ((par, w0_ref), (1 - par, w1_ref)):
+            wall[pl.ds(pl.multiple_of(64 * place + 32 * side, 32), 32), :] = w_ref[32 * k:32 * k + 32, :]
+    wall[64 * OFFS:, :] = jnp.zeros((64, 256), jnp.bfloat16)
     total = jnp.dot(lhs[...], wall[...], preferred_element_type=jnp.float32)
     out_ref[...] = total.T
 
@@ -161,10 +163,12 @@
     outer = lax.ppermute(strip, "space", facing)
     both = lax.all_gather(strip, "space", axis=0, tiled=True, axis_index_groups=chips)
     vmem = pl.BlockSpec(memory_space=pltpu.VMEM)
-    part = pl.pallas_call(
-        conv_kernel,
-        out_shape=jax.ShapeDtypeStruct((256, HALF), jnp.float32),
-        in_specs=[pl.BlockSpec(memory_space=pltpu.SMEM)] + [vmem] * 5,
+    smem = pl.BlockSpec(memory_space=pltpu.SMEM)
+    where = jnp.stack([par, core]).astype(jnp.int32)
+    lhs = pl.pallas_call(
+        pick_kernel,
+        out_shape=jax.ShapeDtypeStruct((HALF, 128 * PAIRS), jnp.bfloat16),
+        in_specs=[smem] + [vmem] * 3,
         out_specs=vmem,
         scratch_shapes=[
             pltpu.VMEM((ROWS, 128), jnp.float32),
@@ -172,13 +176,21 @@
             pltpu.VMEM((48, 128), jnp.int32),
             pltpu.VMEM((128, 128), jnp.int32),
             pltpu.SMEM((128, 128), jnp.int32),
-            pltpu.VMEM((HALF, 128 * PAIRS), jnp.bfloat16),
-            pltpu.VMEM((128 * PAIRS, 256), jnp.bfloat16),
             pltpu.SemaphoreType.DMA((4,)),
         ],
-        compiler_params=pltpu.CompilerParams(vmem_limit_bytes=40 * 2**20),
-        name="conv",
-    )(jnp.stack([par, core]).astype(jnp.int32), gather_map, both, outer, w0, w1)
+        compiler_params=pltpu.CompilerParams(vmem_limit_bytes=20 * 2**20),
+        cost_estimate=pl.CostEstimate(flops=0, transcendentals=0, bytes_accessed=30 * 2**20),
+        name="pick",
+    )(where, gather_map, both, outer)
+    part = pl.pallas_call(
+        multiply_kernel,
+        out_shape=jax.ShapeDtypeStruct((256, HALF), jnp.float32),
+        in_specs=[smem] + [vmem] * 3,
+        out_specs=vmem,
+        scratch_shapes=[pltpu.VMEM((128 * PAIRS, 256), jnp.bfloat16)],
+        compiler_params=pltpu.CompilerParams(vmem_limit_bytes=16 * 2**20),
+        name="multiply",
+    )(where, lhs, w0, w1)
     got = lax.all_to_all(part, "chan", 0, 0, tiled=True).reshape(8, 32, HALF)
     return pl.pallas_call(
         add_kernel,

time: 67.2 us -> 70.5 us (1.049)
  the two profiles are of different devices: /device:TPU:34 before, /device:TPU:25 now
where the time goes in v8:
time: 70.5 us; the launch traced here: 70.3 us
  blocking collectives  34.6 us (49%)
  starting transfers between devices  15.9 us (23%)
  Pallas kernels  13.3 us (19%)
  waiting for transfers between devices  5.3 us (8%)
  other arithmetic  0.89 us (1%)
    all_to_all x1, blocking collectives, local(): got = lax.all_to_all(part, 'chan', 0, 0, tiled=True).reshape(8, 32, HALF)  27.5 us
    pallas_call x1, Pallas kernels, local(): pl.pallas_call(pick_kernel, out_shape=jax.ShapeDtypeStruct((HALF, 128 * P...  11.3 us
    ppermute x2, starting transfers between devices, shift(): return lax.ppermute(value, 'space', pairs)  6.34 us
    ppermute x1, starting transfers between devices, local(): outer = lax.ppermute(strip, 'space', facing)  5.98 us
    ppermute x2, waiting for transfers between devices, shift(): return lax.ppermute(value, 'space', pairs)  5.17 us
    all_gather x1, blocking collectives, local(): lax.all_gather(features.T, 'chan', axis=0, tiled=True, axis_index_groups=...  4.66 us
    ppermute x1, starting transfers between devices, local(): w1 = lax.ppermute(w0, 'chan', flip)  3.61 us
    all_gather x1, blocking collectives, local(): lax.all_gather(strip, 'space', axis=0, tiled=True, axis_index_groups=chips)  2.43 us
  transfers between devices with their start and end apart: 4, of which 3 were waited for; matrix products, arithmetic and copies ran while one was open for 0% of the time, Pallas kernels for 16%

profile of v8, /device:TPU:25, one launch (start us, length us, event | category | flops | bytes accessed | tf_op | source)
XLA Modules:
  0.0 70.3 jit_solution(13140288339077888120)
XLA Ops:
  0.0 0.0 copy-start.1
  0.0 0.8 %fusion.1 = (bf16[8,1024]{1,0:T(8,128)(2,1)S(1)}, bf16[8,1024]{1,0:T(8,128)(2,1)S(1)}) fusion(s32[8,768]{1,0:T(8,128)} %bitcast.11), kind=kLoop, calls=%fused_computation.5 | loop fusion | flops 32768 | bytes 57344 | tf_op jit(solution)/shard_map/convert_element_type | solution.py:152
  0.8 4.7 %all_gather.6 = bf16[64,1024]{1,0:T(8,128)(2,1)S(1)} all-gather(bf16[32,1024]{1,0:T(8,128)(2,1)} %bitcast.10), channel_id=1, replica_groups={{0,1},{2,3},{4,5},{6,7},{8,9},{10,11},{12,13},{14,15},{16,17},{18,19},{..., dimensions={0}, use_global_device_ids=true | all-gather | bytes 196608 | tf_op jit(solution)/shard_map/all_gather | solution.py:150
  5.5 4.4 %collective-permute-start = (bf16[72,1024]{1,0:T(8,128)(2,1)S(1)}, bf16[72,1024]{1,0:T(8,128)(2,1)S(1)}, u32[]{:S(2)}, u32[]{:S(2)}) collective-permute-start(bf16[72,1024]{1,0:T(8,128)(2,1)S(1)} %get-tuple-element.6), channel_id=1, source_target_pairs={{0,64},{8,72},{16,80},{24,88},{32,96},{40,104},{48,112},{56,120},{... | collective-permute-start | bytes 442376 | tf_op jit(solution)/shard_map/ppermute | solution.py:29
  9.9 1.9 %collective-permute-start.1 = (bf16[72,1024]{1,0:T(8,128)(2,1)S(1)}, bf16[72,1024]{1,0:T(8,128)(2,1)S(1)}, u32[]{:S(2)}, u32[]{:S(2)}) collective-permute-start(bf16[72,1024]{1,0:T(8,128)(2,1)S(1)} %get-tuple-element.5), channel_id=1, source_target_pairs={{64,0},{72,8},{80,16},{88,24},{96,32},{104,40},{112,48},{120,56},{... | collective-permute-start | bytes 442376 | tf_op jit(solution)/shard_map/ppermute | solution.py:29
  11.9 0.2 collective-permute-done
  12.0 5.0 %collective-permute-done.1 = bf16[72,1024]{1,0:T(8,128)(2,1)S(1)} collective-permute-done((bf16[72,1024]{1,0:T(8,128)(2,1)S(1)}, bf16[72,1024]{1,0:T(8,128)(2,1)S(1)}, u32[]{:S(2)}, u32[]{:S(2)}) %collective-permute-start.1) | collective-permute-done | bytes 147488 | tf_op jit(solution)/shard_map/ppermute | solution.py:29
  17.0 0.2 concatenate.11
  17.3 6.0 %collective-permute-start.2 = (bf16[216,1024]{1,0:T(8,128)(2,1)S(1)}, bf16[216,1024]{1,0:T(8,128)(2,1)S(1)}, u32[]{:S(2)}, u32[]{:S(2)}) collective-permute-start(bf16[216,1024]{1,0:T(8,128)(2,1)S(1)} %concatenate.11), channel_id=1, source_target_pairs={{8,16},{16,8},{24,32},{32,24},{40,48},{48,40},{72,80},{80,72},{88,... | collective-permute-start | bytes 1327112 | tf_op jit(solution)/shard_map/ppermute | solution.py:163
  23.2 3.6 %collective-permute-start.3 = (bf16[864,256]{1,0:T(8,128)(2,1)}, bf16[864,256]{1,0:T(8,128)(2,1)S(1)}, u32[]{:S(2)}, u32[]{:S(2)}) collective-permute-start(bf16[864,256]{1,0:T(8,128)(2,1)} %bitcast.8), channel_id=1, source_target_pairs={{0,1},{1,0},{2,3},{3,2},{4,5},{5,4},{6,7},{7,6},{8,9},{9,8},{10,11... | collective-permute-start | bytes 1327112 | tf_op jit(solution)/shard_map/ppermute | solution.py:161
  26.9 0.1 pad_add_fusion.where_ref
  26.9 2.4 %all_gather.7.both_ref = bf16[432,1024]{1,0:T(8,128)(2,1)S(1)} all-gather(bf16[216,1024]{1,0:T(8,128)(2,1)S(1)} %concatenate.11), channel_id=1, replica_groups={{0,8},{16,24},{32,40},{48,56},{64,72},{80,88},{96,104},{112,120},{128,1..., dimensions={0}, use_global_device_ids=true | all-gather | bytes 1327104 | tf_op jit(solution)/shard_map/all_gather | solution.py:164
  29.4 0.0 copy-start
  29.4 0.1 collective-permute-done.2.outer_ref
  29.5 0.0 copy-done.1
  29.5 11.3 %pick.1.lhs = bf16[512,1792]{1,0:T(8,128)(2,1)S(1)} custom-call(s32[2]{0:T(128)S(1)} %pad_add_fusion.where_ref, s32[27,1024]{1,0:T(8,128)S(1)} %copy-done.1, bf16[432,1024]{1,0:T(8,128)(2,1)S(1)} %all_gather.7.both_ref, bf16[216,1024]{1,0:T(8,128)(2,1)S(1)} %collective-permute-done.2.outer_ref), custom_call_target="tpu_custom_call" | custom-call | bytes 31457280 | tf_op jit(solution)/shard_map/pick/pallas_call | solution.py:168
  40.8 0.0 collective-permute-done.3.w1_ref
  40.8 0.0 copy-done
  40.8 1.3 %multiply.1 = f32[256,512]{1,0:T(8,128)S(1)} custom-call(s32[2]{0:T(128)S(1)} %pad_add_fusion.where_ref, bf16[512,1792]{1,0:T(8,128)(2,1)S(1)} %pick.1.lhs, bf16[864,256]{1,0:T(8,128)(2,1)S(1)} %bitcast.9, bf16[864,256]{1,0:T(8,128)(2,1)S(1)} %collective-permute-done.3.w1_ref), custom_call_target="tpu_custom_call" | custom-call | tf_op jit(solution)/shard_map/multiply/pallas_call | solution.py:185
  42.1 27.5 %all_to_all.9.got_ref = f32[8,32,512]{2,1,0:T(8,128)S(1)} all-to-all(f32[8,32,512]{2,1,0:T(8,128)S(1)} %bitcast.7), channel_id=1, replica_groups=mesh['space'=64,'chan'=8] {'chan'}, dimensions={0} | all-to-all | bytes 1048576 | tf_op jit(solution)/shard_map/all_to_all | solution.py:194
  69.6 0.7 add.14
  (3 shorter events, 0.1 us)
Async XLA Ops:
  0.0 29.5 %copy-start.1 = (s32[27,1024]{1,0:T(8,128)S(1)}, s32[27,1024]{1,0:T(8,128)}, u32[]{:S(2)}) copy-start(s32[27,1024]{1,0:T(8,128)} %gm_ref.1) | copy-start | bytes 331780
  5.5 6.5 %collective-permute-start = (bf16[72,1024]{1,0:T(8,128)(2,1)S(1)}, bf16[72,1024]{1,0:T(8,128)(2,1)S(1)}, u32[]{:S(2)}, u32[]{:S(2)}) collective-permute-start(bf16[72,1024]{1,0:T(8,128)(2,1)S(1)} %get-tuple-element.6), channel_id=1, source_target_pairs={{0,64},{8,72},{16,80},{24,88},{32,96},{40,104},{48,112},{56,120},{... | collective-permute-start | bytes 442376 | tf_op jit(solution)/shard_map/ppermute | solution.py:29
  9.9 7.1 %collective-permute-start.1 = (bf16[72,1024]{1,0:T(8,128)(2,1)S(1)}, bf16[72,1024]{1,0:T(8,128)(2,1)S(1)}, u32[]{:S(2)}, u32[]{:S(2)}) collective-permute-start(bf16[72,1024]{1,0:T(8,128)(2,1)S(1)} %get-tuple-element.5), channel_id=1, source_target_pairs={{64,0},{72,8},{80,16},{88,24},{96,32},{104,40},{112,48},{120,56},{... | collective-permute-start | bytes 442376 | tf_op jit(solution)/shard_map/ppermute | solution.py:29
  17.3 12.3 %collective-permute-start.2 = (bf16[216,1024]{1,0:T(8,128)(2,1)S(1)}, bf16[216,1024]{1,0:T(8,128)(2,1)S(1)}, u32[]{:S(2)}, u32[]{:S(2)}) collective-permute-start(bf16[216,1024]{1,0:T(8,128)(2,1)S(1)} %concatenate.11), channel_id=1, source_target_pairs={{8,16},{16,8},{24,32},{32,24},{40,48},{48,40},{72,80},{80,72},{88,... | collective-permute-start | bytes 1327112 | tf_op jit(solution)/shard_map/ppermute | solution.py:163
  23.2 17.6 %collective-permute-start.3 = (bf16[864,256]{1,0:T(8,128)(2,1)}, bf16[864,256]{1,0:T(8,128)(2,1)S(1)}, u32[]{:S(2)}, u32[]{:S(2)}) collective-permute-start(bf16[864,256]{1,0:T(8,128)(2,1)} %bitcast.8), channel_id=1, source_target_pairs={{0,1},{1,0},{2,3},{3,2},{4,5},{5,4},{6,7},{7,6},{8,9},{9,8},{10,11... | collective-permute-start | bytes 1327112 | tf_op jit(solution)/shard_map/ppermute | solution.py:161
  29.4 11.4 %copy-start = (bf16[27,32,256]{2,1,0:T(8,128)(2,1)S(1)}, bf16[27,32,256]{2,1,0:T(8,128)(2,1)}, u32[]{:S(2)}) copy-start(bf16[27,32,256]{2,1,0:T(8,128)(2,1)} %param.5) | copy-start | bytes 1327108

commit v9 on v7

--- a/solution.py
+++ b/solution.py
@@ -1,3 +1,5 @@
+import functools
+
 import jax
 import jax.numpy as jnp
 from jax import lax
@@ -29,10 +31,10 @@
     return lax.ppermute(value, "space", pairs)
 
 
-def conv_kernel(where_ref, gm_ref, both_ref, outer_ref, w0_ref, w1_ref,
+def conv_kernel(par_ref, core_ref, gm_ref, both_ref, outer_ref, w0_ref, w1_ref,
                 out_ref, table, digit, lut, comp, index, lhs, wall, sem):
-    par = where_ref[0]
-    core = where_ref[1]
+    par = par_ref[0]
+    core = core_ref[0]
     sources = [both_ref.at[pl.ds(MSG * i, MSG)] for i in range(6)]
     sources += [outer_ref.at[pl.ds(MSG * i, MSG)] for i in range(3)]
     own_base = 3 * core
@@ -95,14 +97,9 @@
     lane = lax.broadcasted_iota(jnp.int32, (8, 128), 1)
     masks = [sub == j for j in range(8)]
     left = lane < 64
-    for copy in copies:
-        copy.wait()
-
-    @pl.loop(0, 4 * (PAIRS - 1))
-    def _(step):
-        pair = step >> 2
-        quarter = step & 3
-        line = quarter * 32 + 2 * pair
+    def pick(pair, quarter):
+        lanes = pl.ds(128 * pair, 128)
+        line = 2 * pair
         for h in range(0, 128, 16):
             tiles = []
             for g in range(h, h + 16, 8):
@@ -110,14 +107,18 @@
                 for side in range(2):
                     acc = None
                     for j in range(8):
-                        at = index.at[pl.ds(side, 127), pl.ds(g + j, 1)][line, 0]
+                        at = index.at[pl.ds(32 * quarter + side, 31), pl.ds(g + j, 1)][line, 0]
                         row = table[pl.ds(at, 8, stride=0), :]
                         acc = row if acc is None else jnp.where(masks[j], row, acc)
                     sides.append(acc)
                 tiles.append(jnp.where(left, sides[0], sides[1]))
-            rows = pl.ds(pl.multiple_of(quarter * 128 + h, 16), 16)
-            lanes = pl.ds(pl.multiple_of(128 * pair, 128), 128)
+            rows = slice(128 * quarter + h, 128 * quarter + h + 16)
             lhs[rows, lanes] = jnp.concatenate(tiles, axis=0).astype(jnp.bfloat16)
+
+    for quarter, copy in enumerate(copies):
+        copy.wait()
+        for pair in range(PAIRS - 1):
+            pick(pair, quarter)
 
     total = jnp.dot(lhs[...], wall[...], preferred_element_type=jnp.float32)
     out_ref[...] = total.T
@@ -164,7 +165,7 @@
     part = pl.pallas_call(
         conv_kernel,
         out_shape=jax.ShapeDtypeStruct((256, HALF), jnp.float32),
-        in_specs=[pl.BlockSpec(memory_space=pltpu.SMEM)] + [vmem] * 5,
+        in_specs=[pl.BlockSpec(memory_space=pltpu.SMEM)] * 2 + [vmem] * 5,
         out_specs=vmem,
         scratch_shapes=[
             pltpu.VMEM((ROWS, 128), jnp.float32),
@@ -178,7 +179,7 @@
         ],
         compiler_params=pltpu.CompilerParams(vmem_limit_bytes=40 * 2**20),
         name="conv",
-    )(jnp.stack([par, core]).astype(jnp.int32), gather_map, both, outer, w0, w1)
+    )(par.reshape(1), core.reshape(1), gather_map, both, outer, w0, w1)
     got = lax.all_to_all(part, "chan", 0, 0, tiled=True).reshape(8, 32, HALF)
     return pl.pallas_call(
         add_kernel,

time: 67.2 us -> 64.5 us (0.960)
  Pallas kernels: 12.6 us -> 9.93 us
    pallas_call x1, Pallas kernels: 11.9 us -> 9.27 us  [local(): pl.pallas_call(conv_kernel, out_shape=jax.ShapeDtypeStruct((256, HALF), j...]
where the time goes in v9:
time: 64.5 us; the launch traced here: 64.3 us
  blocking collectives  36.8 us (57%)
  starting transfers between devices  11.7 us (18%)
  Pallas kernels  9.93 us (15%)
  waiting for transfers between devices  4.71 us (7%)
  other arithmetic  0.83 us (1%)
    all_to_all x1, blocking collectives, local(): got = lax.all_to_all(part, 'chan', 0, 0, tiled=True).reshape(8, 32, HALF)  27.5 us
    pallas_call x1, Pallas kernels, local(): pl.pallas_call(conv_kernel, out_shape=jax.ShapeDtypeStruct((256, HALF), j...  9.27 us
    ppermute x2, starting transfers between devices, shift(): return lax.ppermute(value, 'space', pairs)  5.84 us
    all_gather x1, blocking collectives, local(): lax.all_gather(features.T, 'chan', axis=0, tiled=True, axis_index_groups=...  5.53 us
    ppermute x1, starting transfers between devices, local(): w1 = lax.ppermute(w0, 'chan', flip)  3.89 us
    all_gather x1, blocking collectives, local(): lax.all_gather(strip, 'space', axis=0, tiled=True, axis_index_groups=chips)  3.79 us
    ppermute x1, waiting for transfers between devices, local(): outer = lax.ppermute(strip, 'space', facing)  2.2 us
    ppermute x1, starting transfers between devices, local(): outer = lax.ppermute(strip, 'space', facing)  1.92 us
  transfers between devices with their start and end apart: 4, of which 3 were waited for; matrix products, arithmetic and copies ran while one was open for 0% of the time, Pallas kernels for 0%

profile of v9, /device:TPU:34, one launch (start us, length us, event | category | flops | bytes accessed | tf_op | source)
XLA Modules:
  0.0 64.3 jit_solution(9545626177390041378)
XLA Ops:
  0.0 0.0 copy-start
  0.0 0.8 %fusion.1 = (bf16[8,1024]{1,0:T(8,128)(2,1)S(1)}, bf16[8,1024]{1,0:T(8,128)(2,1)S(1)}) fusion(s32[8,768]{1,0:T(8,128)} %bitcast.11), kind=kLoop, calls=%fused_computation.5 | loop fusion | flops 32768 | bytes 57344 | tf_op jit(solution)/shard_map/convert_element_type | solution.py:151
  0.8 5.5 %all_gather.6 = bf16[64,1024]{1,0:T(8,128)(2,1)S(1)} all-gather(bf16[32,1024]{1,0:T(8,128)(2,1)} %bitcast.10), channel_id=1, replica_groups={{0,1},{2,3},{4,5},{6,7},{8,9},{10,11},{12,13},{14,15},{16,17},{18,19},{..., dimensions={0}, use_global_device_ids=true | all-gather | bytes 196608 | tf_op jit(solution)/shard_map/all_gather | solution.py:149
  6.4 2.4 %collective-permute-start.1 = (bf16[72,1024]{1,0:T(8,128)(2,1)S(1)}, bf16[72,1024]{1,0:T(8,128)(2,1)S(1)}, u32[]{:S(2)}, u32[]{:S(2)}) collective-permute-start(bf16[72,1024]{1,0:T(8,128)(2,1)S(1)} %get-tuple-element.5), channel_id=1, source_target_pairs={{64,0},{72,8},{80,16},{88,24},{96,32},{104,40},{112,48},{120,56},{... | collective-permute-start | bytes 442376 | tf_op jit(solution)/shard_map/ppermute | solution.py:31
  8.8 3.5 %collective-permute-start = (bf16[72,1024]{1,0:T(8,128)(2,1)S(1)}, bf16[72,1024]{1,0:T(8,128)(2,1)S(1)}, u32[]{:S(2)}, u32[]{:S(2)}) collective-permute-start(bf16[72,1024]{1,0:T(8,128)(2,1)S(1)} %get-tuple-element.6), channel_id=1, source_target_pairs={{0,64},{8,72},{16,80},{24,88},{32,96},{40,104},{48,112},{56,120},{... | collective-permute-start | bytes 442376 | tf_op jit(solution)/shard_map/ppermute | solution.py:31
  12.3 0.0 copy-done
  12.3 3.9 %collective-permute-start.3 = (bf16[864,256]{1,0:T(8,128)(2,1)S(1)}, bf16[864,256]{1,0:T(8,128)(2,1)S(1)}, u32[]{:S(2)}, u32[]{:S(2)}) collective-permute-start(bf16[864,256]{1,0:T(8,128)(2,1)S(1)} %bitcast.8), channel_id=1, source_target_pairs={{0,1},{1,0},{2,3},{3,2},{4,5},{5,4},{6,7},{7,6},{8,9},{9,8},{10,11... | collective-permute-start | bytes 1327112 | tf_op jit(solution)/shard_map/ppermute | solution.py:160
  16.2 0.0 collective-permute-done.1
  16.2 0.8 %collective-permute-done = bf16[72,1024]{1,0:T(8,128)(2,1)S(1)} collective-permute-done((bf16[72,1024]{1,0:T(8,128)(2,1)S(1)}, bf16[72,1024]{1,0:T(8,128)(2,1)S(1)}, u32[]{:S(2)}, u32[]{:S(2)}) %collective-permute-start) | collective-permute-done | bytes 147488 | tf_op jit(solution)/shard_map/ppermute | solution.py:31
  17.0 0.2 concatenate.11
  17.2 1.9 %collective-permute-start.2 = (bf16[216,1024]{1,0:T(8,128)(2,1)S(1)}, bf16[216,1024]{1,0:T(8,128)(2,1)S(1)}, u32[]{:S(2)}, u32[]{:S(2)}) collective-permute-start(bf16[216,1024]{1,0:T(8,128)(2,1)S(1)} %concatenate.11), channel_id=1, source_target_pairs={{8,16},{16,8},{24,32},{32,24},{40,48},{48,40},{72,80},{80,72},{88,... | collective-permute-start | bytes 1327112 | tf_op jit(solution)/shard_map/ppermute | solution.py:162
  19.2 0.0 copy-start.1
  19.2 3.8 %all_gather.7.both_ref = bf16[432,1024]{1,0:T(8,128)(2,1)S(1)} all-gather(bf16[216,1024]{1,0:T(8,128)(2,1)S(1)} %concatenate.11), channel_id=1, replica_groups={{0,8},{16,24},{32,40},{48,56},{64,72},{80,88},{96,104},{112,120},{128,1..., dimensions={0}, use_global_device_ids=true | all-gather | bytes 1327104 | tf_op jit(solution)/shard_map/all_gather | solution.py:163
  23.0 1.7 %collective-permute-done.3.w1_ref = bf16[864,256]{1,0:T(8,128)(2,1)S(1)} collective-permute-done((bf16[864,256]{1,0:T(8,128)(2,1)S(1)}, bf16[864,256]{1,0:T(8,128)(2,1)S(1)}, u32[]{:S(2)}, u32[]{:S(2)}) %collective-permute-start.3) | collective-permute-done | bytes 442400 | tf_op jit(solution)/shard_map/ppermute | solution.py:160
  24.7 2.2 %collective-permute-done.2.outer_ref = bf16[216,1024]{1,0:T(8,128)(2,1)S(1)} collective-permute-done((bf16[216,1024]{1,0:T(8,128)(2,1)S(1)}, bf16[216,1024]{1,0:T(8,128)(2,1)S(1)}, u32[]{:S(2)}, u32[]{:S(2)}) %collective-permute-start.2) | collective-permute-done | bytes 442400 | tf_op jit(solution)/shard_map/ppermute | solution.py:162
  26.9 0.0 copy-done.1
  26.9 9.3 %conv.1 = f32[256,512]{1,0:T(8,128)S(1)} custom-call(s32[1]{0:T(128)} %bitcast.par_ref, s32[1]{0:T(128)} %bitcast.1.core_ref, s32[27,1024]{1,0:T(8,128)S(1)} %copy-done.1, bf16[432,1024]{1,0:T(8,128)(2,1)S(1)} %all_gather.7.both_ref, bf16[216,1024]{1,0:T(8,128)(2,1)S(1)} %collective-permute-done.2.outer_ref, bf16[864,256]{1,0:T(8,128)(2,1)S(1)} %bitcast.9, ...), custom_call_target="tpu_custom_call" | custom-call | tf_op jit(solution)/shard_map/conv/pallas_call | solution.py:165
  36.1 27.5 %all_to_all.9.got_ref = f32[8,32,512]{2,1,0:T(8,128)S(1)} all-to-all(f32[8,32,512]{2,1,0:T(8,128)S(1)} %bitcast.7), channel_id=1, replica_groups=mesh['space'=64,'chan'=8] {'chan'}, dimensions={0} | all-to-all | bytes 1048576 | tf_op jit(solution)/shard_map/all_to_all | solution.py:183
  63.6 0.7 %add.12 = bf16[32,1024]{1,0:T(8,128)(2,1)} custom-call(f32[8,32,512]{2,1,0:T(8,128)S(1)} %all_to_all.9.got_ref), custom_call_target="tpu_custom_call" | custom-call | tf_op jit(solution)/shard_map/add/pallas_call | solution.py:184
  (3 shorter events, 0.1 us)
Async XLA Ops:
  0.0 12.3 %copy-start = (bf16[27,32,256]{2,1,0:T(8,128)(2,1)S(1)}, bf16[27,32,256]{2,1,0:T(8,128)(2,1)}, u32[]{:S(2)}) copy-start(bf16[27,32,256]{2,1,0:T(8,128)(2,1)} %param.5) | copy-start | bytes 1327108
  6.4 9.8 %collective-permute-start.1 = (bf16[72,1024]{1,0:T(8,128)(2,1)S(1)}, bf16[72,1024]{1,0:T(8,128)(2,1)S(1)}, u32[]{:S(2)}, u32[]{:S(2)}) collective-permute-start(bf16[72,1024]{1,0:T(8,128)(2,1)S(1)} %get-tuple-element.5), channel_id=1, source_target_pairs={{64,0},{72,8},{80,16},{88,24},{96,32},{104,40},{112,48},{120,56},{... | collective-permute-start | bytes 442376 | tf_op jit(solution)/shard_map/ppermute | solution.py:31
  8.8 8.2 %collective-permute-start = (bf16[72,1024]{1,0:T(8,128)(2,1)S(1)}, bf16[72,1024]{1,0:T(8,128)(2,1)S(1)}, u32[]{:S(2)}, u32[]{:S(2)}) collective-permute-start(bf16[72,1024]{1,0:T(8,128)(2,1)S(1)} %get-tuple-element.6), channel_id=1, source_target_pairs={{0,64},{8,72},{16,80},{24,88},{32,96},{40,104},{48,112},{56,120},{... | collective-permute-start | bytes 442376 | tf_op jit(solution)/shard_map/ppermute | solution.py:31
  12.3 12.4 %collective-permute-start.3 = (bf16[864,256]{1,0:T(8,128)(2,1)S(1)}, bf16[864,256]{1,0:T(8,128)(2,1)S(1)}, u32[]{:S(2)}, u32[]{:S(2)}) collective-permute-start(bf16[864,256]{1,0:T(8,128)(2,1)S(1)} %bitcast.8), channel_id=1, source_target_pairs={{0,1},{1,0},{2,3},{3,2},{4,5},{5,4},{6,7},{7,6},{8,9},{9,8},{10,11... | collective-permute-start | bytes 1327112 | tf_op jit(solution)/shard_map/ppermute | solution.py:160
  17.2 9.6 %collective-permute-start.2 = (bf16[216,1024]{1,0:T(8,128)(2,1)S(1)}, bf16[216,1024]{1,0:T(8,128)(2,1)S(1)}, u32[]{:S(2)}, u32[]{:S(2)}) collective-permute-start(bf16[216,1024]{1,0:T(8,128)(2,1)S(1)} %concatenate.11), channel_id=1, source_target_pairs={{8,16},{16,8},{24,32},{32,24},{40,48},{48,40},{72,80},{80,72},{88,... | collective-permute-start | bytes 1327112 | tf_op jit(solution)/shard_map/ppermute | solution.py:162
  19.2 7.7 %copy-start.1 = (s32[27,1024]{1,0:T(8,128)S(1)}, s32[27,1024]{1,0:T(8,128)}, u32[]{:S(2)}) copy-start(s32[27,1024]{1,0:T(8,128)} %gm_ref.1) | copy-start | bytes 331780

commit v10 on v8

--- a/solution.py
+++ b/solution.py
@@ -1,3 +1,5 @@
+import functools
+
 import jax
 import jax.numpy as jnp
 from jax import lax
@@ -29,10 +31,10 @@
     return lax.ppermute(value, "space", pairs)
 
 
-def pick_kernel(where_ref, gm_ref, both_ref, outer_ref,
+def pick_kernel(par_ref, core_ref, gm_ref, both_ref, outer_ref,
                 lhs, table, digit, lut, comp, index, sem):
-    par = where_ref[0]
-    core = where_ref[1]
+    par = par_ref[0]
+    core = core_ref[0]
     sources = [both_ref.at[pl.ds(MSG * i, MSG)] for i in range(6)]
     sources += [outer_ref.at[pl.ds(MSG * i, MSG)] for i in range(3)]
     own_base = 3 * core
@@ -89,14 +91,9 @@
     lane = lax.broadcasted_iota(jnp.int32, (8, 128), 1)
     masks = [sub == j for j in range(8)]
     left = lane < 64
-    for copy in copies:
-        copy.wait()
-
-    @pl.loop(0, 4 * (PAIRS - 1))
-    def _(step):
-        pair = step >> 2
-        quarter = step & 3
-        line = quarter * 32 + 2 * pair
+    def pick(pair, quarter):
+        lanes = pl.ds(128 * pair, 128)
+        line = 2 * pair
         for h in range(0, 128, 16):
             tiles = []
             for g in range(h, h + 16, 8):
@@ -104,18 +101,22 @@
                 for side in range(2):
                     acc = None
                     for j in range(8):
-                        at = index.at[pl.ds(side, 127), pl.ds(g + j, 1)][line, 0]
+                        at = index.at[pl.ds(32 * quarter + side, 31), pl.ds(g + j, 1)][line, 0]
                         row = table[pl.ds(at, 8, stride=0), :]
                         acc = row if acc is None else jnp.where(masks[j], row, acc)
                     sides.append(acc)
                 tiles.append(jnp.where(left, sides[0], sides[1]))
-            rows = pl.ds(pl.multiple_of(quarter * 128 + h, 16), 16)
-            lanes = pl.ds(pl.multiple_of(128 * pair, 128), 128)
+            rows = slice(128 * quarter + h, 128 * quarter + h + 16)
             lhs[rows, lanes] = jnp.concatenate(tiles, axis=0).astype(jnp.bfloat16)
 
-
-def multiply_kernel(where_ref, lhs, w0_ref, w1_ref, out_ref, wall):
-    par = where_ref[0]
+    for quarter, copy in enumerate(copies):
+        copy.wait()
+        for pair in range(PAIRS - 1):
+            pick(pair, quarter)
+
+
+def multiply_kernel(par_ref, lhs, w0_ref, w1_ref, out_ref, wall):
+    par = par_ref[0]
     for place in range(OFFS):
         k = {CENTRE: OFFS - 1, OFFS - 1: CENTRE}.get(place, place)
         for side, w_ref in ((par, w0_ref), (1 - par, w1_ref)):
@@ -158,17 +159,16 @@
     own = message(FIRST[0])
     up = shift(message(FIRST[1]), 1, 0)
     dn = shift(message(FIRST[2]), -1, 0)
-    w1 = lax.ppermute(w0, "chan", flip)
+    w1 = lax.ppermute(jnp.pad(w0, ((0, 96), (0, 0))), "chan", flip)
     strip = jnp.concatenate([own, up, dn], axis=0)
     outer = lax.ppermute(strip, "space", facing)
     both = lax.all_gather(strip, "space", axis=0, tiled=True, axis_index_groups=chips)
     vmem = pl.BlockSpec(memory_space=pltpu.VMEM)
     smem = pl.BlockSpec(memory_space=pltpu.SMEM)
-    where = jnp.stack([par, core]).astype(jnp.int32)
     lhs = pl.pallas_call(
         pick_kernel,
         out_shape=jax.ShapeDtypeStruct((HALF, 128 * PAIRS), jnp.bfloat16),
-        in_specs=[smem] + [vmem] * 3,
+        in_specs=[smem] * 2 + [vmem] * 3,
         out_specs=vmem,
         scratch_shapes=[
             pltpu.VMEM((ROWS, 128), jnp.float32),
@@ -179,9 +179,9 @@
             pltpu.SemaphoreType.DMA((4,)),
         ],
         compiler_params=pltpu.CompilerParams(vmem_limit_bytes=20 * 2**20),
-        cost_estimate=pl.CostEstimate(flops=0, transcendentals=0, bytes_accessed=30 * 2**20),
+        cost_estimate=pl.CostEstimate(flops=0, transcendentals=0, bytes_accessed=1024),
         name="pick",
-    )(where, gather_map, both, outer)
+    )(par.reshape(1), core.reshape(1), gather_map, both, outer)
     part = pl.pallas_call(
         multiply_kernel,
         out_shape=jax.ShapeDtypeStruct((256, HALF), jnp.float32),
@@ -190,7 +190,7 @@
         scratch_shapes=[pltpu.VMEM((128 * PAIRS, 256), jnp.bfloat16)],
         compiler_params=pltpu.CompilerParams(vmem_limit_bytes=16 * 2**20),
         name="multiply",
-    )(where, lhs, w0, w1)
+    )(par.reshape(1), lhs, w0, w1)
     got = lax.all_to_all(part, "chan", 0, 0, tiled=True).reshape(8, 32, HALF)
     return pl.pallas_call(
         add_kernel,

time: 70.5 us -> 67.3 us (0.955)
  the two profiles are of different devices: /device:TPU:25 before, /device:TPU:26 now
where the time goes in v10:
time: 67.3 us; the launch traced here: 67 us
  blocking collectives  36.7 us (55%)
  starting transfers between devices  12.6 us (19%)
  Pallas kernels  10.2 us (15%)
  waiting for transfers between devices  5.38 us (8%)
  local copies, waits for them, and re-layouts  1.28 us (2%)
  other arithmetic  0.78 us (1%)
    all_to_all x1, blocking collectives, local(): got = lax.all_to_all(part, 'chan', 0, 0, tiled=True).reshape(8, 32, HALF)  27.5 us
    pallas_call x1, Pallas kernels, local(): pl.pallas_call(pick_kernel, out_shape=jax.ShapeDtypeStruct((HALF, 128 * P...  8.73 us
    ppermute x2, starting transfers between devices, shift(): return lax.ppermute(value, 'space', pairs)  6.75 us
    all_gather x1, blocking collectives, local(): lax.all_gather(features.T, 'chan', axis=0, tiled=True, axis_index_groups=...  5.53 us
    ppermute x1, waiting for transfers between devices, local(): outer = lax.ppermute(strip, 'space', facing)  4.01 us
    ppermute x1, starting transfers between devices, local(): w1 = lax.ppermute(jnp.pad(w0, ((0, 96), (0, 0))), 'chan', flip)  3.89 us
    all_gather x1, blocking collectives, local(): lax.all_gather(strip, 'space', axis=0, tiled=True, axis_index_groups=chips)  3.66 us
    ppermute x1, starting transfers between devices, local(): outer = lax.ppermute(strip, 'space', facing)  1.92 us
  transfers between devices with their start and end apart: 4, of which 2 were waited for; matrix products, arithmetic and copies ran while one was open for 2% of the time, Pallas kernels for 13%

profile of v10, /device:TPU:26, one launch (start us, length us, event | category | flops | bytes accessed | tf_op | source)
XLA Modules:
  0.0 67.0 jit_solution(3325759872233833572)
XLA Ops:
  0.0 0.7 %fusion.1 = (bf16[8,1024]{1,0:T(8,128)(2,1)S(1)}, bf16[8,1024]{1,0:T(8,128)(2,1)S(1)}) fusion(s32[8,768]{1,0:T(8,128)} %bitcast.11), kind=kLoop, calls=%fused_computation.5 | loop fusion | flops 32768 | bytes 57344 | tf_op jit(solution)/shard_map/convert_element_type | solution.py:153
  0.7 5.5 %all_gather.6 = bf16[64,1024]{1,0:T(8,128)(2,1)S(1)} all-gather(bf16[32,1024]{1,0:T(8,128)(2,1)} %bitcast.10), channel_id=1, replica_groups={{0,1},{2,3},{4,5},{6,7},{8,9},{10,11},{12,13},{14,15},{16,17},{18,19},{..., dimensions={0}, use_global_device_ids=true | all-gather | bytes 196608 | tf_op jit(solution)/shard_map/all_gather | solution.py:151
  6.3 0.0 copy-start.1
  6.4 4.8 %collective-permute-start = (bf16[72,1024]{1,0:T(8,128)(2,1)S(1)}, bf16[72,1024]{1,0:T(8,128)(2,1)S(1)}, u32[]{:S(2)}, u32[]{:S(2)}) collective-permute-start(bf16[72,1024]{1,0:T(8,128)(2,1)S(1)} %get-tuple-element.6), channel_id=1, source_target_pairs={{0,64},{8,72},{16,80},{24,88},{32,96},{40,104},{48,112},{56,120},{... | collective-permute-start | bytes 442376 | tf_op jit(solution)/shard_map/ppermute | solution.py:31
  11.2 1.9 %collective-permute-start.1 = (bf16[72,1024]{1,0:T(8,128)(2,1)S(1)}, bf16[72,1024]{1,0:T(8,128)(2,1)S(1)}, u32[]{:S(2)}, u32[]{:S(2)}) collective-permute-start(bf16[72,1024]{1,0:T(8,128)(2,1)S(1)} %get-tuple-element.5), channel_id=1, source_target_pairs={{64,0},{72,8},{80,16},{88,24},{96,32},{104,40},{112,48},{120,56},{... | collective-permute-start | bytes 442376 | tf_op jit(solution)/shard_map/ppermute | solution.py:31
  13.1 1.0 %pad.9 = bf16[960,256]{1,0:T(8,128)(2,1)S(1)} pad(bf16[864,256]{1,0:T(8,128)(2,1)} %bitcast.8, bf16[]{:T(256)} %constant.33.clone.1), padding=0_96x0_0 | pad | bytes 933890 | tf_op jit(solution)/shard_map/jit(_pad)/pad | solution.py:162
  14.2 3.9 %collective-permute-start.3 = (bf16[960,256]{1,0:T(8,128)(2,1)S(1)}, bf16[960,256]{1,0:T(8,128)(2,1)S(1)}, u32[]{:S(2)}, u32[]{:S(2)}) collective-permute-start(bf16[960,256]{1,0:T(8,128)(2,1)S(1)} %pad.9), channel_id=1, source_target_pairs={{0,1},{1,0},{2,3},{3,2},{4,5},{5,4},{6,7},{7,6},{8,9},{9,8},{10,11... | collective-permute-start | bytes 1474568 | tf_op jit(solution)/shard_map/ppermute | solution.py:162
  18.1 0.0 collective-permute-done
  18.1 1.4 %collective-permute-done.1 = bf16[72,1024]{1,0:T(8,128)(2,1)S(1)} collective-permute-done((bf16[72,1024]{1,0:T(8,128)(2,1)S(1)}, bf16[72,1024]{1,0:T(8,128)(2,1)S(1)}, u32[]{:S(2)}, u32[]{:S(2)}) %collective-permute-start.1) | collective-permute-done | bytes 147488 | tf_op jit(solution)/shard_map/ppermute | solution.py:31
  19.4 0.2 concatenate.11
  19.7 1.9 %collective-permute-start.2 = (bf16[216,1024]{1,0:T(8,128)(2,1)S(1)}, bf16[216,1024]{1,0:T(8,128)(2,1)S(1)}, u32[]{:S(2)}, u32[]{:S(2)}) collective-permute-start(bf16[216,1024]{1,0:T(8,128)(2,1)S(1)} %concatenate.11), channel_id=1, source_target_pairs={{8,16},{16,8},{24,32},{32,24},{40,48},{48,40},{72,80},{80,72},{88,... | collective-permute-start | bytes 1327112 | tf_op jit(solution)/shard_map/ppermute | solution.py:164
  21.6 3.7 %all_gather.7.both_ref = bf16[432,1024]{1,0:T(8,128)(2,1)S(1)} all-gather(bf16[216,1024]{1,0:T(8,128)(2,1)S(1)} %concatenate.11), channel_id=1, replica_groups={{0,8},{16,24},{32,40},{48,56},{64,72},{80,88},{96,104},{112,120},{128,1..., dimensions={0}, use_global_device_ids=true | all-gather | bytes 1327104 | tf_op jit(solution)/shard_map/all_gather | solution.py:165
  25.3 0.0 copy-start
  25.3 4.0 %collective-permute-done.2.outer_ref = bf16[216,1024]{1,0:T(8,128)(2,1)S(1)} collective-permute-done((bf16[216,1024]{1,0:T(8,128)(2,1)S(1)}, bf16[216,1024]{1,0:T(8,128)(2,1)S(1)}, u32[]{:S(2)}, u32[]{:S(2)}) %collective-permute-start.2) | collective-permute-done | bytes 442400 | tf_op jit(solution)/shard_map/ppermute | solution.py:164
  29.3 0.0 copy-done.1
  29.3 8.7 %pick.1.lhs = bf16[512,1792]{1,0:T(8,128)(2,1)S(1)} custom-call(s32[1]{0:T(128)} %bitcast.par_ref, s32[1]{0:T(128)} %bitcast.1.core_ref, s32[27,1024]{1,0:T(8,128)S(1)} %copy-done.1, bf16[432,1024]{1,0:T(8,128)(2,1)S(1)} %all_gather.7.both_ref, bf16[216,1024]{1,0:T(8,128)(2,1)S(1)} %collective-permute-done.2.outer_ref), custom_call_target="tpu_custom_call" | custom-call | bytes 1024 | tf_op jit(solution)/shard_map/pick/pallas_call | solution.py:168
  38.0 0.0 collective-permute-done.3.w1_ref
  38.0 0.0 copy-done
  38.0 0.8 %multiply.1 = f32[256,512]{1,0:T(8,128)S(1)} custom-call(s32[1]{0:T(128)} %bitcast.par_ref, bf16[512,1792]{1,0:T(8,128)(2,1)S(1)} %pick.1.lhs, bf16[864,256]{1,0:T(8,128)(2,1)S(1)} %bitcast.9, bf16[960,256]{1,0:T(8,128)(2,1)S(1)} %collective-permute-done.3.w1_ref), custom_call_target="tpu_custom_call" | custom-call | tf_op jit(solution)/shard_map/multiply/pallas_call | solution.py:185
  38.8 27.5 %all_to_all.9.got_ref = f32[8,32,512]{2,1,0:T(8,128)S(1)} all-to-all(f32[8,32,512]{2,1,0:T(8,128)S(1)} %bitcast.7), channel_id=1, replica_groups=mesh['space'=64,'chan'=8] {'chan'}, dimensions={0} | all-to-all | bytes 1048576 | tf_op jit(solution)/shard_map/all_to_all | solution.py:194
  66.3 0.7 add.14
  (3 shorter events, 0.1 us)
Async XLA Ops:
  6.3 23.0 %copy-start.1 = (s32[27,1024]{1,0:T(8,128)S(1)}, s32[27,1024]{1,0:T(8,128)}, u32[]{:S(2)}) copy-start(s32[27,1024]{1,0:T(8,128)} %gm_ref.1) | copy-start | bytes 331780
  6.4 11.7 %collective-permute-start = (bf16[72,1024]{1,0:T(8,128)(2,1)S(1)}, bf16[72,1024]{1,0:T(8,128)(2,1)S(1)}, u32[]{:S(2)}, u32[]{:S(2)}) collective-permute-start(bf16[72,1024]{1,0:T(8,128)(2,1)S(1)} %get-tuple-element.6), channel_id=1, source_target_pairs={{0,64},{8,72},{16,80},{24,88},{32,96},{40,104},{48,112},{56,120},{... | collective-permute-start | bytes 442376 | tf_op jit(solution)/shard_map/ppermute | solution.py:31
  11.2 8.2 %collective-permute-start.1 = (bf16[72,1024]{1,0:T(8,128)(2,1)S(1)}, bf16[72,1024]{1,0:T(8,128)(2,1)S(1)}, u32[]{:S(2)}, u32[]{:S(2)}) collective-permute-start(bf16[72,1024]{1,0:T(8,128)(2,1)S(1)} %get-tuple-element.5), channel_id=1, source_target_pairs={{64,0},{72,8},{80,16},{88,24},{96,32},{104,40},{112,48},{120,56},{... | collective-permute-start | bytes 442376 | tf_op jit(solution)/shard_map/ppermute | solution.py:31
  14.2 23.8 %collective-permute-start.3 = (bf16[960,256]{1,0:T(8,128)(2,1)S(1)}, bf16[960,256]{1,0:T(8,128)(2,1)S(1)}, u32[]{:S(2)}, u32[]{:S(2)}) collective-permute-start(bf16[960,256]{1,0:T(8,128)(2,1)S(1)} %pad.9), channel_id=1, source_target_pairs={{0,1},{1,0},{2,3},{3,2},{4,5},{5,4},{6,7},{7,6},{8,9},{9,8},{10,11... | collective-permute-start | bytes 1474568 | tf_op jit(solution)/shard_map/ppermute | solution.py:162
  19.7 9.6 %collective-permute-start.2 = (bf16[216,1024]{1,0:T(8,128)(2,1)S(1)}, bf16[216,1024]{1,0:T(8,128)(2,1)S(1)}, u32[]{:S(2)}, u32[]{:S(2)}) collective-permute-start(bf16[216,1024]{1,0:T(8,128)(2,1)S(1)} %concatenate.11), channel_id=1, source_target_pairs={{8,16},{16,8},{24,32},{32,24},{40,48},{48,40},{72,80},{80,72},{88,... | collective-permute-start | bytes 1327112 | tf_op jit(solution)/shard_map/ppermute | solution.py:164
  25.3 12.8 %copy-start = (bf16[27,32,256]{2,1,0:T(8,128)(2,1)S(1)}, bf16[27,32,256]{2,1,0:T(8,128)(2,1)}, u32[]{:S(2)}) copy-start(bf16[27,32,256]{2,1,0:T(8,128)(2,1)} %param.5) | copy-start | bytes 1327108

commit v11 on v10

--- a/solution.py
+++ b/solution.py
@@ -36,12 +36,16 @@
     par = par_ref[0]
     core = core_ref[0]
     sources = [both_ref.at[pl.ds(MSG * i, MSG)] for i in range(6)]
-    sources += [outer_ref.at[pl.ds(MSG * i, MSG)] for i in range(3)]
+    sources += [outer_ref.at[pl.ds(64 * i, 64)] for i in range(3)]
     own_base = 3 * core
     base_of = (own_base, jnp.where(core == 0, 6, 0), jnp.where(core == 0, 3, 6))
 
-    for block, source in enumerate(sources):
+    for block, source in enumerate(sources[:6]):
         digit[8 * block:8 * block + 8, :] = source[64:72, :HALO].astype(jnp.float32)
+    face = outer_ref[192:200, :HALO].astype(jnp.float32)
+    for i in range(6):
+        at = 48 + 8 * (i // 2) + 3 * (i % 2)
+        digit[at:at + 3, :] = jnp.broadcast_to(face[i:i + 1], (3, HALO))
     for number, (step_row, step_col) in enumerate(STEPS):
         sent = (0, 1, 2)[step_row]
         block = base_of[step_col] + sent
@@ -159,9 +163,15 @@
     own = message(FIRST[0])
     up = shift(message(FIRST[1]), 1, 0)
     dn = shift(message(FIRST[2]), -1, 0)
-    w1 = lax.ppermute(jnp.pad(w0, ((0, 96), (0, 0))), "chan", flip)
+    w1 = lax.ppermute(w0, "chan", flip)
     strip = jnp.concatenate([own, up, dn], axis=0)
-    outer = lax.ppermute(strip, "space", facing)
+    faces = [
+        jnp.concatenate([b[64 + t + i:65 + t + i] for b, t in zip((own, up, dn), at) for i in (0, 3)], axis=0)
+        for at in ((0, 0, 0), (1, 2, 2))
+    ]
+    face = jnp.where(core == 0, faces[0], faces[1])
+    outer = jnp.concatenate([own[:64], up[:64], dn[:64], face, blank], axis=0)
+    outer = lax.ppermute(outer, "space", facing)
     both = lax.all_gather(strip, "space", axis=0, tiled=True, axis_index_groups=chips)
     vmem = pl.BlockSpec(memory_space=pltpu.VMEM)
     smem = pl.BlockSpec(memory_space=pltpu.SMEM)

time: 67.3 us -> 66.8 us (level)
  local copies, waits for them, and re-layouts: 1.28 us -> 0.46 us
    pad x1 -> x0, local copies, waits for them, and re-layouts: 1.05 us -> none  [local(): w1 = lax.ppermute(jnp.pad(w0, ((0, 96), (0, 0))), 'chan', flip)]
    ppermute x2, waiting for transfers between devices: 1.36 us -> 2.35 us  [shift(): return lax.ppermute(value, 'space', pairs)]
  transfers between devices with their start and end apart: 4 -> 4, of which waited for: 2 -> 2; matrix products, arithmetic and copies ran while one was open for 2% -> 1% of each run, Pallas kernels for 13% -> 13%
where the time goes in v11:
time: 66.8 us; the launch traced here: 66.5 us
  blocking collectives  36.7 us (55%)
  starting transfers between devices  12.4 us (19%)
  Pallas kernels  10.2 us (15%)
  waiting for transfers between devices  5.81 us (9%)
  other arithmetic  0.79 us (1%)
    all_to_all x1, blocking collectives, local(): got = lax.all_to_all(part, 'chan', 0, 0, tiled=True).reshape(8, 32, HALF)  27.5 us
    pallas_call x1, Pallas kernels, local(): pl.pallas_call(pick_kernel, out_shape=jax.ShapeDtypeStruct((HALF, 128 * P...  8.73 us
    ppermute x2, starting transfers between devices, shift(): return lax.ppermute(value, 'space', pairs)  6.62 us
    all_gather x1, blocking collectives, local(): lax.all_gather(features.T, 'chan', axis=0, tiled=True, axis_index_groups=...  5.53 us
    ppermute x1, starting transfers between devices, local(): w1 = lax.ppermute(w0, 'chan', flip)  3.89 us
    all_gather x1, blocking collectives, local(): lax.all_gather(strip, 'space', axis=0, tiled=True, axis_index_groups=chips)  3.66 us
    ppermute x1, waiting for transfers between devices, local(): outer = lax.ppermute(outer, 'space', facing)  3.46 us
    ppermute x2, waiting for transfers between devices, shift(): return lax.ppermute(value, 'space', pairs)  2.35 us
  transfers between devices with their start and end apart: 4, of which 2 were waited for; matrix products, arithmetic and copies ran while one was open for 1% of the time, Pallas kernels for 13%

profile of v11, /device:TPU:26, one launch (start us, length us, event | category | flops | bytes accessed | tf_op | source)
XLA Modules:
  0.0 66.5 jit_solution(16851146157469326317)
XLA Ops:
  0.0 0.7 %fusion.1 = (bf16[8,1024]{1,0:T(8,128)(2,1)S(1)}, bf16[8,1024]{1,0:T(8,128)(2,1)S(1)}) fusion(s32[8,768]{1,0:T(8,128)} %bitcast.11), kind=kLoop, calls=%fused_computation.5 | loop fusion | flops 32768 | bytes 57344 | tf_op jit(solution)/shard_map/convert_element_type | solution.py:157
  0.7 5.5 %all_gather.6 = bf16[64,1024]{1,0:T(8,128)(2,1)S(1)} all-gather(bf16[32,1024]{1,0:T(8,128)(2,1)} %bitcast.10), channel_id=1, replica_groups={{0,1},{2,3},{4,5},{6,7},{8,9},{10,11},{12,13},{14,15},{16,17},{18,19},{..., dimensions={0}, use_global_device_ids=true | all-gather | bytes 196608 | tf_op jit(solution)/shard_map/all_gather | solution.py:155
  6.4 4.7 %collective-permute-start = (bf16[72,1024]{1,0:T(8,128)(2,1)S(1)}, bf16[72,1024]{1,0:T(8,128)(2,1)S(1)}, u32[]{:S(2)}, u32[]{:S(2)}) collective-permute-start(bf16[72,1024]{1,0:T(8,128)(2,1)S(1)} %get-tuple-element.14), channel_id=1, source_target_pairs={{0,64},{8,72},{16,80},{24,88},{32,96},{40,104},{48,112},{56,120},{... | collective-permute-start | bytes 442376 | tf_op jit(solution)/shard_map/ppermute | solution.py:31
  11.1 1.9 %collective-permute-start.1 = (bf16[72,1024]{1,0:T(8,128)(2,1)S(1)}, bf16[72,1024]{1,0:T(8,128)(2,1)S(1)}, u32[]{:S(2)}, u32[]{:S(2)}) collective-permute-start(bf16[72,1024]{1,0:T(8,128)(2,1)S(1)} %get-tuple-element.13), channel_id=1, source_target_pairs={{64,0},{72,8},{80,16},{88,24},{96,32},{104,40},{112,48},{120,56},{... | collective-permute-start | bytes 442376 | tf_op jit(solution)/shard_map/ppermute | solution.py:31
  13.0 3.9 %collective-permute-start.3 = (bf16[864,256]{1,0:T(8,128)(2,1)}, bf16[864,256]{1,0:T(8,128)(2,1)S(1)}, u32[]{:S(2)}, u32[]{:S(2)}) collective-permute-start(bf16[864,256]{1,0:T(8,128)(2,1)} %bitcast.8), channel_id=1, source_target_pairs={{0,1},{1,0},{2,3},{3,2},{4,5},{5,4},{6,7},{7,6},{8,9},{9,8},{10,11... | collective-permute-start | bytes 1327112 | tf_op jit(solution)/shard_map/ppermute | solution.py:166
  16.9 0.0 collective-permute-done
  17.0 2.3 %collective-permute-done.1 = bf16[72,1024]{1,0:T(8,128)(2,1)S(1)} collective-permute-done((bf16[72,1024]{1,0:T(8,128)(2,1)S(1)}, bf16[72,1024]{1,0:T(8,128)(2,1)S(1)}, u32[]{:S(2)}, u32[]{:S(2)}) %collective-permute-start.1) | collective-permute-done | bytes 147488 | tf_op jit(solution)/shard_map/ppermute | solution.py:31
  19.3 0.1 concatenate.22
  19.4 0.0 copy-start.1
  19.4 0.1 concatenate.21
  19.5 0.1 concatenate.23
  19.5 1.9 %collective-permute-start.2 = (bf16[200,1024]{1,0:T(8,128)(2,1)S(1)}, bf16[200,1024]{1,0:T(8,128)(2,1)S(1)}, u32[]{:S(2)}, u32[]{:S(2)}) collective-permute-start(bf16[200,1024]{1,0:T(8,128)(2,1)S(1)} %concatenate.23), channel_id=1, source_target_pairs={{8,16},{16,8},{24,32},{32,24},{40,48},{48,40},{72,80},{80,72},{88,... | collective-permute-start | bytes 1228808 | tf_op jit(solution)/shard_map/ppermute | solution.py:174
  21.5 0.2 concatenate.20
  21.7 3.7 %all_gather.7.both_ref = bf16[432,1024]{1,0:T(8,128)(2,1)S(1)} all-gather(bf16[216,1024]{1,0:T(8,128)(2,1)S(1)} %concatenate.20), channel_id=1, replica_groups={{0,8},{16,24},{32,40},{48,56},{64,72},{80,88},{96,104},{112,120},{128,1..., dimensions={0}, use_global_device_ids=true | all-gather | bytes 1327104 | tf_op jit(solution)/shard_map/all_gather | solution.py:175
  25.4 0.0 copy-start
  25.4 3.5 %collective-permute-done.2.outer_ref = bf16[200,1024]{1,0:T(8,128)(2,1)S(1)} collective-permute-done((bf16[200,1024]{1,0:T(8,128)(2,1)S(1)}, bf16[200,1024]{1,0:T(8,128)(2,1)S(1)}, u32[]{:S(2)}, u32[]{:S(2)}) %collective-permute-start.2) | collective-permute-done | bytes 409632 | tf_op jit(solution)/shard_map/ppermute | solution.py:174
  28.8 0.0 copy-done.1
  28.8 8.7 %pick.1.lhs = bf16[512,1792]{1,0:T(8,128)(2,1)S(1)} custom-call(s32[1]{0:T(128)} %bitcast.par_ref, s32[1]{0:T(128)} %bitcast.1.core_ref, s32[27,1024]{1,0:T(8,128)S(1)} %copy-done.1, bf16[432,1024]{1,0:T(8,128)(2,1)S(1)} %all_gather.7.both_ref, bf16[200,1024]{1,0:T(8,128)(2,1)S(1)} %collective-permute-done.2.outer_ref), custom_call_target="tpu_custom_call" | custom-call | bytes 1024 | tf_op jit(solution)/shard_map/pick/pallas_call | solution.py:178
  37.6 0.0 collective-permute-done.3.w1_ref
  37.6 0.0 copy-done
  37.6 0.8 %multiply.1 = f32[256,512]{1,0:T(8,128)S(1)} custom-call(s32[1]{0:T(128)} %bitcast.par_ref, bf16[512,1792]{1,0:T(8,128)(2,1)S(1)} %pick.1.lhs, bf16[864,256]{1,0:T(8,128)(2,1)S(1)} %bitcast.9, bf16[864,256]{1,0:T(8,128)(2,1)S(1)} %collective-permute-done.3.w1_ref), custom_call_target="tpu_custom_call" | custom-call | tf_op jit(solution)/shard_map/multiply/pallas_call | solution.py:195
  38.4 27.5 %all_to_all.9.got_ref = f32[8,32,512]{2,1,0:T(8,128)S(1)} all-to-all(f32[8,32,512]{2,1,0:T(8,128)S(1)} %bitcast.7), channel_id=1, replica_groups=mesh['space'=64,'chan'=8] {'chan'}, dimensions={0} | all-to-all | bytes 1048576 | tf_op jit(solution)/shard_map/all_to_all | solution.py:204
  65.9 0.7 add.12
  (9 shorter events, 0.1 us)
Async XLA Ops:
  6.4 10.6 %collective-permute-start = (bf16[72,1024]{1,0:T(8,128)(2,1)S(1)}, bf16[72,1024]{1,0:T(8,128)(2,1)S(1)}, u32[]{:S(2)}, u32[]{:S(2)}) collective-permute-start(bf16[72,1024]{1,0:T(8,128)(2,1)S(1)} %get-tuple-element.14), channel_id=1, source_target_pairs={{0,64},{8,72},{16,80},{24,88},{32,96},{40,104},{48,112},{56,120},{... | collective-permute-start | bytes 442376 | tf_op jit(solution)/shard_map/ppermute | solution.py:31
  11.1 8.2 %collective-permute-start.1 = (bf16[72,1024]{1,0:T(8,128)(2,1)S(1)}, bf16[72,1024]{1,0:T(8,128)(2,1)S(1)}, u32[]{:S(2)}, u32[]{:S(2)}) collective-permute-start(bf16[72,1024]{1,0:T(8,128)(2,1)S(1)} %get-tuple-element.13), channel_id=1, source_target_pairs={{64,0},{72,8},{80,16},{88,24},{96,32},{104,40},{112,48},{120,56},{... | collective-permute-start | bytes 442376 | tf_op jit(solution)/shard_map/ppermute | solution.py:31
  13.0 24.6 %collective-permute-start.3 = (bf16[864,256]{1,0:T(8,128)(2,1)}, bf16[864,256]{1,0:T(8,128)(2,1)S(1)}, u32[]{:S(2)}, u32[]{:S(2)}) collective-permute-start(bf16[864,256]{1,0:T(8,128)(2,1)} %bitcast.8), channel_id=1, source_target_pairs={{0,1},{1,0},{2,3},{3,2},{4,5},{5,4},{6,7},{7,6},{8,9},{9,8},{10,11... | collective-permute-start | bytes 1327112 | tf_op jit(solution)/shard_map/ppermute | solution.py:166
  19.4 9.4 %copy-start.1 = (s32[27,1024]{1,0:T(8,128)S(1)}, s32[27,1024]{1,0:T(8,128)}, u32[]{:S(2)}) copy-start(s32[27,1024]{1,0:T(8,128)} %gm_ref.1) | copy-start | bytes 331780
  19.5 9.3 %collective-permute-start.2 = (bf16[200,1024]{1,0:T(8,128)(2,1)S(1)}, bf16[200,1024]{1,0:T(8,128)(2,1)S(1)}, u32[]{:S(2)}, u32[]{:S(2)}) collective-permute-start(bf16[200,1024]{1,0:T(8,128)(2,1)S(1)} %concatenate.23), channel_id=1, source_target_pairs={{8,16},{16,8},{24,32},{32,24},{40,48},{48,40},{72,80},{80,72},{88,... | collective-permute-start | bytes 1228808 | tf_op jit(solution)/shard_map/ppermute | solution.py:174
  25.4 12.2 %copy-start = (bf16[27,32,256]{2,1,0:T(8,128)(2,1)S(1)}, bf16[27,32,256]{2,1,0:T(8,128)(2,1)}, u32[]{:S(2)}) copy-start(bf16[27,32,256]{2,1,0:T(8,128)(2,1)} %param.5) | copy-start | bytes 1327108
